TPU v7x, 32 devices: a whole 2x2x4 slice. The times are simulated.
32 devices in a mesh: grp: 2 (over y), tm: 8 (over z, x), space: 2 (over core).
Axes of the slice: x: 2, y: 2, z: 4, core: 2. Of those that a mesh axis runs over, the one named last changes fastest.
Arguments:
- tokens: bfloat16 [16, 24, 64, 1024], P(('grp', 'tm'), 'space'), parts along dimension 0, may hold values from -28 to 28
- gains: float32 [2, 1024], replicated, may hold values from 0.5 to 2
- qkv_weights: bfloat16 [2, 1024, 1536], replicated, may hold values from -1.125 to 1.125
- out_weights: bfloat16 [2, 512, 1024], replicated, may hold values from -0.25 to 0.25
Outputs:
- video_out: bfloat16 [16, 24, 64, 1024], P(('grp', 'tm'), 'space'), parts along dimension 0
There are 2 independent parts, one for each index of `grp`. A program takes and returns all parts, laid end to end along the dimension named above; an argument that names none is the same for every part. Nothing has to cross between parts.
All inputs are finite; a program needn't handle non-finite values.
Results may differ from a plain program's by a relative error of at most 0.007.
Values may be sent and summed in bfloat16 or wider, within the bound.
No kernel may reach another device: no remote copies, remote signals or barrier semaphores. Data moves between devices by JAX's collectives and lax.ppermute only.
A program may use at most 64 MiB of HBM per device.

v0:
```python
import functools

import jax
import jax.numpy as jnp
from jax import lax
from jax.experimental import pallas as pl
from jax.experimental.pallas import tpu as pltpu
from jax.sharding import PartitionSpec as P


HEAD = 64
EPS = 1e-06
QUAD = 4
CHUNKS = 2
COLB = 8
POSB = 16
NEG = -1e30
VMEM_BYTES = 16 * 1024 * 1024


def params():
    return pltpu.CompilerParams(vmem_limit_bytes=VMEM_BYTES)


def normalise(stream, gain):
    scale = lax.rsqrt(jnp.mean(stream * stream, axis=-1, keepdims=True) + EPS)
    return (stream * scale * gain).astype(jnp.bfloat16)


def group_bias(keys, group):
    left = lax.broadcasted_iota(jnp.int32, (1, group, keys), 1)
    right = lax.broadcasted_iota(jnp.int32, (1, group, keys), 2) % group
    return jnp.where(left == right, 0.0, NEG)


def attend_quad(query, key, value, bias):
    rows, width = query.shape
    keys = key.shape[0]
    lanes = lax.broadcasted_iota(jnp.int32, (rows, width), 1) // HEAD
    heads = width // HEAD
    zero = jnp.zeros_like(query)
    stacked = jnp.concatenate([jnp.where(lanes == h, query, zero) for h in range(heads)], axis=0)
    scores = lax.dot_general(
        stacked, key, (((1,), (1,)), ((), ())), preferred_element_type=jnp.float32
    )
    scores = scores.reshape(heads * rows // bias.shape[1], bias.shape[1], keys) + bias
    raised = jnp.exp(scores - jnp.max(scores, axis=-1, keepdims=True))
    total = jnp.sum(raised, axis=-1, keepdims=True).reshape(heads * rows, 1)
    raised = raised.reshape(heads * rows, keys).astype(jnp.bfloat16)
    mixed = jnp.dot(raised, value, preferred_element_type=jnp.float32) * (1.0 / total)
    out = mixed[:rows]
    for h in range(1, heads):
        out = jnp.where(lanes == h, mixed[h * rows : (h + 1) * rows], out)
    return out.astype(jnp.bfloat16)


def attend(q_ref, kv_ref, other_ref, spans, group, put):
    inner = q_ref.shape[1]
    width = QUAD * HEAD
    keys = 2 * sum(size for _, size in spans[0])
    bias = group_bias(keys, group)

    def rows(ref, span, lo):
        return [ref[at : at + size, lo : lo + width] for at, size in span]

    def join(parts):
        return parts[0] if len(parts) == 1 else jnp.concatenate(parts, axis=0)

    for span in spans:
        for lo in range(0, inner, width):
            key = join(rows(kv_ref, span, lo) + rows(other_ref, span, lo))
            value = join(rows(kv_ref, span, inner + lo) + rows(other_ref, span, inner + lo))
            put(span, lo, attend_quad(join(rows(q_ref, span, lo)), key, value, bias))


def project(normed, weight, q_ref, kv_ref, inner):
    for i, lo in enumerate((inner, 2 * inner, 0)):
        part = jnp.dot(normed, weight(i), preferred_element_type=jnp.float32).astype(jnp.bfloat16)
        if lo:
            kv_ref[:, lo - inner : lo] = part
        else:
            q_ref[...] = part * jnp.bfloat16(HEAD**-0.5)


def height_project_kernel(
    c, x_ref, gain_ref, w_ref, q_ref, kv_ref, x_buf, w_buf, gain_buf, x_sem, w_sem, gain_sem
):
    blocks, rows, colb, feat = x_buf.shape
    inner = q_ref.shape[1]
    loads = [
        pltpu.make_async_copy(
            x_ref.at[:, pl.ds((c * blocks + b) * colb, colb), :], x_buf.at[b], x_sem.at[b]
        )
        for b in range(blocks)
    ]
    fetches = [
        pltpu.make_async_copy(
            w_ref.at[0, :, pl.ds(lo, inner)], w_buf.at[i], w_sem.at[i]
        )
        for i, lo in enumerate((inner, 2 * inner, 0))
    ]
    gain_load = pltpu.make_async_copy(gain_ref, gain_buf, gain_sem)
    for copy in [gain_load] + loads + fetches:
        copy.start()
    gain_load.wait()
    parts = []
    for b in range(blocks):
        loads[b].wait()
        stream = x_buf[b].astype(jnp.float32).reshape(rows * colb, feat)
        parts.append(normalise(stream, gain_buf[0:1, :]))
    normed = jnp.concatenate(parts, axis=0)

    def weight(i):
        fetches[i].wait()
        return w_buf[i]

    project(normed, weight, q_ref, kv_ref, inner)


def height_kernel(
    c, hi_ref, x_ref, q_ref, kv_ref, other_ref, w_ref, *refs
):
    full_ref, mix_ref, x_buf, w_buf, x_sem, w_sem = refs[-6:]
    piece_refs = refs[:-6]
    blocks, rows, colb, feat = x_buf.shape
    per = rows * colb
    loads = [
        pltpu.make_async_copy(
            x_ref.at[:, pl.ds((c * blocks + b) * colb, colb), :], x_buf.at[b], x_sem.at[b]
        )
        for b in range(blocks)
    ]
    fetch = pltpu.make_async_copy(w_ref.at[0], w_buf, w_sem)
    fetch.start()
    for copy in loads:
        copy.start()

    def put(span, lo, out):
        at, size = span[0]
        mix_ref[at : at + size, lo : lo + out.shape[1]] = out

    attend(q_ref, kv_ref, other_ref, [[(b * per, per)] for b in range(blocks)], colb, put)
    fetch.wait()
    for b in range(blocks):
        loads[b].wait()
        stream = x_buf[b].astype(jnp.float32).reshape(per, feat)
        update = jnp.dot(
            mix_ref[b * per : (b + 1) * per, :], w_buf[...], preferred_element_type=jnp.float32
        )
        full_ref[b * per : (b + 1) * per, :] = (stream + update).astype(jnp.bfloat16)
    each = piece_refs[0].shape[0]
    for k, piece_ref in enumerate(piece_refs):
        start = pl.multiple_of(jnp.bitwise_xor(hi_ref[0], k) * each, each)
        piece_ref[...] = full_ref[pl.ds(start, each), :]


def time_project_kernel(*refs):
    gain_ref, w_ref, q_ref, kv_ref = refs[-4:]
    inner = q_ref.shape[1]
    normed = jnp.concatenate(
        [normalise(ref[...].astype(jnp.float32), gain_ref[1:2, :]) for ref in refs[:-4]], axis=0
    )
    starts = (inner, 2 * inner, 0)
    project(normed, lambda i: w_ref[:, starts[i] : starts[i] + inner], q_ref, kv_ref, inner)


def time_kernel(q_ref, kv_ref, other_ref, *mix_refs):
    each = mix_refs[0].shape[0]
    spans = [
        [(k * each + p, POSB) for k in range(len(mix_refs))] for p in range(0, each, POSB)
    ]

    def put(span, lo, out):
        at = span[0][0]
        for k, ref in enumerate(mix_refs):
            ref[at : at + POSB, lo : lo + out.shape[1]] = out[k * POSB : (k + 1) * POSB]

    attend(q_ref, kv_ref, other_ref, spans, POSB, put)


def finish_kernel(frames, hi_ref, full_ref, w_ref, *refs):
    out_ref, mix_ref = refs[-2:]
    rows, cols, feat = out_ref.shape
    per = rows * COLB
    each = refs[0].shape[0]
    for k in range(frames):
        start = pl.multiple_of(jnp.bitwise_xor(hi_ref[0], k) * each, each)
        mix_ref[pl.ds(start, each), :] = refs[k][...]
    for b in range(cols // COLB):
        update = jnp.dot(
            mix_ref[b * per : (b + 1) * per, :], w_ref[...], preferred_element_type=jnp.float32
        )
        total = full_ref[b * per : (b + 1) * per, :].astype(jnp.float32) + update
        out_ref[:, b * COLB : (b + 1) * COLB, :] = total.reshape(rows, COLB, feat).astype(
            jnp.bfloat16
        )


SMEM = pl.BlockSpec(memory_space=pltpu.SMEM)
HBM = pl.BlockSpec(memory_space=pltpu.HBM)


def cost(flops, moved):
    return pl.CostEstimate(flops=int(flops), bytes_accessed=int(moved), transcendentals=0)


def fast(tokens, gains, qkv_weights, out_weights):
    high = lax.axis_size("tm") // 2
    half = high // 2
    hi = (lax.axis_index("tm") // 2).astype(jnp.int32)[None]
    rows, cols, feat = tokens.shape[1:]
    inner = out_weights.shape[1]
    wide = cols // CHUNKS
    blocks = wide // COLB
    count = rows * wide
    each = count // high
    bf = jnp.bfloat16
    x = pltpu.with_memory_space_constraint(tokens[0], pltpu.HBM)
    gains_far = pltpu.with_memory_space_constraint(gains, pltpu.HBM)
    qkv_far = pltpu.with_memory_space_constraint(qkv_weights, pltpu.HBM)
    out_far = pltpu.with_memory_space_constraint(out_weights, pltpu.HBM)

    def pick(i, n):
        return pl.BlockSpec((None,) + n, lambda _: (i,) + (0,) * len(n))

    def whole(*shape):
        return pl.BlockSpec(shape, lambda _: (0,) * len(shape))

    def call(kernel, flops, **rest):
        return pl.pallas_call(
            kernel,
            grid=(1,),
            compiler_params=params(),
            cost_estimate=cost(flops, 4 * count * feat),
            **rest,
        )

    qkv_out = dict(
        out_specs=[whole(count, inner), whole(count, 2 * inner)],
        out_shape=[
            jax.ShapeDtypeStruct((count, inner), bf),
            jax.ShapeDtypeStruct((count, 2 * inner), bf),
        ],
    )
    qkv_in = [whole(count, inner), whole(count, 2 * inner), whole(count, 2 * inner)]
    x_scratch = pltpu.VMEM((blocks, rows, COLB, feat), bf)
    work = 2 * count * feat * inner

    def after(values, earlier):
        return lax.optimization_barrier((values, earlier))[0]

    def height_project(c, x):
        return call(
            functools.partial(height_project_kernel, c),
            3 * work,
            in_specs=[HBM, HBM, HBM],
            scratch_shapes=[
                x_scratch,
                pltpu.VMEM((3, feat, inner), bf),
                pltpu.VMEM(gains.shape, gains.dtype),
                pltpu.SemaphoreType.DMA((blocks,)),
                pltpu.SemaphoreType.DMA((3,)),
                pltpu.SemaphoreType.DMA,
            ],
            **qkv_out,
        )(x, gains_far, qkv_far)

    def height(c, q, kv, other):
        outs = call(
            functools.partial(height_kernel, c),
            4 * work,
            in_specs=[SMEM, HBM] + qkv_in + [HBM],
            out_specs=[whole(each, feat)] * high + [whole(count, feat)],
            out_shape=[jax.ShapeDtypeStruct((each, feat), bf)] * high
            + [jax.ShapeDtypeStruct((count, feat), bf)],
            scratch_shapes=[
                pltpu.VMEM((count, inner), bf),
                x_scratch,
                pltpu.VMEM((inner, feat), bf),
                pltpu.SemaphoreType.DMA((blocks,)),
                pltpu.SemaphoreType.DMA,
            ],
        )(hi, x, q, kv, other, out_far)
        return outs[:-1], outs[-1]

    def time_project(pieces):
        return call(
            time_project_kernel,
            3 * work,
            in_specs=[whole(each, feat)] * high
            + [whole(*gains.shape), pick(1, (feat, 3 * inner))],
            **qkv_out,
        )(*pieces, gains, qkv_weights)

    def timed(q, kv, other):
        return call(
            time_kernel,
            2 * work,
            in_specs=qkv_in,
            out_specs=[whole(each, inner)] * high,
            out_shape=[jax.ShapeDtypeStruct((each, inner), bf)] * high,
        )(q, kv, other)

    def finish(c, full, mixes, prior):
        aliases, extra_specs, extra = {}, [], []
        if prior is not None:
            aliases = {high + 3: 0}
            extra_specs, extra = [pl.BlockSpec(memory_space=pl.ANY)], [prior]
        return call(
            functools.partial(finish_kernel, high),
            work,
            in_specs=[SMEM, whole(count, feat), pick(1, (inner, feat))]
            + [whole(each, inner)] * high
            + extra_specs,
            out_specs=pl.BlockSpec((rows, wide, feat), lambda _: (0, c, 0)),
            out_shape=jax.ShapeDtypeStruct((rows, cols, feat), bf),
            scratch_shapes=[pltpu.VMEM((count, inner), bf)],
            input_output_aliases=aliases,
        )(hi, full, out_weights, *mixes, *extra)

    def swap(a):
        return lax.ppermute(a, "space", [(0, 1), (1, 0)])

    def route(k):
        pairs = []
        for z in range(high):
            for lo in range(2):
                for s in range(2):
                    there = z ^ k
                    to = (there * 2 + (s ^ (there >= half))) * 2 + (lo ^ (z >= half))
                    pairs.append(((z * 2 + lo) * 2 + s, to))
        return pairs

    def exchange(pieces):
        return [lax.ppermute(p, ("tm", "space"), route(k)) for k, p in enumerate(pieces)]

    def after(values, earlier):
        return lax.optimization_barrier((values, earlier))[0]

    projected, others, heights, arrived, home = [], [], [], [], []
    last = hi
    for c in range(CHUNKS):
        q, kv = height_project(c, after(x, last))
        projected.append((q, kv))
        others.append(swap(kv))
        last = q
    for c in range(CHUNKS):
        q, kv = projected[c]
        heights.append(height(c, after(q, last), kv, others[c]))
        last = heights[-1][1]
        arrived.append(exchange(heights[-1][0]))
    for c in range(CHUNKS):
        q, kv = time_project(after(arrived[c], last))
        mixes = timed(q, kv, swap(kv))
        last = mixes[0]
        home.append(exchange(mixes))
    out = None
    for c in range(CHUNKS):
        out = finish(c, after(heights[c][1], last), home[c], out)
    return out[None]


def attend_plain(stream, gain, qkv_weight, out_weight):
    groups, length, _ = stream.shape
    inner = out_weight.shape[0]
    heads = inner // HEAD
    wide = stream.astype(jnp.float32)
    normed = normalise(wide, gain)
    projected = jnp.einsum(
        "glf,fe->gle", normed, qkv_weight, preferred_element_type=jnp.float32
    ).astype(jnp.bfloat16)
    q, k, v = jnp.split(projected.reshape(groups, length, 3 * heads, HEAD), 3, axis=2)
    scores = jnp.einsum("gqhd,gkhd->ghqk", q, k, preferred_element_type=jnp.float32) * HEAD**-0.5
    weights = jax.nn.softmax(scores, axis=-1).astype(jnp.bfloat16)
    mixture = jnp.einsum("ghqk,gkhd->gqhd", weights, v, preferred_element_type=jnp.float32)
    mixture = mixture.astype(jnp.bfloat16).reshape(groups, length, inner)
    update = jnp.einsum("gle,ef->glf", mixture, out_weight, preferred_element_type=jnp.float32)
    return (wide + update).astype(jnp.bfloat16)


def plain(tokens, gains, qkv_weights, out_weights):
    frames = lax.axis_size("tm")
    local = lax.all_to_all(tokens[0], "space", split_axis=1, concat_axis=0, tiled=True)
    height_n, wide, feat = local.shape
    by_column = jnp.transpose(local, (1, 0, 2))
    done = attend_plain(by_column, gains[0], qkv_weights[0], out_weights[0])
    flat = done.reshape(frames, wide * height_n // frames, feat)
    by_frame = lax.all_to_all(flat, "tm", split_axis=0, concat_axis=0, tiled=True)
    done = attend_plain(
        jnp.transpose(by_frame, (1, 0, 2)), gains[1], qkv_weights[1], out_weights[1]
    )
    back = lax.all_to_all(
        jnp.transpose(done, (1, 0, 2)), "tm", split_axis=0, concat_axis=0, tiled=True
    )
    by_row = jnp.transpose(back.reshape(wide, height_n, feat), (1, 0, 2))
    return lax.all_to_all(by_row, "space", split_axis=0, concat_axis=1, tiled=True)[None]


def solution(mesh):
    frames, pair = mesh.shape["tm"], mesh.shape["space"]
    high = frames // 2

    def shards(tokens, gains, qkv_weights, out_weights):
        _, rows, cols, feat = tokens.shape
        inner = out_weights.shape[1]
        count = rows * cols // CHUNKS
        fits = (
            pair == 2
            and frames == 2 * high
            and high > 1
            and high & (high - 1) == 0
            and cols % (CHUNKS * COLB) == 0
            and count % (high * POSB) == 0
            and inner % (QUAD * HEAD) == 0
            and feat % 128 == 0
        )
        body = fast if fits else plain
        return body(tokens, gains, qkv_weights, out_weights)

    return jax.shard_map(
        shards,
        mesh=mesh,
        in_specs=(P(("grp", "tm"), "space", None, None), P(), P(), P()),
        out_specs=P(("grp", "tm"), "space", None, None),
        check_vma=False,
    )
```

profile of v0, /device:TPU:9, one launch (start us, length us, event | category | flops | bytes accessed | tf_op | source)
XLA Modules:
  0.0 87.3 jit_solution(2533429604175239742)
XLA Ops:
  0.0 4.0 %shard_map.46 = (bf16[384,512]{1,0:T(8,128)(2,1)S(1)}, bf16[384,1024]{1,0:T(8,128)(2,1)S(1)}) custom-call(bf16[12,64,1024]{2,1,0:T(8,128)(2,1)} %bitcast.5, f32[2,1024]{1,0:T(2,128)} %refs_4_.3, bf16[2,1024,1536]{2,1,0:T(8,128)(2,1)} %refs_5_.3), custom_call_target="tpu_custom_call" | custom-call | flops 1207959552 | bytes 1572864 | tf_op jit(solution)/shard_map/pallas_call | solution.py:253
  4.7 4.1 %shard_map.47 = (bf16[384,512]{1,0:T(8,128)(2,1)S(1)}, bf16[384,1024]{1,0:T(8,128)(2,1)S(1)}) custom-call(bf16[12,64,1024]{2,1,0:T(8,128)(2,1)} %bitcast.6, f32[2,1024]{1,0:T(2,128)} %refs_4_.3, bf16[2,1024,1536]{2,1,0:T(8,128)(2,1)} %refs_5_.3), custom_call_target="tpu_custom_call" | custom-call | flops 1207959552 | bytes 1572864 | tf_op jit(solution)/shard_map/pallas_call | solution.py:253
  8.9 3.6 %shard_map.48 = (bf16[96,1024]{1,0:T(8,128)(2,1)S(1)}, bf16[96,1024]{1,0:T(8,128)(2,1)S(1)}, bf16[96,1024]{1,0:T(8,128)(2,1)S(1)}, bf16[96,1024]{1,0:T(8,128)(2,1)S(1)}, bf16[384,1024]{1,0:T(8,128)(2,1)S(1)}) custom-call(s32[1]{0:T(128)} %bitcast.hi_ref, bf16[12,64,1024]{2,1,0:T(8,128)(2,1)} %bitcast.7, bf16[384,512]{1,0:T(8,128)(2,1)S(1)} %get-tuple-element.49.q_ref, ...), custom_call_target="tpu_custom_call" | custom-call | flops 1610612736 | bytes 1572864 | tf_op jit(solution)/shard_map/pallas_call | solution.py:269
  12.6 3.5 %collective-permute-start.6 = (bf16[96,1024]{1,0:T(8,128)(2,1)S(1)}, bf16[96,1024]{1,0:T(8,128)(2,1)S(1)}, u32[]{:S(2)}, u32[]{:S(2)}) collective-permute-start(bf16[96,1024]{1,0:T(8,128)(2,1)S(1)} %get-tuple-element.59), channel_id=1, source_target_pairs={{0,0},{1,2},{2,1},{3,3},{4,4},{5,6},{6,5},{7,7},{8,11},{9,9},{10,1... | collective-permute-start | bytes 589832 | tf_op jit(solution)/shard_map/ppermute | solution.py:335
  16.1 2.7 %collective-permute-start.8 = (bf16[96,1024]{1,0:T(8,128)(2,1)S(1)}, bf16[96,1024]{1,0:T(8,128)(2,1)S(1)}, u32[]{:S(2)}, u32[]{:S(2)}) collective-permute-start(bf16[96,1024]{1,0:T(8,128)(2,1)S(1)} %get-tuple-element.61), channel_id=1, source_target_pairs={{0,10},{1,8},{2,11},{3,9},{4,14},{5,12},{6,15},{7,13},{8,1},{9,3},... | collective-permute-start | bytes 589832 | tf_op jit(solution)/shard_map/ppermute | solution.py:335
  19.0 3.9 %shard_map.49 = (bf16[96,1024]{1,0:T(8,128)(2,1)S(1)}, bf16[96,1024]{1,0:T(8,128)(2,1)S(1)}, bf16[96,1024]{1,0:T(8,128)(2,1)S(1)}, bf16[96,1024]{1,0:T(8,128)(2,1)S(1)}, bf16[384,1024]{1,0:T(8,128)(2,1)S(1)}) custom-call(s32[1]{0:T(128)} %bitcast.hi_ref, bf16[12,64,1024]{2,1,0:T(8,128)(2,1)} %bitcast.8, bf16[384,512]{1,0:T(8,128)(2,1)S(1)} %get-tuple-element.52.q_ref, ...), custom_call_target="tpu_custom_call" | custom-call | flops 1610612736 | bytes 1572864 | tf_op jit(solution)/shard_map/pallas_call | solution.py:269
  22.9 1.9 %collective-permute-done.7.refs_1_ = bf16[96,1024]{1,0:T(8,128)(2,1)S(1)} collective-permute-done((bf16[96,1024]{1,0:T(8,128)(2,1)S(1)}, bf16[96,1024]{1,0:T(8,128)(2,1)S(1)}, u32[]{:S(2)}, u32[]{:S(2)}) %collective-permute-start.7) | collective-permute-done | bytes 196640 | tf_op jit(solution)/shard_map/ppermute | solution.py:335
  24.8 7.2 %collective-permute-done.8.refs_2_ = bf16[96,1024]{1,0:T(8,128)(2,1)S(1)} collective-permute-done((bf16[96,1024]{1,0:T(8,128)(2,1)S(1)}, bf16[96,1024]{1,0:T(8,128)(2,1)S(1)}, u32[]{:S(2)}, u32[]{:S(2)}) %collective-permute-start.8) | collective-permute-done | bytes 196640 | tf_op jit(solution)/shard_map/ppermute | solution.py:335
  32.0 3.3 %collective-permute-done.9.refs_3_ = bf16[96,1024]{1,0:T(8,128)(2,1)S(1)} collective-permute-done((bf16[96,1024]{1,0:T(8,128)(2,1)S(1)}, bf16[96,1024]{1,0:T(8,128)(2,1)S(1)}, u32[]{:S(2)}, u32[]{:S(2)}) %collective-permute-start.9) | collective-permute-done | bytes 196640 | tf_op jit(solution)/shard_map/ppermute | solution.py:335
  35.3 1.6 %shard_map.50 = (bf16[384,512]{1,0:T(8,128)(2,1)S(1)}, bf16[384,1024]{1,0:T(8,128)(2,1)S(1)}) custom-call(bf16[96,1024]{1,0:T(8,128)(2,1)S(1)} %collective-permute-done.6.refs_0_, bf16[96,1024]{1,0:T(8,128)(2,1)S(1)} %collective-permute-done.7.refs_1_, bf16[96,1024]{1,0:T(8,128)(2,1)S(1)} %collective-permute-done.8.refs_2_, ...), custom_call_target="tpu_custom_call" | custom-call | flops 1207959552 | bytes 1572864 | tf_op jit(solution)/shard_map/pallas_call | solution.py:287
  37.0 3.4 %collective-permute-start.2 = (bf16[96,1024]{1,0:T(8,128)(2,1)S(1)}, bf16[96,1024]{1,0:T(8,128)(2,1)S(1)}, u32[]{:S(2)}, u32[]{:S(2)}) collective-permute-start(bf16[96,1024]{1,0:T(8,128)(2,1)S(1)} %get-tuple-element.55), channel_id=1, source_target_pairs={{0,0},{1,2},{2,1},{3,3},{4,4},{5,6},{6,5},{7,7},{8,11},{9,9},{10,1... | collective-permute-start | bytes 589832 | tf_op jit(solution)/shard_map/ppermute | solution.py:335
  40.5 3.6 %collective-permute-start.4 = (bf16[96,1024]{1,0:T(8,128)(2,1)S(1)}, bf16[96,1024]{1,0:T(8,128)(2,1)S(1)}, u32[]{:S(2)}, u32[]{:S(2)}) collective-permute-start(bf16[96,1024]{1,0:T(8,128)(2,1)S(1)} %get-tuple-element.57), channel_id=1, source_target_pairs={{0,10},{1,8},{2,11},{3,9},{4,14},{5,12},{6,15},{7,13},{8,1},{9,3},... | collective-permute-start | bytes 589832 | tf_op jit(solution)/shard_map/ppermute | solution.py:335
  45.5 3.4 %collective-permute-done.3.refs_1_ = bf16[96,1024]{1,0:T(8,128)(2,1)S(1)} collective-permute-done((bf16[96,1024]{1,0:T(8,128)(2,1)S(1)}, bf16[96,1024]{1,0:T(8,128)(2,1)S(1)}, u32[]{:S(2)}, u32[]{:S(2)}) %collective-permute-start.3) | collective-permute-done | bytes 196640 | tf_op jit(solution)/shard_map/ppermute | solution.py:335
  48.9 7.4 %collective-permute-done.4.refs_2_ = bf16[96,1024]{1,0:T(8,128)(2,1)S(1)} collective-permute-done((bf16[96,1024]{1,0:T(8,128)(2,1)S(1)}, bf16[96,1024]{1,0:T(8,128)(2,1)S(1)}, u32[]{:S(2)}, u32[]{:S(2)}) %collective-permute-start.4) | collective-permute-done | bytes 196640 | tf_op jit(solution)/shard_map/ppermute | solution.py:335
  56.3 3.4 %collective-permute-done.5.refs_3_ = bf16[96,1024]{1,0:T(8,128)(2,1)S(1)} collective-permute-done((bf16[96,1024]{1,0:T(8,128)(2,1)S(1)}, bf16[96,1024]{1,0:T(8,128)(2,1)S(1)}, u32[]{:S(2)}, u32[]{:S(2)}) %collective-permute-start.5) | collective-permute-done | bytes 196640 | tf_op jit(solution)/shard_map/ppermute | solution.py:335
  59.7 1.5 %shard_map.52 = (bf16[384,512]{1,0:T(8,128)(2,1)S(1)}, bf16[384,1024]{1,0:T(8,128)(2,1)S(1)}) custom-call(bf16[96,1024]{1,0:T(8,128)(2,1)S(1)} %collective-permute-done.2.refs_0_, bf16[96,1024]{1,0:T(8,128)(2,1)S(1)} %collective-permute-done.3.refs_1_, bf16[96,1024]{1,0:T(8,128)(2,1)S(1)} %collective-permute-done.4.refs_2_, ...), custom_call_target="tpu_custom_call" | custom-call | flops 1207959552 | bytes 1572864 | tf_op jit(solution)/shard_map/pallas_call | solution.py:287
  61.5 3.7 %collective-permute-start.18 = (bf16[96,512]{1,0:T(8,128)(2,1)S(1)}, bf16[96,512]{1,0:T(8,128)(2,1)S(1)}, u32[]{:S(2)}, u32[]{:S(2)}) collective-permute-start(bf16[96,512]{1,0:T(8,128)(2,1)S(1)} %get-tuple-element.83), channel_id=1, source_target_pairs={{0,10},{1,8},{2,11},{3,9},{4,14},{5,12},{6,15},{7,13},{8,1},{9,3},... | collective-permute-start | bytes 294920 | tf_op jit(solution)/shard_map/ppermute | solution.py:335
  65.5 2.8 %collective-permute-start.16 = (bf16[96,512]{1,0:T(8,128)(2,1)S(1)}, bf16[96,512]{1,0:T(8,128)(2,1)S(1)}, u32[]{:S(2)}, u32[]{:S(2)}) collective-permute-start(bf16[96,512]{1,0:T(8,128)(2,1)S(1)} %get-tuple-element.69), channel_id=1, source_target_pairs={{0,0},{1,2},{2,1},{3,3},{4,4},{5,6},{6,5},{7,7},{8,11},{9,9},{10,1... | collective-permute-start | bytes 294920 | tf_op jit(solution)/shard_map/ppermute | solution.py:335
  71.2 1.7 %collective-permute-start.14 = (bf16[96,512]{1,0:T(8,128)(2,1)S(1)}, bf16[96,512]{1,0:T(8,128)(2,1)S(1)}, u32[]{:S(2)}, u32[]{:S(2)}) collective-permute-start(bf16[96,512]{1,0:T(8,128)(2,1)S(1)} %get-tuple-element.79), channel_id=1, source_target_pairs={{0,10},{1,8},{2,11},{3,9},{4,14},{5,12},{6,15},{7,13},{8,1},{9,3},... | collective-permute-start | bytes 294920 | tf_op jit(solution)/shard_map/ppermute | solution.py:335
  73.3 6.3 %collective-permute-done.19.refs_3_ = bf16[96,512]{1,0:T(8,128)(2,1)S(1)} collective-permute-done((bf16[96,512]{1,0:T(8,128)(2,1)S(1)}, bf16[96,512]{1,0:T(8,128)(2,1)S(1)}, u32[]{:S(2)}, u32[]{:S(2)}) %collective-permute-start.19) | collective-permute-done | bytes 98336 | tf_op jit(solution)/shard_map/ppermute | solution.py:335
  79.6 1.9 %collective-permute-start.12 = (bf16[96,512]{1,0:T(8,128)(2,1)S(1)}, bf16[96,512]{1,0:T(8,128)(2,1)S(1)}, u32[]{:S(2)}, u32[]{:S(2)}) collective-permute-start(bf16[96,512]{1,0:T(8,128)(2,1)S(1)} %get-tuple-element.76), channel_id=1, source_target_pairs={{0,0},{1,2},{2,1},{3,3},{4,4},{5,6},{6,5},{7,7},{8,11},{9,9},{10,1... | collective-permute-start | bytes 294920 | tf_op jit(solution)/shard_map/ppermute | solution.py:335
  81.6 1.7 %shard_map.54.refs_4_ = bf16[12,64,1024]{2,1,0:T(8,128)(2,1)} custom-call(s32[1]{0:T(128)} %bitcast.hi_ref, bf16[384,1024]{1,0:T(8,128)(2,1)S(1)} %get-tuple-element.81.full_ref, bf16[2,512,1024]{2,1,0:T(8,128)(2,1)S(1)} %copy-done, bf16[96,512]{1,0:T(8,128)(2,1)S(1)} %collective-permute-done.16.refs_0_, ...), custom_call_target="tpu_custom_call" | custom-call | flops 402653184 | bytes 1572864 | tf_op jit(solution)/shard_map/pallas_call | solution.py:309
  83.4 2.1 %collective-permute-done.12.refs_0_ = bf16[96,512]{1,0:T(8,128)(2,1)S(1)} collective-permute-done((bf16[96,512]{1,0:T(8,128)(2,1)S(1)}, bf16[96,512]{1,0:T(8,128)(2,1)S(1)}, u32[]{:S(2)}, u32[]{:S(2)}) %collective-permute-start.12) | collective-permute-done | bytes 98336 | tf_op jit(solution)/shard_map/ppermute | solution.py:335
  85.5 1.8 %shard_map.55 = bf16[12,64,1024]{2,1,0:T(8,128)(2,1)} custom-call(s32[1]{0:T(128)} %bitcast.hi_ref, bf16[384,1024]{1,0:T(8,128)(2,1)S(1)} %get-tuple-element.77.full_ref, bf16[2,512,1024]{2,1,0:T(8,128)(2,1)S(1)} %copy-done, bf16[96,512]{1,0:T(8,128)(2,1)S(1)} %collective-permute-done.12.refs_0_, ...), custom_call_target="tpu_custom_call", output_to_operand_aliasing={{}: (7, {})} | custom-call | flops 402653184 | bytes 1572864 | tf_op jit(solution)/shard_map/pallas_call | solution.py:309
  (35 shorter events, 6.5 us)
Async XLA Ops:
  4.0 5.0 %collective-permute-start = (bf16[384,1024]{1,0:T(8,128)(2,1)S(1)}, bf16[384,1024]{1,0:T(8,128)(2,1)S(1)}, u32[]{:S(2)}, u32[]{:S(2)}) collective-permute-start(bf16[384,1024]{1,0:T(8,128)(2,1)S(1)} %get-tuple-element.50.kv_ref), channel_id=1, source_target_pairs={{0,1},{1,0},{2,3},{3,2},{4,5},{5,4},{6,7},{7,6},{8,9},{9,8},{10,11... | collective-permute-start | bytes 2359304 | tf_op jit(solution)/shard_map/ppermute | solution.py:322
  4.7 30.6 %slice-start = ((s8[6291456]{0:T(1024)(128)(4,1)}), s8[4194304]{0:T(1024)(128)(4,1)S(1)}, s32[]{:S(2)}) async-start(s8[6291456]{0:T(1024)(128)(4,1)} %bitcast.3), calls=%async_computation | async-start | bytes 8388608
  8.8 10.1 %collective-permute-start.1 = (bf16[384,1024]{1,0:T(8,128)(2,1)S(1)}, bf16[384,1024]{1,0:T(8,128)(2,1)S(1)}, u32[]{:S(2)}, u32[]{:S(2)}) collective-permute-start(bf16[384,1024]{1,0:T(8,128)(2,1)S(1)} %get-tuple-element.53.kv_ref), channel_id=1, source_target_pairs={{0,1},{1,0},{2,3},{3,2},{4,5},{5,4},{6,7},{7,6},{8,9},{9,8},{10,11... | collective-permute-start | bytes 2359304 | tf_op jit(solution)/shard_map/ppermute | solution.py:322
  8.9 26.4 %slice-start.1 = ((s8[6291456]{0:T(1024)(128)(4,1)}), s8[2097152]{0:T(1024)(128)(4,1)S(1)}, s32[]{:S(2)}) async-start(s8[6291456]{0:T(1024)(128)(4,1)} %bitcast.3), calls=%async_computation.1 | async-start | bytes 4194304
  12.6 10.4 %collective-permute-start.6 = (bf16[96,1024]{1,0:T(8,128)(2,1)S(1)}, bf16[96,1024]{1,0:T(8,128)(2,1)S(1)}, u32[]{:S(2)}, u32[]{:S(2)}) collective-permute-start(bf16[96,1024]{1,0:T(8,128)(2,1)S(1)} %get-tuple-element.59), channel_id=1, source_target_pairs={{0,0},{1,2},{2,1},{3,3},{4,4},{5,6},{6,5},{7,7},{8,11},{9,9},{10,1... | collective-permute-start | bytes 589832 | tf_op jit(solution)/shard_map/ppermute | solution.py:335
  16.1 8.8 %collective-permute-start.7 = (bf16[96,1024]{1,0:T(8,128)(2,1)S(1)}, bf16[96,1024]{1,0:T(8,128)(2,1)S(1)}, u32[]{:S(2)}, u32[]{:S(2)}) collective-permute-start(bf16[96,1024]{1,0:T(8,128)(2,1)S(1)} %get-tuple-element.60), channel_id=1, source_target_pairs={{0,4},{1,6},{2,5},{3,7},{4,0},{5,2},{6,1},{7,3},{8,15},{9,13},{10,... | collective-permute-start | bytes 589832 | tf_op jit(solution)/shard_map/ppermute | solution.py:335
  16.1 15.9 %collective-permute-start.8 = (bf16[96,1024]{1,0:T(8,128)(2,1)S(1)}, bf16[96,1024]{1,0:T(8,128)(2,1)S(1)}, u32[]{:S(2)}, u32[]{:S(2)}) collective-permute-start(bf16[96,1024]{1,0:T(8,128)(2,1)S(1)} %get-tuple-element.61), channel_id=1, source_target_pairs={{0,10},{1,8},{2,11},{3,9},{4,14},{5,12},{6,15},{7,13},{8,1},{9,3},... | collective-permute-start | bytes 589832 | tf_op jit(solution)/shard_map/ppermute | solution.py:335
  18.9 16.4 %collective-permute-start.9 = (bf16[96,1024]{1,0:T(8,128)(2,1)S(1)}, bf16[96,1024]{1,0:T(8,128)(2,1)S(1)}, u32[]{:S(2)}, u32[]{:S(2)}) collective-permute-start(bf16[96,1024]{1,0:T(8,128)(2,1)S(1)} %get-tuple-element.62), channel_id=1, source_target_pairs={{0,14},{1,12},{2,15},{3,13},{4,10},{5,8},{6,11},{7,9},{8,5},{9,7},... | collective-permute-start | bytes 589832 | tf_op jit(solution)/shard_map/ppermute | solution.py:335
  19.0 16.3 %copy-start.1 = (f32[2,1024]{1,0:T(2,128)S(1)}, f32[2,1024]{1,0:T(2,128)}, u32[]{:S(2)}) copy-start(f32[2,1024]{1,0:T(2,128)} %refs_4_.3) | copy-start | bytes 24580
  36.9 7.2 %collective-permute-start.10 = (bf16[384,1024]{1,0:T(8,128)(2,1)S(1)}, bf16[384,1024]{1,0:T(8,128)(2,1)S(1)}, u32[]{:S(2)}, u32[]{:S(2)}) collective-permute-start(bf16[384,1024]{1,0:T(8,128)(2,1)S(1)} %get-tuple-element.68.kv_ref), channel_id=1, source_target_pairs={{0,1},{1,0},{2,3},{3,2},{4,5},{5,4},{6,7},{7,6},{8,9},{9,8},{10,11... | collective-permute-start | bytes 2359304 | tf_op jit(solution)/shard_map/ppermute | solution.py:322
  37.0 8.5 %collective-permute-start.2 = (bf16[96,1024]{1,0:T(8,128)(2,1)S(1)}, bf16[96,1024]{1,0:T(8,128)(2,1)S(1)}, u32[]{:S(2)}, u32[]{:S(2)}) collective-permute-start(bf16[96,1024]{1,0:T(8,128)(2,1)S(1)} %get-tuple-element.55), channel_id=1, source_target_pairs={{0,0},{1,2},{2,1},{3,3},{4,4},{5,6},{6,5},{7,7},{8,11},{9,9},{10,1... | collective-permute-start | bytes 589832 | tf_op jit(solution)/shard_map/ppermute | solution.py:335
  40.4 8.6 %collective-permute-start.3 = (bf16[96,1024]{1,0:T(8,128)(2,1)S(1)}, bf16[96,1024]{1,0:T(8,128)(2,1)S(1)}, u32[]{:S(2)}, u32[]{:S(2)}) collective-permute-start(bf16[96,1024]{1,0:T(8,128)(2,1)S(1)} %get-tuple-element.56), channel_id=1, source_target_pairs={{0,4},{1,6},{2,5},{3,7},{4,0},{5,2},{6,1},{7,3},{8,15},{9,13},{10,... | collective-permute-start | bytes 589832 | tf_op jit(solution)/shard_map/ppermute | solution.py:335
  40.5 15.9 %collective-permute-start.4 = (bf16[96,1024]{1,0:T(8,128)(2,1)S(1)}, bf16[96,1024]{1,0:T(8,128)(2,1)S(1)}, u32[]{:S(2)}, u32[]{:S(2)}) collective-permute-start(bf16[96,1024]{1,0:T(8,128)(2,1)S(1)} %get-tuple-element.57), channel_id=1, source_target_pairs={{0,10},{1,8},{2,11},{3,9},{4,14},{5,12},{6,15},{7,13},{8,1},{9,3},... | collective-permute-start | bytes 589832 | tf_op jit(solution)/shard_map/ppermute | solution.py:335
  44.1 15.7 %collective-permute-start.5 = (bf16[96,1024]{1,0:T(8,128)(2,1)S(1)}, bf16[96,1024]{1,0:T(8,128)(2,1)S(1)}, u32[]{:S(2)}, u32[]{:S(2)}) collective-permute-start(bf16[96,1024]{1,0:T(8,128)(2,1)S(1)} %get-tuple-element.58), channel_id=1, source_target_pairs={{0,14},{1,12},{2,15},{3,13},{4,10},{5,8},{6,11},{7,9},{8,5},{9,7},... | collective-permute-start | bytes 589832 | tf_op jit(solution)/shard_map/ppermute | solution.py:335
  61.3 20.2 %copy-start = (bf16[2,512,1024]{2,1,0:T(8,128)(2,1)S(1)}, bf16[2,512,1024]{2,1,0:T(8,128)(2,1)}, u32[]{:S(2)}) copy-start(bf16[2,512,1024]{2,1,0:T(8,128)(2,1)} %w_ref.11) | copy-start | bytes 6291460
  61.3 7.0 %collective-permute-start.11 = (bf16[384,1024]{1,0:T(8,128)(2,1)S(1)}, bf16[384,1024]{1,0:T(8,128)(2,1)S(1)}, u32[]{:S(2)}, u32[]{:S(2)}) collective-permute-start(bf16[384,1024]{1,0:T(8,128)(2,1)S(1)} %get-tuple-element.75.kv_ref), channel_id=1, source_target_pairs={{0,1},{1,0},{2,3},{3,2},{4,5},{5,4},{6,7},{7,6},{8,9},{9,8},{10,11... | collective-permute-start | bytes 2359304 | tf_op jit(solution)/shard_map/ppermute | solution.py:322
  61.4 9.8 %collective-permute-start.17 = (bf16[96,512]{1,0:T(8,128)(2,1)S(1)}, bf16[96,512]{1,0:T(8,128)(2,1)S(1)}, u32[]{:S(2)}, u32[]{:S(2)}) collective-permute-start(bf16[96,512]{1,0:T(8,128)(2,1)S(1)} %get-tuple-element.82), channel_id=1, source_target_pairs={{0,4},{1,6},{2,5},{3,7},{4,0},{5,2},{6,1},{7,3},{8,15},{9,13},{10,... | collective-permute-start | bytes 294920 | tf_op jit(solution)/shard_map/ppermute | solution.py:335
  61.5 11.5 %collective-permute-start.18 = (bf16[96,512]{1,0:T(8,128)(2,1)S(1)}, bf16[96,512]{1,0:T(8,128)(2,1)S(1)}, u32[]{:S(2)}, u32[]{:S(2)}) collective-permute-start(bf16[96,512]{1,0:T(8,128)(2,1)S(1)} %get-tuple-element.83), channel_id=1, source_target_pairs={{0,10},{1,8},{2,11},{3,9},{4,14},{5,12},{6,15},{7,13},{8,1},{9,3},... | collective-permute-start | bytes 294920 | tf_op jit(solution)/shard_map/ppermute | solution.py:335
  65.2 14.4 %collective-permute-start.19 = (bf16[96,512]{1,0:T(8,128)(2,1)S(1)}, bf16[96,512]{1,0:T(8,128)(2,1)S(1)}, u32[]{:S(2)}, u32[]{:S(2)}) collective-permute-start(bf16[96,512]{1,0:T(8,128)(2,1)S(1)} %get-tuple-element.84), channel_id=1, source_target_pairs={{0,14},{1,12},{2,15},{3,13},{4,10},{5,8},{6,11},{7,9},{8,5},{9,7},... | collective-permute-start | bytes 294920 | tf_op jit(solution)/shard_map/ppermute | solution.py:335
  65.5 16.0 %collective-permute-start.16 = (bf16[96,512]{1,0:T(8,128)(2,1)S(1)}, bf16[96,512]{1,0:T(8,128)(2,1)S(1)}, u32[]{:S(2)}, u32[]{:S(2)}) collective-permute-start(bf16[96,512]{1,0:T(8,128)(2,1)S(1)} %get-tuple-element.69), channel_id=1, source_target_pairs={{0,0},{1,2},{2,1},{3,3},{4,4},{5,6},{6,5},{7,7},{8,11},{9,9},{10,1... | collective-permute-start | bytes 294920 | tf_op jit(solution)/shard_map/ppermute | solution.py:335
  69.7 13.6 %collective-permute-start.13 = (bf16[96,512]{1,0:T(8,128)(2,1)S(1)}, bf16[96,512]{1,0:T(8,128)(2,1)S(1)}, u32[]{:S(2)}, u32[]{:S(2)}) collective-permute-start(bf16[96,512]{1,0:T(8,128)(2,1)S(1)} %get-tuple-element.78), channel_id=1, source_target_pairs={{0,4},{1,6},{2,5},{3,7},{4,0},{5,2},{6,1},{7,3},{8,15},{9,13},{10,... | collective-permute-start | bytes 294920 | tf_op jit(solution)/shard_map/ppermute | solution.py:335
  71.2 12.1 %collective-permute-start.14 = (bf16[96,512]{1,0:T(8,128)(2,1)S(1)}, bf16[96,512]{1,0:T(8,128)(2,1)S(1)}, u32[]{:S(2)}, u32[]{:S(2)}) collective-permute-start(bf16[96,512]{1,0:T(8,128)(2,1)S(1)} %get-tuple-element.79), channel_id=1, source_target_pairs={{0,10},{1,8},{2,11},{3,9},{4,14},{5,12},{6,15},{7,13},{8,1},{9,3},... | collective-permute-start | bytes 294920 | tf_op jit(solution)/shard_map/ppermute | solution.py:335
  73.0 10.4 %collective-permute-start.15 = (bf16[96,512]{1,0:T(8,128)(2,1)S(1)}, bf16[96,512]{1,0:T(8,128)(2,1)S(1)}, u32[]{:S(2)}, u32[]{:S(2)}) collective-permute-start(bf16[96,512]{1,0:T(8,128)(2,1)S(1)} %get-tuple-element.80), channel_id=1, source_target_pairs={{0,14},{1,12},{2,15},{3,13},{4,10},{5,8},{6,11},{7,9},{8,5},{9,7},... | collective-permute-start | bytes 294920 | tf_op jit(solution)/shard_map/ppermute | solution.py:335
  79.6 5.9 %collective-permute-start.12 = (bf16[96,512]{1,0:T(8,128)(2,1)S(1)}, bf16[96,512]{1,0:T(8,128)(2,1)S(1)}, u32[]{:S(2)}, u32[]{:S(2)}) collective-permute-start(bf16[96,512]{1,0:T(8,128)(2,1)S(1)} %get-tuple-element.76), channel_id=1, source_target_pairs={{0,0},{1,2},{2,1},{3,3},{4,4},{5,6},{6,5},{7,7},{8,11},{9,9},{10,1... | collective-permute-start | bytes 294920 | tf_op jit(solution)/shard_map/ppermute | solution.py:335
where the time goes:
time: 87.5 us; the launch traced here: 87.3 us
  waiting for transfers between devices  35.1 us (40%)
  starting transfers between devices  26.9 us (31%)
  Pallas kernels  25.1 us (29%)
    ppermute x16, waiting for transfers between devices, exchange(): lax.ppermute(p, ('tm', 'space'), route(k))  35.1 us
    ppermute x16, starting transfers between devices, exchange(): lax.ppermute(p, ('tm', 'space'), route(k))  25.9 us
    pallas_call x2, Pallas kernels, height_project(): call(functools.partial(height_project_kernel, c), 3 * work, in_specs=[HBM...  8.08 us
    pallas_call x2, Pallas kernels, height(): call(functools.partial(height_kernel, c), 4 * work, in_specs=[SMEM, HBM]...  7.59 us
    pallas_call x2, Pallas kernels, finish(): call(functools.partial(finish_kernel, high), work, in_specs=[SMEM, whole(...  3.5 us
    pallas_call x2, Pallas kernels, time_project(): call(time_project_kernel, 3 * work, in_specs=[whole(each, feat)] * high +...  3.1 us
    pallas_call x2, Pallas kernels, timed(): call(time_kernel, 2 * work, in_specs=qkv_in, out_specs=[whole(each, inner...  2.81 us
  transfers between devices with their start and end apart: 20, of which 9 were waited for; matrix products, arithmetic and copies ran while one was open for 0% of the time, Pallas kernels for 19%

commit v1 on v0

--- a/solution.py
+++ b/solution.py
@@ -13,6 +13,7 @@
 QUAD = 4
 CHUNKS = 2
 COLB = 8
+SPLIT = 4
 POSB = 16
 NEG = -1e30
 VMEM_BYTES = 16 * 1024 * 1024
@@ -73,67 +74,66 @@
             put(span, lo, attend_quad(join(rows(q_ref, span, lo)), key, value, bias))
 
 
-def project(normed, weight, q_ref, kv_ref, inner):
-    for i, lo in enumerate((inner, 2 * inner, 0)):
-        part = jnp.dot(normed, weight(i), preferred_element_type=jnp.float32).astype(jnp.bfloat16)
-        if lo:
-            kv_ref[:, lo - inner : lo] = part
-        else:
-            q_ref[...] = part * jnp.bfloat16(HEAD**-0.5)
-
-
-def height_project_kernel(
-    c, x_ref, gain_ref, w_ref, q_ref, kv_ref, x_buf, w_buf, gain_buf, x_sem, w_sem, gain_sem
+def project(normed, w_ref, q_ref, kv_ref, inner):
+    kv_ref[...] = jnp.dot(
+        normed, w_ref[:, inner:], preferred_element_type=jnp.float32
+    ).astype(jnp.bfloat16)
+    q_ref[...] = jnp.dot(
+        normed, w_ref[:, :inner], preferred_element_type=jnp.float32
+    ).astype(jnp.bfloat16) * jnp.bfloat16(HEAD**-0.5)
+
+
+def load_project_kernel(
+    chunks, x_ref, gain_ref, w_ref, q_ref, kv_ref, w_out, gain_out, *refs
 ):
-    blocks, rows, colb, feat = x_buf.shape
+    x_outs = refs[:chunks]
+    x_sem, w_sem, gain_sem = refs[chunks:]
+    blocks, rows, colb, feat = x_outs[0].shape
     inner = q_ref.shape[1]
     loads = [
-        pltpu.make_async_copy(
-            x_ref.at[:, pl.ds((c * blocks + b) * colb, colb), :], x_buf.at[b], x_sem.at[b]
-        )
-        for b in range(blocks)
+        pltpu.make_async_copy(x_ref.at[:, pl.ds(i * colb, colb), :], x_out.at[b], x_sem.at[i])
+        for x_out, i, b in (
+            (x_outs[c], c * blocks + b, b) for c in range(chunks) for b in range(blocks)
+        )
     ]
+    step = feat // SPLIT
     fetches = [
         pltpu.make_async_copy(
-            w_ref.at[0, :, pl.ds(lo, inner)], w_buf.at[i], w_sem.at[i]
-        )
-        for i, lo in enumerate((inner, 2 * inner, 0))
+            w_ref.at[0, pl.ds(i * step, step), :], w_out.at[pl.ds(i * step, step), :], w_sem.at[i]
+        )
+        for i in range(SPLIT)
     ]
-    gain_load = pltpu.make_async_copy(gain_ref, gain_buf, gain_sem)
-    for copy in [gain_load] + loads + fetches:
+    gain_load = pltpu.make_async_copy(gain_ref, gain_out, gain_sem)
+    for copy in [gain_load] + loads[:blocks] + fetches + loads[blocks:]:
         copy.start()
     gain_load.wait()
     parts = []
     for b in range(blocks):
         loads[b].wait()
-        stream = x_buf[b].astype(jnp.float32).reshape(rows * colb, feat)
-        parts.append(normalise(stream, gain_buf[0:1, :]))
+        stream = x_outs[0][b].astype(jnp.float32).reshape(rows * colb, feat)
+        parts.append(normalise(stream, gain_out[0:1, :]))
     normed = jnp.concatenate(parts, axis=0)
-
-    def weight(i):
-        fetches[i].wait()
-        return w_buf[i]
-
-    project(normed, weight, q_ref, kv_ref, inner)
-
-
-def height_kernel(
-    c, hi_ref, x_ref, q_ref, kv_ref, other_ref, w_ref, *refs
-):
-    full_ref, mix_ref, x_buf, w_buf, x_sem, w_sem = refs[-6:]
-    piece_refs = refs[:-6]
-    blocks, rows, colb, feat = x_buf.shape
+    for fetch in fetches:
+        fetch.wait()
+    project(normed, w_out, q_ref, kv_ref, inner)
+    for load in loads[blocks:]:
+        load.wait()
+
+
+def height_project_kernel(x_ref, gain_ref, w_ref, q_ref, kv_ref):
+    blocks, rows, colb, feat = x_ref.shape
+    inner = q_ref.shape[1]
+    stream = x_ref[...].astype(jnp.float32).reshape(blocks * rows * colb, feat)
+    project(normalise(stream, gain_ref[0:1, :]), w_ref, q_ref, kv_ref, inner)
+
+
+def height_kernel(hi_ref, x_ref, q_ref, kv_ref, other_ref, w_ref, *refs):
+    full_ref, mix_ref, w_buf, w_sem = refs[-4:]
+    piece_refs = refs[:-4]
+    blocks, rows, colb, feat = x_ref.shape
     per = rows * colb
-    loads = [
-        pltpu.make_async_copy(
-            x_ref.at[:, pl.ds((c * blocks + b) * colb, colb), :], x_buf.at[b], x_sem.at[b]
-        )
-        for b in range(blocks)
-    ]
     fetch = pltpu.make_async_copy(w_ref.at[0], w_buf, w_sem)
     fetch.start()
-    for copy in loads:
-        copy.start()
 
     def put(span, lo, out):
         at, size = span[0]
@@ -142,8 +142,7 @@
     attend(q_ref, kv_ref, other_ref, [[(b * per, per)] for b in range(blocks)], colb, put)
     fetch.wait()
     for b in range(blocks):
-        loads[b].wait()
-        stream = x_buf[b].astype(jnp.float32).reshape(per, feat)
+        stream = x_ref[b].astype(jnp.float32).reshape(per, feat)
         update = jnp.dot(
             mix_ref[b * per : (b + 1) * per, :], w_buf[...], preferred_element_type=jnp.float32
         )
@@ -160,8 +159,11 @@
     normed = jnp.concatenate(
         [normalise(ref[...].astype(jnp.float32), gain_ref[1:2, :]) for ref in refs[:-4]], axis=0
     )
-    starts = (inner, 2 * inner, 0)
-    project(normed, lambda i: w_ref[:, starts[i] : starts[i] + inner], q_ref, kv_ref, inner)
+    project(normed, w_ref, q_ref, kv_ref, inner)
+
+
+def gate_kernel(in_ref, out_ref):
+    out_ref[0] = in_ref[0]
 
 
 def time_kernel(q_ref, kv_ref, other_ref, *mix_refs):
@@ -243,45 +245,64 @@
         ],
     )
     qkv_in = [whole(count, inner), whole(count, 2 * inner), whole(count, 2 * inner)]
-    x_scratch = pltpu.VMEM((blocks, rows, COLB, feat), bf)
     work = 2 * count * feat * inner
 
     def after(values, earlier):
         return lax.optimization_barrier((values, earlier))[0]
 
-    def height_project(c, x):
+    held = (blocks, rows, COLB, feat)
+    loaded = [(feat, 3 * inner), gains.shape] + [held] * CHUNKS
+    types = [bf, gains.dtype] + [bf] * CHUNKS
+
+    def load_project(x):
         return call(
-            functools.partial(height_project_kernel, c),
+            functools.partial(load_project_kernel, CHUNKS),
             3 * work,
             in_specs=[HBM, HBM, HBM],
+            out_specs=qkv_out["out_specs"] + [whole(*shape) for shape in loaded],
+            out_shape=qkv_out["out_shape"]
+            + [jax.ShapeDtypeStruct(shape, kind) for shape, kind in zip(loaded, types)],
             scratch_shapes=[
-                x_scratch,
-                pltpu.VMEM((3, feat, inner), bf),
-                pltpu.VMEM(gains.shape, gains.dtype),
-                pltpu.SemaphoreType.DMA((blocks,)),
-                pltpu.SemaphoreType.DMA((3,)),
+                pltpu.SemaphoreType.DMA((blocks * CHUNKS,)),
+                pltpu.SemaphoreType.DMA((SPLIT,)),
                 pltpu.SemaphoreType.DMA,
             ],
+        )(x, gains_far, qkv_far)
+
+    def height_project(x, gain, weight):
+        return call(
+            height_project_kernel,
+            3 * work,
+            in_specs=[whole(*held), whole(*gains.shape), whole(feat, 3 * inner)],
             **qkv_out,
-        )(x, gains_far, qkv_far)
-
-    def height(c, q, kv, other):
+        )(x, gain, weight)
+
+    def height(x, q, kv, other):
         outs = call(
-            functools.partial(height_kernel, c),
+            height_kernel,
             4 * work,
-            in_specs=[SMEM, HBM] + qkv_in + [HBM],
+            in_specs=[SMEM, whole(*held)] + qkv_in + [HBM],
             out_specs=[whole(each, feat)] * high + [whole(count, feat)],
             out_shape=[jax.ShapeDtypeStruct((each, feat), bf)] * high
             + [jax.ShapeDtypeStruct((count, feat), bf)],
             scratch_shapes=[
                 pltpu.VMEM((count, inner), bf),
-                x_scratch,
                 pltpu.VMEM((inner, feat), bf),
-                pltpu.SemaphoreType.DMA((blocks,)),
                 pltpu.SemaphoreType.DMA,
             ],
         )(hi, x, q, kv, other, out_far)
         return outs[:-1], outs[-1]
+
+    def gate(value):
+        return pl.pallas_call(
+            gate_kernel,
+            in_specs=[SMEM],
+            out_specs=SMEM,
+            out_shape=jax.ShapeDtypeStruct(value.shape, value.dtype),
+            compiler_params=params(),
+            cost_estimate=cost(1, 8),
+            name="gate",
+        )(value)
 
     def time_project(pieces):
         return call(
@@ -301,7 +322,7 @@
             out_shape=[jax.ShapeDtypeStruct((each, inner), bf)] * high,
         )(q, kv, other)
 
-    def finish(c, full, mixes, prior):
+    def finish(c, hi, full, mixes, prior):
         aliases, extra_specs, extra = {}, [], []
         if prior is not None:
             aliases = {high + 3: 0}
@@ -331,32 +352,46 @@
                     pairs.append(((z * 2 + lo) * 2 + s, to))
         return pairs
 
-    def exchange(pieces):
-        return [lax.ppermute(p, ("tm", "space"), route(k)) for k, p in enumerate(pieces)]
-
-    def after(values, earlier):
-        return lax.optimization_barrier((values, earlier))[0]
-
-    projected, others, heights, arrived, home = [], [], [], [], []
-    last = hi
-    for c in range(CHUNKS):
-        q, kv = height_project(c, after(x, last))
-        projected.append((q, kv))
-        others.append(swap(kv))
-        last = q
+    def permute(piece, k):
+        return lax.ppermute(piece, ("tm", "space"), route(k))
+
+    order = list(range(high - 1, -1, -1))
+
+    def exchange(pieces, ks):
+        return {k: permute(pieces[k], k) for k in ks}
+
+    q, kv, weight, gain, *xs = load_project(after(x, hi))
+    projected, others, heights, arrived, home = [(q, kv)], [], [], [], []
+    others.append(swap(kv))
+    for c in range(1, CHUNKS):
+        projected.append(height_project(after(xs[c], projected[-1][0]), gain, weight))
+        others.append(swap(projected[c][1]))
+    last = projected[-1][0]
     for c in range(CHUNKS):
         q, kv = projected[c]
-        heights.append(height(c, after(q, last), kv, others[c]))
+        heights.append(height(xs[c], after(q, last), kv, others[c]))
         last = heights[-1][1]
-        arrived.append(exchange(heights[-1][0]))
+        arrived.append(exchange(heights[-1][0], order))
+    heavy, light = order[: high // 2], order[high // 2 :]
+    mixes = None
     for c in range(CHUNKS):
-        q, kv = time_project(after(arrived[c], last))
-        mixes = timed(q, kv, swap(kv))
+        pieces = [arrived[c][k] for k in range(high)]
+        q, kv = time_project(after(pieces, last))
+        other = swap(kv)
+        if mixes is not None:
+            mixes = after(mixes, q)
+            home[-1].update(exchange(mixes, heavy))
+        mixes = timed(q, kv, other)
         last = mixes[0]
-        home.append(exchange(mixes))
+        home.append(exchange(mixes, light))
+        if c + 1 < CHUNKS:
+            hi = gate(after(hi, last))
+            last = hi
+    home[-1].update(exchange(mixes, heavy))
     out = None
     for c in range(CHUNKS):
-        out = finish(c, after(heights[c][1], last), home[c], out)
+        mixes = [home[c][k] for k in range(high)]
+        out = finish(c, hi, after(heights[c][1], last), mixes, out)
     return out[None]
 
 

time: 87.5 us -> 84.9 us (0.970)
  the two profiles are of different devices: /device:TPU:9 before, /device:TPU:1 now
where the time goes in v1:
time: 84.9 us; the launch traced here: 84.7 us
  starting transfers between devices  37.1 us (44%)
  Pallas kernels  23.7 us (28%)
  waiting for transfers between devices  23.6 us (28%)
    ppermute x16, starting transfers between devices, permute(): return lax.ppermute(piece, ('tm', 'space'), route(k))  36.3 us
    ppermute x16, waiting for transfers between devices, permute(): return lax.ppermute(piece, ('tm', 'space'), route(k))  23.5 us
    pallas_call x2, Pallas kernels, height(): call(height_kernel, 4 * work, in_specs=[SMEM, whole(*held)] + qkv_in + [H...  6.95 us
    pallas_call x2, Pallas kernels, finish(): call(functools.partial(finish_kernel, high), work, in_specs=[SMEM, whole(...  4.77 us
    pallas_call x1, Pallas kernels, load_project(): call(functools.partial(load_project_kernel, CHUNKS), 3 * work, in_specs=[...  4.02 us
    pallas_call x2, Pallas kernels, time_project(): call(time_project_kernel, 3 * work, in_specs=[whole(each, feat)] * high +...  3.1 us
    pallas_call x2, Pallas kernels, timed(): call(time_kernel, 2 * work, in_specs=qkv_in, out_specs=[whole(each, inner...  2.81 us
  transfers between devices with their start and end apart: 20, of which 6 were waited for; matrix products, arithmetic and copies ran while one was open for 0% of the time, Pallas kernels for 17%

profile of v1, /device:TPU:1, one launch (start us, length us, event | category | flops | bytes accessed | tf_op | source)
XLA Modules:
  0.0 84.7 jit_solution(11048300686612461624)
XLA Ops:
  0.0 4.0 %shard_map.46 = (bf16[384,512]{1,0:T(8,128)(2,1)S(1)}, bf16[384,1024]{1,0:T(8,128)(2,1)S(1)}, bf16[1024,1536]{1,0:T(8,128)(2,1)S(1)}, f32[2,1024]{1,0:T(2,128)S(...) custom-call(bf16[12,64,1024]{2,1,0:T(8,128)(2,1)} %bitcast.5, f32[2,1024]{1,0:T(2,128)} %refs_4_.3, ...), custom_call_target="tpu_custom_call" | custom-call | flops 1207959552 | bytes 1572864 | tf_op jit(solution)/shard_map/pallas_call | solution.py:258
  4.1 1.6 %shard_map.47 = (bf16[384,512]{1,0:T(8,128)(2,1)S(1)}, bf16[384,1024]{1,0:T(8,128)(2,1)S(1)}) custom-call(bf16[4,12,8,1024]{3,2,1,0:T(8,128)(2,1)S(1)} %get-tuple-element.56.x_ref, f32[2,1024]{1,0:T(2,128)S(1)} %get-tuple-element.57.gain_ref, bf16[1024,1536]{1,0:T(8,128)(2,1)S(1)} %get-tuple-element.58.w_ref), custom_call_target="tpu_custom_call" | custom-call | flops 1207959552 | bytes 1572864 | tf_op jit(solution)/shard_map/pallas_call | solution.py:273
  6.4 3.5 %shard_map.48 = (bf16[96,1024]{1,0:T(8,128)(2,1)S(1)}, bf16[96,1024]{1,0:T(8,128)(2,1)S(1)}, bf16[96,1024]{1,0:T(8,128)(2,1)S(1)}, bf16[96,1024]{1,0:T(8,128)(2,1)S(1)}, bf16[384,1024]{1,0:T(8,128)(2,1)S(1)}) custom-call(s32[1]{0:T(128)} %bitcast.hi_ref.in_ref, bf16[4,12,8,1024]{3,2,1,0:T(8,128)(2,1)S(1)} %get-tuple-element.53.x_ref, ...), custom_call_target="tpu_custom_call" | custom-call | flops 1610612736 | bytes 1572864 | tf_op jit(solution)/shard_map/pallas_call | solution.py:281
  9.9 4.5 %collective-permute-start.1 = (bf16[96,1024]{1,0:T(8,128)(2,1)S(1)}, bf16[96,1024]{1,0:T(8,128)(2,1)S(1)}, u32[]{:S(2)}, u32[]{:S(2)}) collective-permute-start(bf16[96,1024]{1,0:T(8,128)(2,1)S(1)} %get-tuple-element.62), channel_id=1, source_target_pairs={{0,0},{1,2},{2,1},{3,3},{4,4},{5,6},{6,5},{7,7},{8,11},{9,9},{10,1... | collective-permute-start | bytes 589832 | tf_op jit(solution)/shard_map/ppermute | solution.py:356
  15.7 2.6 %collective-permute-start.3 = (bf16[96,1024]{1,0:T(8,128)(2,1)S(1)}, bf16[96,1024]{1,0:T(8,128)(2,1)S(1)}, u32[]{:S(2)}, u32[]{:S(2)}) collective-permute-start(bf16[96,1024]{1,0:T(8,128)(2,1)S(1)} %get-tuple-element.64), channel_id=1, source_target_pairs={{0,10},{1,8},{2,11},{3,9},{4,14},{5,12},{6,15},{7,13},{8,1},{9,3},... | collective-permute-start | bytes 589832 | tf_op jit(solution)/shard_map/ppermute | solution.py:356
  18.3 3.5 %shard_map.49 = (bf16[96,1024]{1,0:T(8,128)(2,1)S(1)}, bf16[96,1024]{1,0:T(8,128)(2,1)S(1)}, bf16[96,1024]{1,0:T(8,128)(2,1)S(1)}, bf16[96,1024]{1,0:T(8,128)(2,1)S(1)}, bf16[384,1024]{1,0:T(8,128)(2,1)S(1)}) custom-call(s32[1]{0:T(128)} %bitcast.hi_ref.in_ref, bf16[4,12,8,1024]{3,2,1,0:T(8,128)(2,1)S(1)} %get-tuple-element.56.x_ref, ...), custom_call_target="tpu_custom_call" | custom-call | flops 1610612736 | bytes 1572864 | tf_op jit(solution)/shard_map/pallas_call | solution.py:281
  21.8 1.5 %collective-permute-done.2.refs_1_ = bf16[96,1024]{1,0:T(8,128)(2,1)S(1)} collective-permute-done((bf16[96,1024]{1,0:T(8,128)(2,1)S(1)}, bf16[96,1024]{1,0:T(8,128)(2,1)S(1)}, u32[]{:S(2)}, u32[]{:S(2)}) %collective-permute-start.2) | collective-permute-done | bytes 196640 | tf_op jit(solution)/shard_map/ppermute | solution.py:356
  23.3 7.8 %collective-permute-done.3.refs_2_ = bf16[96,1024]{1,0:T(8,128)(2,1)S(1)} collective-permute-done((bf16[96,1024]{1,0:T(8,128)(2,1)S(1)}, bf16[96,1024]{1,0:T(8,128)(2,1)S(1)}, u32[]{:S(2)}, u32[]{:S(2)}) %collective-permute-start.3) | collective-permute-done | bytes 196640 | tf_op jit(solution)/shard_map/ppermute | solution.py:356
  31.2 1.6 %shard_map.50 = (bf16[384,512]{1,0:T(8,128)(2,1)S(1)}, bf16[384,1024]{1,0:T(8,128)(2,1)S(1)}) custom-call(bf16[96,1024]{1,0:T(8,128)(2,1)S(1)} %collective-permute-done.1.refs_0_, bf16[96,1024]{1,0:T(8,128)(2,1)S(1)} %collective-permute-done.2.refs_1_, bf16[96,1024]{1,0:T(8,128)(2,1)S(1)} %collective-permute-done.3.refs_2_, ...), custom_call_target="tpu_custom_call" | custom-call | flops 1207959552 | bytes 1572864 | tf_op jit(solution)/shard_map/pallas_call | solution.py:308
  32.8 4.5 %collective-permute-start.7 = (bf16[96,1024]{1,0:T(8,128)(2,1)S(1)}, bf16[96,1024]{1,0:T(8,128)(2,1)S(1)}, u32[]{:S(2)}, u32[]{:S(2)}) collective-permute-start(bf16[96,1024]{1,0:T(8,128)(2,1)S(1)} %get-tuple-element.78), channel_id=1, source_target_pairs={{0,0},{1,2},{2,1},{3,3},{4,4},{5,6},{6,5},{7,7},{8,11},{9,9},{10,1... | collective-permute-start | bytes 589832 | tf_op jit(solution)/shard_map/ppermute | solution.py:356
  37.3 2.7 %collective-permute-start.8 = (bf16[96,1024]{1,0:T(8,128)(2,1)S(1)}, bf16[96,1024]{1,0:T(8,128)(2,1)S(1)}, u32[]{:S(2)}, u32[]{:S(2)}) collective-permute-start(bf16[96,1024]{1,0:T(8,128)(2,1)S(1)} %get-tuple-element.79), channel_id=1, source_target_pairs={{0,4},{1,6},{2,5},{3,7},{4,0},{5,2},{6,1},{7,3},{8,15},{9,13},{10,... | collective-permute-start | bytes 589832 | tf_op jit(solution)/shard_map/ppermute | solution.py:356
  40.0 1.5 %collective-permute-start.9 = (bf16[96,1024]{1,0:T(8,128)(2,1)S(1)}, bf16[96,1024]{1,0:T(8,128)(2,1)S(1)}, u32[]{:S(2)}, u32[]{:S(2)}) collective-permute-start(bf16[96,1024]{1,0:T(8,128)(2,1)S(1)} %get-tuple-element.80), channel_id=1, source_target_pairs={{0,10},{1,8},{2,11},{3,9},{4,14},{5,12},{6,15},{7,13},{8,1},{9,3},... | collective-permute-start | bytes 589832 | tf_op jit(solution)/shard_map/ppermute | solution.py:356
  41.5 1.9 %collective-permute-start.10 = (bf16[96,1024]{1,0:T(8,128)(2,1)S(1)}, bf16[96,1024]{1,0:T(8,128)(2,1)S(1)}, u32[]{:S(2)}, u32[]{:S(2)}) collective-permute-start(bf16[96,1024]{1,0:T(8,128)(2,1)S(1)} %get-tuple-element.81), channel_id=1, source_target_pairs={{0,14},{1,12},{2,15},{3,13},{4,10},{5,8},{6,11},{7,9},{8,5},{9,7},... | collective-permute-start | bytes 589832 | tf_op jit(solution)/shard_map/ppermute | solution.py:356
  46.5 10.3 %collective-permute-done.9.refs_2_ = bf16[96,1024]{1,0:T(8,128)(2,1)S(1)} collective-permute-done((bf16[96,1024]{1,0:T(8,128)(2,1)S(1)}, bf16[96,1024]{1,0:T(8,128)(2,1)S(1)}, u32[]{:S(2)}, u32[]{:S(2)}) %collective-permute-start.9) | collective-permute-done | bytes 196640 | tf_op jit(solution)/shard_map/ppermute | solution.py:356
  56.8 1.5 %shard_map.52 = (bf16[384,512]{1,0:T(8,128)(2,1)S(1)}, bf16[384,1024]{1,0:T(8,128)(2,1)S(1)}) custom-call(bf16[96,1024]{1,0:T(8,128)(2,1)S(1)} %collective-permute-done.7.refs_0_, bf16[96,1024]{1,0:T(8,128)(2,1)S(1)} %collective-permute-done.8.refs_1_, bf16[96,1024]{1,0:T(8,128)(2,1)S(1)} %collective-permute-done.9.refs_2_, ...), custom_call_target="tpu_custom_call" | custom-call | flops 1207959552 | bytes 1572864 | tf_op jit(solution)/shard_map/pallas_call | solution.py:308
  58.4 3.4 %collective-permute-start.16 = (bf16[96,512]{1,0:T(8,128)(2,1)S(1)}, bf16[96,512]{1,0:T(8,128)(2,1)S(1)}, u32[]{:S(2)}, u32[]{:S(2)}) collective-permute-start(bf16[96,512]{1,0:T(8,128)(2,1)S(1)} %get-tuple-element.76), channel_id=1, source_target_pairs={{0,0},{1,2},{2,1},{3,3},{4,4},{5,6},{6,5},{7,7},{8,11},{9,9},{10,1... | collective-permute-start | bytes 294920 | tf_op jit(solution)/shard_map/ppermute | solution.py:356
  61.8 3.0 %collective-permute-start.17 = (bf16[96,512]{1,0:T(8,128)(2,1)S(1)}, bf16[96,512]{1,0:T(8,128)(2,1)S(1)}, u32[]{:S(2)}, u32[]{:S(2)}) collective-permute-start(bf16[96,512]{1,0:T(8,128)(2,1)S(1)} %get-tuple-element.94), channel_id=1, source_target_pairs={{0,4},{1,6},{2,5},{3,7},{4,0},{5,2},{6,1},{7,3},{8,15},{9,13},{10,... | collective-permute-start | bytes 294920 | tf_op jit(solution)/shard_map/ppermute | solution.py:356
  66.0 2.0 %collective-permute-start.19 = (bf16[96,512]{1,0:T(8,128)(2,1)S(1)}, bf16[96,512]{1,0:T(8,128)(2,1)S(1)}, u32[]{:S(2)}, u32[]{:S(2)}) collective-permute-start(bf16[96,512]{1,0:T(8,128)(2,1)S(1)} %get-tuple-element.98), channel_id=1, source_target_pairs={{0,14},{1,12},{2,15},{3,13},{4,10},{5,8},{6,11},{7,9},{8,5},{9,7},... | collective-permute-start | bytes 294920 | tf_op jit(solution)/shard_map/ppermute | solution.py:356
  68.0 1.4 %shard_map.53 = (bf16[96,512]{1,0:T(8,128)(2,1)S(1)}, bf16[96,512]{1,0:T(8,128)(2,1)S(1)}, bf16[96,512]{1,0:T(8,128)(2,1)S(1)}, bf16[96,512]{1,0:T(8,128)(2,1)S(1)}) custom-call(bf16[384,512]{1,0:T(8,128)(2,1)S(1)} %get-tuple-element.86.q_ref, bf16[384,1024]{1,0:T(8,128)(2,1)S(1)} %get-tuple-element.87.kv_ref, ...), custom_call_target="tpu_custom_call" | custom-call | flops 805306368 | bytes 1572864 | tf_op jit(solution)/shard_map/pallas_call | solution.py:317
  70.3 1.8 %collective-permute-start.14 = (bf16[96,512]{1,0:T(8,128)(2,1)S(1)}, bf16[96,512]{1,0:T(8,128)(2,1)S(1)}, u32[]{:S(2)}, u32[]{:S(2)}) collective-permute-start(bf16[96,512]{1,0:T(8,128)(2,1)S(1)} %get-tuple-element.91), channel_id=1, source_target_pairs={{0,10},{1,8},{2,11},{3,9},{4,14},{5,12},{6,15},{7,13},{8,1},{9,3},... | collective-permute-start | bytes 294920 | tf_op jit(solution)/shard_map/ppermute | solution.py:356
  73.6 3.6 %collective-permute-start.12 = (bf16[96,512]{1,0:T(8,128)(2,1)S(1)}, bf16[96,512]{1,0:T(8,128)(2,1)S(1)}, u32[]{:S(2)}, u32[]{:S(2)}) collective-permute-start(bf16[96,512]{1,0:T(8,128)(2,1)S(1)} %get-tuple-element.88), channel_id=1, source_target_pairs={{0,0},{1,2},{2,1},{3,3},{4,4},{5,6},{6,5},{7,7},{8,11},{9,9},{10,1... | collective-permute-start | bytes 294920 | tf_op jit(solution)/shard_map/ppermute | solution.py:356
  77.2 2.4 %shard_map.54.refs_4_ = bf16[12,64,1024]{2,1,0:T(8,128)(2,1)} custom-call(s32[1]{0:T(128)} %gate.1.hi_ref, bf16[384,1024]{1,0:T(8,128)(2,1)S(1)} %get-tuple-element.93.full_ref, bf16[2,512,1024]{2,1,0:T(8,128)(2,1)S(1)} %copy-done, bf16[96,512]{1,0:T(8,128)(2,1)S(1)} %collective-permute-done.16.refs_0_, bf16[96,512]{1,0:T(8,128)(2,1)S(1)} %collective-permute-done.17.refs_1_, ...), custom_call_target="tpu_custom_call" | custom-call | flops 402653184 | bytes 1572864 | tf_op jit(solution)/shard_map/pallas_call | solution.py:330
  79.6 2.7 %collective-permute-done.14.refs_2_ = bf16[96,512]{1,0:T(8,128)(2,1)S(1)} collective-permute-done((bf16[96,512]{1,0:T(8,128)(2,1)S(1)}, bf16[96,512]{1,0:T(8,128)(2,1)S(1)}, u32[]{:S(2)}, u32[]{:S(2)}) %collective-permute-start.14) | collective-permute-done | bytes 98336 | tf_op jit(solution)/shard_map/ppermute | solution.py:356
  82.3 2.4 %shard_map.55 = bf16[12,64,1024]{2,1,0:T(8,128)(2,1)} custom-call(s32[1]{0:T(128)} %gate.1.hi_ref, bf16[384,1024]{1,0:T(8,128)(2,1)S(1)} %get-tuple-element.89.full_ref, bf16[2,512,1024]{2,1,0:T(8,128)(2,1)S(1)} %copy-done, bf16[96,512]{1,0:T(8,128)(2,1)S(1)} %collective-permute-done.12.refs_0_, ...), custom_call_target="tpu_custom_call", output_to_operand_aliasing={{}: (7, {})} | custom-call | flops 402653184 | bytes 1572864 | tf_op jit(solution)/shard_map/pallas_call | solution.py:330
  (36 shorter events, 8.9 us)
Async XLA Ops:
  4.0 2.4 %collective-permute-start = (bf16[384,1024]{1,0:T(8,128)(2,1)S(1)}, bf16[384,1024]{1,0:T(8,128)(2,1)S(1)}, u32[]{:S(2)}, u32[]{:S(2)}) collective-permute-start(bf16[384,1024]{1,0:T(8,128)(2,1)S(1)} %get-tuple-element.61.kv_ref), channel_id=1, source_target_pairs={{0,1},{1,0},{2,3},{3,2},{4,5},{5,4},{6,7},{7,6},{8,9},{9,8},{10,11... | collective-permute-start | bytes 2359304 | tf_op jit(solution)/shard_map/ppermute | solution.py:343
  4.1 27.0 %slice-start = ((s8[6291456]{0:T(1024)(128)(4,1)}), s8[4194304]{0:T(1024)(128)(4,1)S(1)}, s32[]{:S(2)}) async-start(s8[6291456]{0:T(1024)(128)(4,1)} %bitcast.3), calls=%async_computation | async-start | bytes 8388608
  5.7 12.6 %collective-permute-start.5 = (bf16[384,1024]{1,0:T(8,128)(2,1)S(1)}, bf16[384,1024]{1,0:T(8,128)(2,1)S(1)}, u32[]{:S(2)}, u32[]{:S(2)}) collective-permute-start(bf16[384,1024]{1,0:T(8,128)(2,1)S(1)} %get-tuple-element.68.kv_ref), channel_id=1, source_target_pairs={{0,1},{1,0},{2,3},{3,2},{4,5},{5,4},{6,7},{7,6},{8,9},{9,8},{10,11... | collective-permute-start | bytes 2359304 | tf_op jit(solution)/shard_map/ppermute | solution.py:343
  6.4 24.8 %slice-start.1 = ((s8[6291456]{0:T(1024)(128)(4,1)}), s8[2097152]{0:T(1024)(128)(4,1)S(1)}, s32[]{:S(2)}) async-start(s8[6291456]{0:T(1024)(128)(4,1)} %bitcast.3), calls=%async_computation.1 | async-start | bytes 4194304
  9.9 11.9 %collective-permute-start.1 = (bf16[96,1024]{1,0:T(8,128)(2,1)S(1)}, bf16[96,1024]{1,0:T(8,128)(2,1)S(1)}, u32[]{:S(2)}, u32[]{:S(2)}) collective-permute-start(bf16[96,1024]{1,0:T(8,128)(2,1)S(1)} %get-tuple-element.62), channel_id=1, source_target_pairs={{0,0},{1,2},{2,1},{3,3},{4,4},{5,6},{6,5},{7,7},{8,11},{9,9},{10,1... | collective-permute-start | bytes 589832 | tf_op jit(solution)/shard_map/ppermute | solution.py:356
  14.4 9.0 %collective-permute-start.2 = (bf16[96,1024]{1,0:T(8,128)(2,1)S(1)}, bf16[96,1024]{1,0:T(8,128)(2,1)S(1)}, u32[]{:S(2)}, u32[]{:S(2)}) collective-permute-start(bf16[96,1024]{1,0:T(8,128)(2,1)S(1)} %get-tuple-element.63), channel_id=1, source_target_pairs={{0,4},{1,6},{2,5},{3,7},{4,0},{5,2},{6,1},{7,3},{8,15},{9,13},{10,... | collective-permute-start | bytes 589832 | tf_op jit(solution)/shard_map/ppermute | solution.py:356
  15.7 15.4 %collective-permute-start.3 = (bf16[96,1024]{1,0:T(8,128)(2,1)S(1)}, bf16[96,1024]{1,0:T(8,128)(2,1)S(1)}, u32[]{:S(2)}, u32[]{:S(2)}) collective-permute-start(bf16[96,1024]{1,0:T(8,128)(2,1)S(1)} %get-tuple-element.64), channel_id=1, source_target_pairs={{0,10},{1,8},{2,11},{3,9},{4,14},{5,12},{6,15},{7,13},{8,1},{9,3},... | collective-permute-start | bytes 589832 | tf_op jit(solution)/shard_map/ppermute | solution.py:356
  18.3 12.8 %collective-permute-start.4 = (bf16[96,1024]{1,0:T(8,128)(2,1)S(1)}, bf16[96,1024]{1,0:T(8,128)(2,1)S(1)}, u32[]{:S(2)}, u32[]{:S(2)}) collective-permute-start(bf16[96,1024]{1,0:T(8,128)(2,1)S(1)} %get-tuple-element.65), channel_id=1, source_target_pairs={{0,14},{1,12},{2,15},{3,13},{4,10},{5,8},{6,11},{7,9},{8,5},{9,7},... | collective-permute-start | bytes 589832 | tf_op jit(solution)/shard_map/ppermute | solution.py:356
  18.3 12.9 %copy-start.1 = (f32[2,1024]{1,0:T(2,128)S(1)}, f32[2,1024]{1,0:T(2,128)}, u32[]{:S(2)}) copy-start(f32[2,1024]{1,0:T(2,128)} %refs_4_.3) | copy-start | bytes 24580
  32.7 10.7 %collective-permute-start.6 = (bf16[384,1024]{1,0:T(8,128)(2,1)S(1)}, bf16[384,1024]{1,0:T(8,128)(2,1)S(1)}, u32[]{:S(2)}, u32[]{:S(2)}) collective-permute-start(bf16[384,1024]{1,0:T(8,128)(2,1)S(1)} %get-tuple-element.75.kv_ref), channel_id=1, source_target_pairs={{0,1},{1,0},{2,3},{3,2},{4,5},{5,4},{6,7},{7,6},{8,9},{9,8},{10,11... | collective-permute-start | bytes 2359304 | tf_op jit(solution)/shard_map/ppermute | solution.py:343
  32.8 12.5 %collective-permute-start.7 = (bf16[96,1024]{1,0:T(8,128)(2,1)S(1)}, bf16[96,1024]{1,0:T(8,128)(2,1)S(1)}, u32[]{:S(2)}, u32[]{:S(2)}) collective-permute-start(bf16[96,1024]{1,0:T(8,128)(2,1)S(1)} %get-tuple-element.78), channel_id=1, source_target_pairs={{0,0},{1,2},{2,1},{3,3},{4,4},{5,6},{6,5},{7,7},{8,11},{9,9},{10,1... | collective-permute-start | bytes 589832 | tf_op jit(solution)/shard_map/ppermute | solution.py:356
  37.3 9.1 %collective-permute-start.8 = (bf16[96,1024]{1,0:T(8,128)(2,1)S(1)}, bf16[96,1024]{1,0:T(8,128)(2,1)S(1)}, u32[]{:S(2)}, u32[]{:S(2)}) collective-permute-start(bf16[96,1024]{1,0:T(8,128)(2,1)S(1)} %get-tuple-element.79), channel_id=1, source_target_pairs={{0,4},{1,6},{2,5},{3,7},{4,0},{5,2},{6,1},{7,3},{8,15},{9,13},{10,... | collective-permute-start | bytes 589832 | tf_op jit(solution)/shard_map/ppermute | solution.py:356
  40.0 16.8 %collective-permute-start.9 = (bf16[96,1024]{1,0:T(8,128)(2,1)S(1)}, bf16[96,1024]{1,0:T(8,128)(2,1)S(1)}, u32[]{:S(2)}, u32[]{:S(2)}) collective-permute-start(bf16[96,1024]{1,0:T(8,128)(2,1)S(1)} %get-tuple-element.80), channel_id=1, source_target_pairs={{0,10},{1,8},{2,11},{3,9},{4,14},{5,12},{6,15},{7,13},{8,1},{9,3},... | collective-permute-start | bytes 589832 | tf_op jit(solution)/shard_map/ppermute | solution.py:356
  41.5 15.3 %collective-permute-start.10 = (bf16[96,1024]{1,0:T(8,128)(2,1)S(1)}, bf16[96,1024]{1,0:T(8,128)(2,1)S(1)}, u32[]{:S(2)}, u32[]{:S(2)}) collective-permute-start(bf16[96,1024]{1,0:T(8,128)(2,1)S(1)} %get-tuple-element.81), channel_id=1, source_target_pairs={{0,14},{1,12},{2,15},{3,13},{4,10},{5,8},{6,11},{7,9},{8,5},{9,7},... | collective-permute-start | bytes 589832 | tf_op jit(solution)/shard_map/ppermute | solution.py:356
  58.3 18.9 %copy-start = (bf16[2,512,1024]{2,1,0:T(8,128)(2,1)S(1)}, bf16[2,512,1024]{2,1,0:T(8,128)(2,1)}, u32[]{:S(2)}) copy-start(bf16[2,512,1024]{2,1,0:T(8,128)(2,1)} %w_ref.9) | copy-start | bytes 6291460
  58.3 9.6 %collective-permute-start.11 = (bf16[384,1024]{1,0:T(8,128)(2,1)S(1)}, bf16[384,1024]{1,0:T(8,128)(2,1)S(1)}, u32[]{:S(2)}, u32[]{:S(2)}) collective-permute-start(bf16[384,1024]{1,0:T(8,128)(2,1)S(1)} %get-tuple-element.87.kv_ref), channel_id=1, source_target_pairs={{0,1},{1,0},{2,3},{3,2},{4,5},{5,4},{6,7},{7,6},{8,9},{9,8},{10,11... | collective-permute-start | bytes 2359304 | tf_op jit(solution)/shard_map/ppermute | solution.py:343
  58.4 13.8 %collective-permute-start.16 = (bf16[96,512]{1,0:T(8,128)(2,1)S(1)}, bf16[96,512]{1,0:T(8,128)(2,1)S(1)}, u32[]{:S(2)}, u32[]{:S(2)}) collective-permute-start(bf16[96,512]{1,0:T(8,128)(2,1)S(1)} %get-tuple-element.76), channel_id=1, source_target_pairs={{0,0},{1,2},{2,1},{3,3},{4,4},{5,6},{6,5},{7,7},{8,11},{9,9},{10,1... | collective-permute-start | bytes 294920 | tf_op jit(solution)/shard_map/ppermute | solution.py:356
  61.8 8.5 %collective-permute-start.17 = (bf16[96,512]{1,0:T(8,128)(2,1)S(1)}, bf16[96,512]{1,0:T(8,128)(2,1)S(1)}, u32[]{:S(2)}, u32[]{:S(2)}) collective-permute-start(bf16[96,512]{1,0:T(8,128)(2,1)S(1)} %get-tuple-element.94), channel_id=1, source_target_pairs={{0,4},{1,6},{2,5},{3,7},{4,0},{5,2},{6,1},{7,3},{8,15},{9,13},{10,... | collective-permute-start | bytes 294920 | tf_op jit(solution)/shard_map/ppermute | solution.py:356
  64.7 8.8 %collective-permute-start.18 = (bf16[96,512]{1,0:T(8,128)(2,1)S(1)}, bf16[96,512]{1,0:T(8,128)(2,1)S(1)}, u32[]{:S(2)}, u32[]{:S(2)}) collective-permute-start(bf16[96,512]{1,0:T(8,128)(2,1)S(1)} %get-tuple-element.97), channel_id=1, source_target_pairs={{0,10},{1,8},{2,11},{3,9},{4,14},{5,12},{6,15},{7,13},{8,1},{9,3},... | collective-permute-start | bytes 294920 | tf_op jit(solution)/shard_map/ppermute | solution.py:356
  66.0 11.2 %collective-permute-start.19 = (bf16[96,512]{1,0:T(8,128)(2,1)S(1)}, bf16[96,512]{1,0:T(8,128)(2,1)S(1)}, u32[]{:S(2)}, u32[]{:S(2)}) collective-permute-start(bf16[96,512]{1,0:T(8,128)(2,1)S(1)} %get-tuple-element.98), channel_id=1, source_target_pairs={{0,14},{1,12},{2,15},{3,13},{4,10},{5,8},{6,11},{7,9},{8,5},{9,7},... | collective-permute-start | bytes 294920 | tf_op jit(solution)/shard_map/ppermute | solution.py:356
  69.4 10.2 %collective-permute-start.13 = (bf16[96,512]{1,0:T(8,128)(2,1)S(1)}, bf16[96,512]{1,0:T(8,128)(2,1)S(1)}, u32[]{:S(2)}, u32[]{:S(2)}) collective-permute-start(bf16[96,512]{1,0:T(8,128)(2,1)S(1)} %get-tuple-element.90), channel_id=1, source_target_pairs={{0,4},{1,6},{2,5},{3,7},{4,0},{5,2},{6,1},{7,3},{8,15},{9,13},{10,... | collective-permute-start | bytes 294920 | tf_op jit(solution)/shard_map/ppermute | solution.py:356
  70.3 12.0 %collective-permute-start.14 = (bf16[96,512]{1,0:T(8,128)(2,1)S(1)}, bf16[96,512]{1,0:T(8,128)(2,1)S(1)}, u32[]{:S(2)}, u32[]{:S(2)}) collective-permute-start(bf16[96,512]{1,0:T(8,128)(2,1)S(1)} %get-tuple-element.91), channel_id=1, source_target_pairs={{0,10},{1,8},{2,11},{3,9},{4,14},{5,12},{6,15},{7,13},{8,1},{9,3},... | collective-permute-start | bytes 294920 | tf_op jit(solution)/shard_map/ppermute | solution.py:356
  72.2 10.1 %collective-permute-start.15 = (bf16[96,512]{1,0:T(8,128)(2,1)S(1)}, bf16[96,512]{1,0:T(8,128)(2,1)S(1)}, u32[]{:S(2)}, u32[]{:S(2)}) collective-permute-start(bf16[96,512]{1,0:T(8,128)(2,1)S(1)} %get-tuple-element.92), channel_id=1, source_target_pairs={{0,14},{1,12},{2,15},{3,13},{4,10},{5,8},{6,11},{7,9},{8,5},{9,7},... | collective-permute-start | bytes 294920 | tf_op jit(solution)/shard_map/ppermute | solution.py:356
  73.6 8.7 %collective-permute-start.12 = (bf16[96,512]{1,0:T(8,128)(2,1)S(1)}, bf16[96,512]{1,0:T(8,128)(2,1)S(1)}, u32[]{:S(2)}, u32[]{:S(2)}) collective-permute-start(bf16[96,512]{1,0:T(8,128)(2,1)S(1)} %get-tuple-element.88), channel_id=1, source_target_pairs={{0,0},{1,2},{2,1},{3,3},{4,4},{5,6},{6,5},{7,7},{8,11},{9,9},{10,1... | collective-permute-start | bytes 294920 | tf_op jit(solution)/shard_map/ppermute | solution.py:356

commit v2 on v1

--- a/solution.py
+++ b/solution.py
@@ -74,27 +74,31 @@
             put(span, lo, attend_quad(join(rows(q_ref, span, lo)), key, value, bias))
 
 
-def project(normed, w_ref, q_ref, kv_ref, inner):
+def project_keys(normed, w_ref, kv_ref):
+    inner = kv_ref.shape[1] // 2
     kv_ref[...] = jnp.dot(
         normed, w_ref[:, inner:], preferred_element_type=jnp.float32
     ).astype(jnp.bfloat16)
+
+
+def project_queries(normed, w_ref, q_ref):
     q_ref[...] = jnp.dot(
-        normed, w_ref[:, :inner], preferred_element_type=jnp.float32
+        normed, w_ref[:, : q_ref.shape[1]], preferred_element_type=jnp.float32
     ).astype(jnp.bfloat16) * jnp.bfloat16(HEAD**-0.5)
 
 
-def load_project_kernel(
-    chunks, x_ref, gain_ref, w_ref, q_ref, kv_ref, w_out, gain_out, *refs
-):
-    x_outs = refs[:chunks]
-    x_sem, w_sem, gain_sem = refs[chunks:]
+def load_kernel(x_ref, gain_ref, w_ref, kv_ref, normed_ref, w_out, gain_out, *refs):
+    x_outs, (x_sem, w_sem, gain_sem) = refs[:CHUNKS], refs[CHUNKS:]
     blocks, rows, colb, feat = x_outs[0].shape
-    inner = q_ref.shape[1]
+    inner = kv_ref.shape[1] // 2
     loads = [
-        pltpu.make_async_copy(x_ref.at[:, pl.ds(i * colb, colb), :], x_out.at[b], x_sem.at[i])
-        for x_out, i, b in (
-            (x_outs[c], c * blocks + b, b) for c in range(chunks) for b in range(blocks)
-        )
+        pltpu.make_async_copy(
+            x_ref.at[:, pl.ds((c * blocks + b) * colb, colb), :],
+            x_outs[c].at[b],
+            x_sem.at[c * blocks + b],
+        )
+        for c in range(CHUNKS)
+        for b in range(blocks)
     ]
     step = feat // SPLIT
     fetches = [
@@ -107,59 +111,66 @@
     for copy in [gain_load] + loads[:blocks] + fetches + loads[blocks:]:
         copy.start()
     gain_load.wait()
-    parts = []
+    per = rows * colb
     for b in range(blocks):
         loads[b].wait()
-        stream = x_outs[0][b].astype(jnp.float32).reshape(rows * colb, feat)
-        parts.append(normalise(stream, gain_out[0:1, :]))
-    normed = jnp.concatenate(parts, axis=0)
-    for fetch in fetches:
+        stream = x_outs[0][b].astype(jnp.float32).reshape(per, feat)
+        normed_ref[b * per : (b + 1) * per, :] = normalise(stream, gain_out[0:1, :])
+    total = None
+    for i, fetch in enumerate(fetches):
         fetch.wait()
-    project(normed, w_out, q_ref, kv_ref, inner)
+        span = slice(i * step, (i + 1) * step)
+        part = jnp.dot(
+            normed_ref[:, span], w_out[span, inner:], preferred_element_type=jnp.float32
+        )
+        total = part if total is None else total + part
+    kv_ref[...] = total.astype(jnp.bfloat16)
     for load in loads[blocks:]:
         load.wait()
 
 
-def height_project_kernel(x_ref, gain_ref, w_ref, q_ref, kv_ref):
+def second_kernel(first_ref, x_ref, gain_ref, w_ref, q0_ref, q_ref, kv_ref):
     blocks, rows, colb, feat = x_ref.shape
-    inner = q_ref.shape[1]
     stream = x_ref[...].astype(jnp.float32).reshape(blocks * rows * colb, feat)
-    project(normalise(stream, gain_ref[0:1, :]), w_ref, q_ref, kv_ref, inner)
-
-
-def height_kernel(hi_ref, x_ref, q_ref, kv_ref, other_ref, w_ref, *refs):
-    full_ref, mix_ref, w_buf, w_sem = refs[-4:]
-    piece_refs = refs[:-4]
-    blocks, rows, colb, feat = x_ref.shape
+    normed = normalise(stream, gain_ref[0:1, :])
+    project_keys(normed, w_ref, kv_ref)
+    project_queries(first_ref[...], w_ref, q0_ref)
+    project_queries(normed, w_ref, q_ref)
+
+
+def height_kernel(ks, hi_ref, x_ref, q_ref, kv_ref, other_ref, w_ref, *refs):
+    mix_ref, w_buf, w_sem = refs[-3:]
+    _, rows, colb, feat = x_ref.shape
     per = rows * colb
     fetch = pltpu.make_async_copy(w_ref.at[0], w_buf, w_sem)
     fetch.start()
-
-    def put(span, lo, out):
-        at, size = span[0]
-        mix_ref[at : at + size, lo : lo + out.shape[1]] = out
-
-    attend(q_ref, kv_ref, other_ref, [[(b * per, per)] for b in range(blocks)], colb, put)
+    inner = q_ref.shape[1]
+    width = QUAD * HEAD
+    bias = group_bias(2 * per, colb)
+    places = [jnp.bitwise_xor(hi_ref[0], k) for k in ks]
+    for i, place in enumerate(places):
+        span = pl.ds(pl.multiple_of(place * per, per), per)
+        for lo in range(0, inner, width):
+            here, there = slice(lo, lo + width), slice(inner + lo, inner + lo + width)
+            key = jnp.concatenate([kv_ref[span, here], other_ref[span, here]], axis=0)
+            value = jnp.concatenate([kv_ref[span, there], other_ref[span, there]], axis=0)
+            mix_ref[i * per : (i + 1) * per, here] = attend_quad(
+                q_ref[span, here], key, value, bias
+            )
     fetch.wait()
-    for b in range(blocks):
-        stream = x_ref[b].astype(jnp.float32).reshape(per, feat)
-        update = jnp.dot(
-            mix_ref[b * per : (b + 1) * per, :], w_buf[...], preferred_element_type=jnp.float32
-        )
-        full_ref[b * per : (b + 1) * per, :] = (stream + update).astype(jnp.bfloat16)
-    each = piece_refs[0].shape[0]
-    for k, piece_ref in enumerate(piece_refs):
-        start = pl.multiple_of(jnp.bitwise_xor(hi_ref[0], k) * each, each)
-        piece_ref[...] = full_ref[pl.ds(start, each), :]
+    update = jnp.dot(mix_ref[...], w_buf[...], preferred_element_type=jnp.float32)
+    for i, place in enumerate(places):
+        stream = x_ref[place].astype(jnp.float32).reshape(per, feat)
+        refs[i][...] = (stream + update[i * per : (i + 1) * per]).astype(jnp.bfloat16)
 
 
 def time_project_kernel(*refs):
     gain_ref, w_ref, q_ref, kv_ref = refs[-4:]
-    inner = q_ref.shape[1]
     normed = jnp.concatenate(
         [normalise(ref[...].astype(jnp.float32), gain_ref[1:2, :]) for ref in refs[:-4]], axis=0
     )
-    project(normed, w_ref, q_ref, kv_ref, inner)
+    project_keys(normed, w_ref, kv_ref)
+    project_queries(normed, w_ref, q_ref)
 
 
 def gate_kernel(in_ref, out_ref):
@@ -180,22 +191,25 @@
     attend(q_ref, kv_ref, other_ref, spans, POSB, put)
 
 
-def finish_kernel(frames, hi_ref, full_ref, w_ref, *refs):
-    out_ref, mix_ref = refs[-2:]
-    rows, cols, feat = out_ref.shape
-    per = rows * COLB
-    each = refs[0].shape[0]
-    for k in range(frames):
-        start = pl.multiple_of(jnp.bitwise_xor(hi_ref[0], k) * each, each)
-        mix_ref[pl.ds(start, each), :] = refs[k][...]
-    for b in range(cols // COLB):
-        update = jnp.dot(
-            mix_ref[b * per : (b + 1) * per, :], w_ref[...], preferred_element_type=jnp.float32
-        )
-        total = full_ref[b * per : (b + 1) * per, :].astype(jnp.float32) + update
-        out_ref[:, b * COLB : (b + 1) * COLB, :] = total.reshape(rows, COLB, feat).astype(
-            jnp.bfloat16
-        )
+def finish_kernel(c, high, hi_ref, w_ref, *refs):
+    pieces, mixes = refs[:high], refs[high : 2 * high]
+    out_ref, buf, sem = refs[-3:]
+    _, rows, colb, feat = buf.shape
+    per = rows * colb
+    mixed = jnp.concatenate([ref[...] for ref in mixes], axis=0)
+    update = jnp.dot(mixed, w_ref[...], preferred_element_type=jnp.float32)
+    copies = []
+    for k in range(high):
+        total = pieces[k][...].astype(jnp.float32) + update[k * per : (k + 1) * per]
+        buf[k] = total.reshape(rows, colb, feat).astype(jnp.bfloat16)
+        place = c * high + jnp.bitwise_xor(hi_ref[0], k)
+        column = pl.multiple_of(place * colb, colb)
+        copies.append(
+            pltpu.make_async_copy(buf.at[k], out_ref.at[:, pl.ds(column, colb), :], sem.at[k])
+        )
+        copies[-1].start()
+    for copy in copies:
+        copy.wait()
 
 
 SMEM = pl.BlockSpec(memory_space=pltpu.SMEM)
@@ -251,17 +265,17 @@
         return lax.optimization_barrier((values, earlier))[0]
 
     held = (blocks, rows, COLB, feat)
-    loaded = [(feat, 3 * inner), gains.shape] + [held] * CHUNKS
-    types = [bf, gains.dtype] + [bf] * CHUNKS
-
-    def load_project(x):
-        return call(
-            functools.partial(load_project_kernel, CHUNKS),
-            3 * work,
+
+    def load(x):
+        shapes = [(count, 2 * inner), (count, feat), (feat, 3 * inner), gains.shape]
+        shapes += [held] * CHUNKS
+        kinds = [bf, bf, bf, gains.dtype] + [bf] * CHUNKS
+        return call(
+            load_kernel,
+            2 * work,
             in_specs=[HBM, HBM, HBM],
-            out_specs=qkv_out["out_specs"] + [whole(*shape) for shape in loaded],
-            out_shape=qkv_out["out_shape"]
-            + [jax.ShapeDtypeStruct(shape, kind) for shape, kind in zip(loaded, types)],
+            out_specs=[whole(*shape) for shape in shapes],
+            out_shape=[jax.ShapeDtypeStruct(*pair) for pair in zip(shapes, kinds)],
             scratch_shapes=[
                 pltpu.SemaphoreType.DMA((blocks * CHUNKS,)),
                 pltpu.SemaphoreType.DMA((SPLIT,)),
@@ -269,29 +283,33 @@
             ],
         )(x, gains_far, qkv_far)
 
-    def height_project(x, gain, weight):
-        return call(
-            height_project_kernel,
-            3 * work,
-            in_specs=[whole(*held), whole(*gains.shape), whole(feat, 3 * inner)],
-            **qkv_out,
-        )(x, gain, weight)
-
-    def height(x, q, kv, other):
-        outs = call(
-            height_kernel,
+    def second(first, x, gain, weight):
+        return call(
+            second_kernel,
             4 * work,
+            in_specs=[
+                whole(count, feat),
+                whole(*held),
+                whole(*gains.shape),
+                whole(feat, 3 * inner),
+            ],
+            out_specs=[whole(count, inner)] + qkv_out["out_specs"],
+            out_shape=[jax.ShapeDtypeStruct((count, inner), bf)] + qkv_out["out_shape"],
+        )(first, x, gain, weight)
+
+    def height(ks, x, q, kv, other):
+        return call(
+            functools.partial(height_kernel, ks),
+            2 * work,
             in_specs=[SMEM, whole(*held)] + qkv_in + [HBM],
-            out_specs=[whole(each, feat)] * high + [whole(count, feat)],
-            out_shape=[jax.ShapeDtypeStruct((each, feat), bf)] * high
-            + [jax.ShapeDtypeStruct((count, feat), bf)],
+            out_specs=[whole(each, feat)] * len(ks),
+            out_shape=[jax.ShapeDtypeStruct((each, feat), bf)] * len(ks),
             scratch_shapes=[
-                pltpu.VMEM((count, inner), bf),
+                pltpu.VMEM((len(ks) * each, inner), bf),
                 pltpu.VMEM((inner, feat), bf),
                 pltpu.SemaphoreType.DMA,
             ],
         )(hi, x, q, kv, other, out_far)
-        return outs[:-1], outs[-1]
 
     def gate(value):
         return pl.pallas_call(
@@ -322,22 +340,22 @@
             out_shape=[jax.ShapeDtypeStruct((each, inner), bf)] * high,
         )(q, kv, other)
 
-    def finish(c, hi, full, mixes, prior):
-        aliases, extra_specs, extra = {}, [], []
+    def finish(c, hi, pieces, mixes, prior):
+        extra_specs, extra = [], []
         if prior is not None:
-            aliases = {high + 3: 0}
             extra_specs, extra = [pl.BlockSpec(memory_space=pl.ANY)], [prior]
         return call(
-            functools.partial(finish_kernel, high),
+            functools.partial(finish_kernel, c, high),
             work,
-            in_specs=[SMEM, whole(count, feat), pick(1, (inner, feat))]
+            in_specs=[SMEM, pick(1, (inner, feat))]
+            + [whole(each, feat)] * high
             + [whole(each, inner)] * high
             + extra_specs,
-            out_specs=pl.BlockSpec((rows, wide, feat), lambda _: (0, c, 0)),
+            out_specs=HBM,
             out_shape=jax.ShapeDtypeStruct((rows, cols, feat), bf),
-            scratch_shapes=[pltpu.VMEM((count, inner), bf)],
-            input_output_aliases=aliases,
-        )(hi, full, out_weights, *mixes, *extra)
+            scratch_shapes=[pltpu.VMEM(held, bf), pltpu.SemaphoreType.DMA((high,))],
+            input_output_aliases={2 * high + 2: 0} if extra else {},
+        )(hi, out_weights, *pieces, *mixes, *extra)
 
     def swap(a):
         return lax.ppermute(a, "space", [(0, 1), (1, 0)])
@@ -356,27 +374,35 @@
         return lax.ppermute(piece, ("tm", "space"), route(k))
 
     order = list(range(high - 1, -1, -1))
+    heavy, light = order[:half], order[half:]
 
     def exchange(pieces, ks):
         return {k: permute(pieces[k], k) for k in ks}
 
-    q, kv, weight, gain, *xs = load_project(after(x, hi))
-    projected, others, heights, arrived, home = [(q, kv)], [], [], [], []
-    others.append(swap(kv))
-    for c in range(1, CHUNKS):
-        projected.append(height_project(after(xs[c], projected[-1][0]), gain, weight))
-        others.append(swap(projected[c][1]))
-    last = projected[-1][0]
+    kv, first, weight, gain, *xs = load(after(x, hi))
+    others = [swap(kv)]
+    q0, q1, kv1 = second(first, xs[1], gain, weight)
+    others.append(swap(kv1))
+    queries, keys = [q0, q1], [kv, kv1]
+    pieces, arrived, home = [], [], []
+    last = q1
     for c in range(CHUNKS):
-        q, kv = projected[c]
-        heights.append(height(xs[c], after(q, last), kv, others[c]))
-        last = heights[-1][1]
-        arrived.append(exchange(heights[-1][0], order))
-    heavy, light = order[: high // 2], order[high // 2 :]
+        made, got = {}, {}
+        for name, ks in (("far", heavy), ("near", light)):
+            q = after(queries[c], last)
+            outs = height(ks, xs[c], q, keys[c], others[c])
+            last = outs[0]
+            made.update(zip(ks, outs))
+            ready = dict(made)
+            if c and name == "far":
+                ready[heavy[-1]] = after(made[heavy[-1]], arrived[-1][heavy[-1]])
+            got.update(exchange(ready, ks))
+        pieces.append(made)
+        arrived.append(got)
     mixes = None
     for c in range(CHUNKS):
-        pieces = [arrived[c][k] for k in range(high)]
-        q, kv = time_project(after(pieces, last))
+        got = [arrived[c][k] for k in range(high)]
+        q, kv = time_project(after(got, last))
         other = swap(kv)
         if mixes is not None:
             mixes = after(mixes, q)
@@ -390,8 +416,9 @@
     home[-1].update(exchange(mixes, heavy))
     out = None
     for c in range(CHUNKS):
+        made = after([pieces[c][k] for k in range(high)], last)
         mixes = [home[c][k] for k in range(high)]
-        out = finish(c, hi, after(heights[c][1], last), mixes, out)
+        out = finish(c, hi, made, mixes, out)
     return out[None]
 
 
@@ -444,7 +471,7 @@
             and frames == 2 * high
             and high > 1
             and high & (high - 1) == 0
-            and cols % (CHUNKS * COLB) == 0
+            and cols == CHUNKS * COLB * high
             and count % (high * POSB) == 0
             and inner % (QUAD * HEAD) == 0
             and feat % 128 == 0

time: 84.9 us -> 83.4 us (0.982)
  starting transfers between devices: 37.1 us -> 35.2 us
  waiting for transfers between devices: 23.6 us -> 24.7 us
  Pallas kernels: 23.7 us -> 22.8 us
    ppermute x16, starting transfers between devices: 36.3 us -> 33.2 us  [permute(): return lax.ppermute(piece, ('tm', 'space'), route(k))]
    ppermute x16, waiting for transfers between devices: 23.5 us -> 24.7 us  [permute(): return lax.ppermute(piece, ('tm', 'space'), route(k))]
    ppermute x4, starting transfers between devices: 0.77 us -> 2 us  [swap(): return lax.ppermute(a, 'space', [(0, 1), (1, 0)])]
    pallas_call x6 -> x8, Pallas kernels: 17.3 us -> 16.3 us  [the longest x4 6.7 us: height(): call(functools.partial(height_kernel, ks), 2 * work, in_specs=[SMEM, whol...]
  transfers between devices with their start and end apart: 20 -> 20, of which waited for: 6 -> 7; matrix products, arithmetic and copies ran while one was open for 0% -> 0% of each run, Pallas kernels for 17% -> 17%
where the time goes in v2:
time: 83.4 us; the launch traced here: 83.1 us
  starting transfers between devices  35.2 us (42%)
  waiting for transfers between devices  24.7 us (30%)
  Pallas kernels  22.8 us (27%)
    ppermute x16, starting transfers between devices, permute(): return lax.ppermute(piece, ('tm', 'space'), route(k))  33.2 us
    ppermute x16, waiting for transfers between devices, permute(): return lax.ppermute(piece, ('tm', 'space'), route(k))  24.7 us
    pallas_call x4, Pallas kernels, height(): call(functools.partial(height_kernel, ks), 2 * work, in_specs=[SMEM, whol...  6.7 us
    pallas_call x2, Pallas kernels, finish(): call(functools.partial(finish_kernel, c, high), work, in_specs=[SMEM, pic...  3.95 us
    pallas_call x1, Pallas kernels, load(): call(load_kernel, 2 * work, in_specs=[HBM, HBM, HBM], out_specs=[whole(*s...  3.73 us
    pallas_call x2, Pallas kernels, time_project(): call(time_project_kernel, 3 * work, in_specs=[whole(each, feat)] * high +...  3.09 us
    pallas_call x2, Pallas kernels, timed(): call(time_kernel, 2 * work, in_specs=qkv_in, out_specs=[whole(each, inner...  2.82 us
    ppermute x4, starting transfers between devices, swap(): return lax.ppermute(a, 'space', [(0, 1), (1, 0)])  2 us
  transfers between devices with their start and end apart: 20, of which 7 were waited for; matrix products, arithmetic and copies ran while one was open for 0% of the time, Pallas kernels for 17%

profile of v2, /device:TPU:1, one launch (start us, length us, event | category | flops | bytes accessed | tf_op | source)
XLA Modules:
  0.0 83.1 jit_solution(2923732745268937193)
XLA Ops:
  0.0 3.7 %shard_map.46 = (bf16[384,1024]{1,0:T(8,128)(2,1)S(1)}, bf16[384,1024]{1,0:T(8,128)(2,1)S(1)}, bf16[1024,1536]{1,0:T(8,128)(2,1)S(1)}, f32[2,1024]{1,0:T(2,128)S...) custom-call(bf16[12,64,1024]{2,1,0:T(8,128)(2,1)} %bitcast.5, f32[2,1024]{1,0:T(2,128)} %refs_4_.3, ...), custom_call_target="tpu_custom_call" | custom-call | flops 805306368 | bytes 1572864 | tf_op jit(solution)/shard_map/pallas_call | solution.py:273
  3.8 2.0 %shard_map.47 = (bf16[384,512]{1,0:T(8,128)(2,1)S(1)}, bf16[384,512]{1,0:T(8,128)(2,1)S(1)}, bf16[384,1024]{1,0:T(8,128)(2,1)S(1)}) custom-call(bf16[384,1024]{1,0:T(8,128)(2,1)S(1)} %get-tuple-element.61.first_ref, bf16[4,12,8,1024]{3,2,1,0:T(8,128)(2,1)S(1)} %get-tuple-element.62.x_ref, f32[2,1024]{1,0:T(2,128)S(1)} %get-tuple-element.63.gain_ref, ...), custom_call_target="tpu_custom_call" | custom-call | flops 1610612736 | bytes 1572864 | tf_op jit(solution)/shard_map/pallas_call | solution.py:287
  6.3 1.6 %shard_map.48 = (bf16[96,1024]{1,0:T(8,128)(2,1)S(1)}, bf16[96,1024]{1,0:T(8,128)(2,1)S(1)}) custom-call(s32[1]{0:T(128)} %bitcast.hi_ref.in_ref, bf16[4,12,8,1024]{3,2,1,0:T(8,128)(2,1)S(1)} %get-tuple-element.60.x_ref, bf16[384,512]{1,0:T(8,128)(2,1)S(1)} %get-tuple-element.70.q_ref, bf16[384,1024]{1,0:T(8,128)(2,1)S(1)} %get-tuple-element.68.kv_ref, ...), custom_call_target="tpu_custom_call" | custom-call | flops 805306368 | bytes 1572864 | tf_op jit(solution)/shard_map/pallas_call | solution.py:301
  8.0 1.8 %shard_map.49 = (bf16[96,1024]{1,0:T(8,128)(2,1)S(1)}, bf16[96,1024]{1,0:T(8,128)(2,1)S(1)}) custom-call(s32[1]{0:T(128)} %bitcast.hi_ref.in_ref, bf16[4,12,8,1024]{3,2,1,0:T(8,128)(2,1)S(1)} %get-tuple-element.60.x_ref, bf16[384,512]{1,0:T(8,128)(2,1)S(1)} %get-tuple-element.70.q_ref, bf16[384,1024]{1,0:T(8,128)(2,1)S(1)} %get-tuple-element.68.kv_ref, ...), custom_call_target="tpu_custom_call" | custom-call | flops 805306368 | bytes 1572864 | tf_op jit(solution)/shard_map/pallas_call | solution.py:301
  9.8 4.5 %collective-permute-start.1 = (bf16[96,1024]{1,0:T(8,128)(2,1)S(1)}, bf16[96,1024]{1,0:T(8,128)(2,1)S(1)}, u32[]{:S(2)}, u32[]{:S(2)}) collective-permute-start(bf16[96,1024]{1,0:T(8,128)(2,1)S(1)} %get-tuple-element.104.refs_0_), channel_id=1, source_target_pairs={{0,0},{1,2},{2,1},{3,3},{4,4},{5,6},{6,5},{7,7},{8,11},{9,9},{10,1... | collective-permute-start | bytes 589832 | tf_op jit(solution)/shard_map/ppermute | solution.py:374
  15.5 2.7 %collective-permute-start.3 = (bf16[96,1024]{1,0:T(8,128)(2,1)S(1)}, bf16[96,1024]{1,0:T(8,128)(2,1)S(1)}, u32[]{:S(2)}, u32[]{:S(2)}) collective-permute-start(bf16[96,1024]{1,0:T(8,128)(2,1)S(1)} %get-tuple-element.106.refs_2_), channel_id=1, source_target_pairs={{0,10},{1,8},{2,11},{3,9},{4,14},{5,12},{6,15},{7,13},{8,1},{9,3},... | collective-permute-start | bytes 589832 | tf_op jit(solution)/shard_map/ppermute | solution.py:374
  18.2 1.6 %shard_map.50 = (bf16[96,1024]{1,0:T(8,128)(2,1)S(1)}, bf16[96,1024]{1,0:T(8,128)(2,1)S(1)}) custom-call(s32[1]{0:T(128)} %bitcast.hi_ref.in_ref, bf16[4,12,8,1024]{3,2,1,0:T(8,128)(2,1)S(1)} %get-tuple-element.62.x_ref, bf16[384,512]{1,0:T(8,128)(2,1)S(1)} %get-tuple-element.77.q_ref, bf16[384,1024]{1,0:T(8,128)(2,1)S(1)} %get-tuple-element.75.kv_ref, ...), custom_call_target="tpu_custom_call" | custom-call | flops 805306368 | bytes 1572864 | tf_op jit(solution)/shard_map/pallas_call | solution.py:301
  19.9 1.6 %shard_map.51 = (bf16[96,1024]{1,0:T(8,128)(2,1)S(1)}, bf16[96,1024]{1,0:T(8,128)(2,1)S(1)}) custom-call(s32[1]{0:T(128)} %bitcast.hi_ref.in_ref, bf16[4,12,8,1024]{3,2,1,0:T(8,128)(2,1)S(1)} %get-tuple-element.62.x_ref, bf16[384,512]{1,0:T(8,128)(2,1)S(1)} %get-tuple-element.77.q_ref, bf16[384,1024]{1,0:T(8,128)(2,1)S(1)} %get-tuple-element.75.kv_ref, ...), custom_call_target="tpu_custom_call" | custom-call | flops 805306368 | bytes 1572864 | tf_op jit(solution)/shard_map/pallas_call | solution.py:301
  21.5 1.7 %collective-permute-done.2.refs_1_ = bf16[96,1024]{1,0:T(8,128)(2,1)S(1)} collective-permute-done((bf16[96,1024]{1,0:T(8,128)(2,1)S(1)}, bf16[96,1024]{1,0:T(8,128)(2,1)S(1)}, u32[]{:S(2)}, u32[]{:S(2)}) %collective-permute-start.2) | collective-permute-done | bytes 196640 | tf_op jit(solution)/shard_map/ppermute | solution.py:374
  23.3 7.6 %collective-permute-done.3.refs_2_ = bf16[96,1024]{1,0:T(8,128)(2,1)S(1)} collective-permute-done((bf16[96,1024]{1,0:T(8,128)(2,1)S(1)}, bf16[96,1024]{1,0:T(8,128)(2,1)S(1)}, u32[]{:S(2)}, u32[]{:S(2)}) %collective-permute-start.3) | collective-permute-done | bytes 196640 | tf_op jit(solution)/shard_map/ppermute | solution.py:374
  32.6 5.2 %collective-permute-start.8 = (bf16[96,1024]{1,0:T(8,128)(2,1)S(1)}, bf16[96,1024]{1,0:T(8,128)(2,1)S(1)}, u32[]{:S(2)}, u32[]{:S(2)}) collective-permute-start(bf16[96,1024]{1,0:T(8,128)(2,1)S(1)} %get-tuple-element.98.refs_1_), channel_id=1, source_target_pairs={{0,4},{1,6},{2,5},{3,7},{4,0},{5,2},{6,1},{7,3},{8,15},{9,13},{10,... | collective-permute-start | bytes 589832 | tf_op jit(solution)/shard_map/ppermute | solution.py:374
  37.8 2.5 %collective-permute-start.10 = (bf16[96,1024]{1,0:T(8,128)(2,1)S(1)}, bf16[96,1024]{1,0:T(8,128)(2,1)S(1)}, u32[]{:S(2)}, u32[]{:S(2)}) collective-permute-start(bf16[96,1024]{1,0:T(8,128)(2,1)S(1)} %get-tuple-element.100.refs_3_), channel_id=1, source_target_pairs={{0,14},{1,12},{2,15},{3,13},{4,10},{5,8},{6,11},{7,9},{8,5},{9,7},... | collective-permute-start | bytes 589832 | tf_op jit(solution)/shard_map/ppermute | solution.py:374
  40.2 3.1 %collective-permute-start.7 = (bf16[96,1024]{1,0:T(8,128)(2,1)S(1)}, bf16[96,1024]{1,0:T(8,128)(2,1)S(1)}, u32[]{:S(2)}, u32[]{:S(2)}) collective-permute-start(bf16[96,1024]{1,0:T(8,128)(2,1)S(1)} %get-tuple-element.97.refs_0_), channel_id=1, source_target_pairs={{0,0},{1,2},{2,1},{3,3},{4,4},{5,6},{6,5},{7,7},{8,11},{9,9},{10,1... | collective-permute-start | bytes 589832 | tf_op jit(solution)/shard_map/ppermute | solution.py:374
  45.3 4.2 %collective-permute-done.7.refs_0_ = bf16[96,1024]{1,0:T(8,128)(2,1)S(1)} collective-permute-done((bf16[96,1024]{1,0:T(8,128)(2,1)S(1)}, bf16[96,1024]{1,0:T(8,128)(2,1)S(1)}, u32[]{:S(2)}, u32[]{:S(2)}) %collective-permute-start.7) | collective-permute-done | bytes 196640 | tf_op jit(solution)/shard_map/ppermute | solution.py:374
  50.3 7.4 %collective-permute-done.9.refs_2_ = bf16[96,1024]{1,0:T(8,128)(2,1)S(1)} collective-permute-done((bf16[96,1024]{1,0:T(8,128)(2,1)S(1)}, bf16[96,1024]{1,0:T(8,128)(2,1)S(1)}, u32[]{:S(2)}, u32[]{:S(2)}) %collective-permute-start.9) | collective-permute-done | bytes 196640 | tf_op jit(solution)/shard_map/ppermute | solution.py:374
  60.5 2.5 %collective-permute-start.16 = (bf16[96,512]{1,0:T(8,128)(2,1)S(1)}, bf16[96,512]{1,0:T(8,128)(2,1)S(1)}, u32[]{:S(2)}, u32[]{:S(2)}) collective-permute-start(bf16[96,512]{1,0:T(8,128)(2,1)S(1)} %get-tuple-element.85), channel_id=1, source_target_pairs={{0,0},{1,2},{2,1},{3,3},{4,4},{5,6},{6,5},{7,7},{8,11},{9,9},{10,1... | collective-permute-start | bytes 294920 | tf_op jit(solution)/shard_map/ppermute | solution.py:374
  63.1 2.3 %collective-permute-start.18 = (bf16[96,512]{1,0:T(8,128)(2,1)S(1)}, bf16[96,512]{1,0:T(8,128)(2,1)S(1)}, u32[]{:S(2)}, u32[]{:S(2)}) collective-permute-start(bf16[96,512]{1,0:T(8,128)(2,1)S(1)} %get-tuple-element.111), channel_id=1, source_target_pairs={{0,10},{1,8},{2,11},{3,9},{4,14},{5,12},{6,15},{7,13},{8,1},{9,3},... | collective-permute-start | bytes 294920 | tf_op jit(solution)/shard_map/ppermute | solution.py:374
  65.4 2.5 %collective-permute-start.19 = (bf16[96,512]{1,0:T(8,128)(2,1)S(1)}, bf16[96,512]{1,0:T(8,128)(2,1)S(1)}, u32[]{:S(2)}, u32[]{:S(2)}) collective-permute-start(bf16[96,512]{1,0:T(8,128)(2,1)S(1)} %get-tuple-element.112), channel_id=1, source_target_pairs={{0,14},{1,12},{2,15},{3,13},{4,10},{5,8},{6,11},{7,9},{8,5},{9,7},... | collective-permute-start | bytes 294920 | tf_op jit(solution)/shard_map/ppermute | solution.py:374
  69.5 2.2 %collective-permute-start.14 = (bf16[96,512]{1,0:T(8,128)(2,1)S(1)}, bf16[96,512]{1,0:T(8,128)(2,1)S(1)}, u32[]{:S(2)}, u32[]{:S(2)}) collective-permute-start(bf16[96,512]{1,0:T(8,128)(2,1)S(1)} %get-tuple-element.102), channel_id=1, source_target_pairs={{0,10},{1,8},{2,11},{3,9},{4,14},{5,12},{6,15},{7,13},{8,1},{9,3},... | collective-permute-start | bytes 294920 | tf_op jit(solution)/shard_map/ppermute | solution.py:374
  71.7 1.7 %collective-permute-start.15 = (bf16[96,512]{1,0:T(8,128)(2,1)S(1)}, bf16[96,512]{1,0:T(8,128)(2,1)S(1)}, u32[]{:S(2)}, u32[]{:S(2)}) collective-permute-start(bf16[96,512]{1,0:T(8,128)(2,1)S(1)} %get-tuple-element.103), channel_id=1, source_target_pairs={{0,14},{1,12},{2,15},{3,13},{4,10},{5,8},{6,11},{7,9},{8,5},{9,7},... | collective-permute-start | bytes 294920 | tf_op jit(solution)/shard_map/ppermute | solution.py:374
  74.2 2.5 %collective-permute-start.12 = (bf16[96,512]{1,0:T(8,128)(2,1)S(1)}, bf16[96,512]{1,0:T(8,128)(2,1)S(1)}, u32[]{:S(2)}, u32[]{:S(2)}) collective-permute-start(bf16[96,512]{1,0:T(8,128)(2,1)S(1)} %get-tuple-element.96), channel_id=1, source_target_pairs={{0,0},{1,2},{2,1},{3,3},{4,4},{5,6},{6,5},{7,7},{8,11},{9,9},{10,1... | collective-permute-start | bytes 294920 | tf_op jit(solution)/shard_map/ppermute | solution.py:374
  76.7 2.0 %shard_map.56.refs_8_ = bf16[12,64,1024]{2,1,0:T(8,128)(2,1)} custom-call(s32[1]{0:T(128)} %gate.1.hi_ref, bf16[2,512,1024]{2,1,0:T(8,128)(2,1)S(1)} %copy-done, bf16[96,1024]{1,0:T(8,128)(2,1)S(1)} %get-tuple-element.104.refs_0_, bf16[96,1024]{1,0:T(8,128)(2,1)S(1)} %get-tuple-element.105.refs_1_, bf16[96,1024]{1,0:T(8,128)(2,1)S(1)} %get-tuple-element.106.refs_2_, ...), custom_call_target="tpu_custom_call" | custom-call | flops 402653184 | bytes 1572864 | tf_op jit(solution)/shard_map/pallas_call | solution.py:347
  78.7 2.3 %collective-permute-done.14.refs_6_ = bf16[96,512]{1,0:T(8,128)(2,1)S(1)} collective-permute-done((bf16[96,512]{1,0:T(8,128)(2,1)S(1)}, bf16[96,512]{1,0:T(8,128)(2,1)S(1)}, u32[]{:S(2)}, u32[]{:S(2)}) %collective-permute-start.14) | collective-permute-done | bytes 98336 | tf_op jit(solution)/shard_map/ppermute | solution.py:374
  81.0 2.0 %shard_map.57 = bf16[12,64,1024]{2,1,0:T(8,128)(2,1)} custom-call(s32[1]{0:T(128)} %gate.1.hi_ref, bf16[2,512,1024]{2,1,0:T(8,128)(2,1)S(1)} %copy-done, bf16[96,1024]{1,0:T(8,128)(2,1)S(1)} %get-tuple-element.97.refs_0_, bf16[96,1024]{1,0:T(8,128)(2,1)S(1)} %get-tuple-element.98.refs_1_, ...), custom_call_target="tpu_custom_call", output_to_operand_aliasing={{}: (10, {})} | custom-call | flops 402653184 | bytes 1572864 | tf_op jit(solution)/shard_map/pallas_call | solution.py:347
  (38 shorter events, 11.4 us)
Async XLA Ops:
  3.7 2.6 %collective-permute-start = (bf16[384,1024]{1,0:T(8,128)(2,1)S(1)}, bf16[384,1024]{1,0:T(8,128)(2,1)S(1)}, u32[]{:S(2)}, u32[]{:S(2)}) collective-permute-start(bf16[384,1024]{1,0:T(8,128)(2,1)S(1)} %get-tuple-element.68.kv_ref), channel_id=1, source_target_pairs={{0,1},{1,0},{2,3},{3,2},{4,5},{5,4},{6,7},{7,6},{8,9},{9,8},{10,11... | collective-permute-start | bytes 2359304 | tf_op jit(solution)/shard_map/ppermute | solution.py:361
  5.8 12.5 %collective-permute-start.5 = (bf16[384,1024]{1,0:T(8,128)(2,1)S(1)}, bf16[384,1024]{1,0:T(8,128)(2,1)S(1)}, u32[]{:S(2)}, u32[]{:S(2)}) collective-permute-start(bf16[384,1024]{1,0:T(8,128)(2,1)S(1)} %get-tuple-element.75.kv_ref), channel_id=1, source_target_pairs={{0,1},{1,0},{2,3},{3,2},{4,5},{5,4},{6,7},{7,6},{8,9},{9,8},{10,11... | collective-permute-start | bytes 2359304 | tf_op jit(solution)/shard_map/ppermute | solution.py:361
  8.0 22.9 %slice-start = ((s8[6291456]{0:T(1024)(128)(4,1)}), s8[4194304]{0:T(1024)(128)(4,1)S(1)}, s32[]{:S(2)}) async-start(s8[6291456]{0:T(1024)(128)(4,1)} %bitcast.3), calls=%async_computation | async-start | bytes 8388608
  9.8 11.7 %collective-permute-start.1 = (bf16[96,1024]{1,0:T(8,128)(2,1)S(1)}, bf16[96,1024]{1,0:T(8,128)(2,1)S(1)}, u32[]{:S(2)}, u32[]{:S(2)}) collective-permute-start(bf16[96,1024]{1,0:T(8,128)(2,1)S(1)} %get-tuple-element.104.refs_0_), channel_id=1, source_target_pairs={{0,0},{1,2},{2,1},{3,3},{4,4},{5,6},{6,5},{7,7},{8,11},{9,9},{10,1... | collective-permute-start | bytes 589832 | tf_op jit(solution)/shard_map/ppermute | solution.py:374
  14.3 9.0 %collective-permute-start.2 = (bf16[96,1024]{1,0:T(8,128)(2,1)S(1)}, bf16[96,1024]{1,0:T(8,128)(2,1)S(1)}, u32[]{:S(2)}, u32[]{:S(2)}) collective-permute-start(bf16[96,1024]{1,0:T(8,128)(2,1)S(1)} %get-tuple-element.105.refs_1_), channel_id=1, source_target_pairs={{0,4},{1,6},{2,5},{3,7},{4,0},{5,2},{6,1},{7,3},{8,15},{9,13},{10,... | collective-permute-start | bytes 589832 | tf_op jit(solution)/shard_map/ppermute | solution.py:374
  15.5 15.4 %slice-start.1 = ((s8[6291456]{0:T(1024)(128)(4,1)}), s8[2097152]{0:T(1024)(128)(4,1)S(1)}, s32[]{:S(2)}) async-start(s8[6291456]{0:T(1024)(128)(4,1)} %bitcast.3), calls=%async_computation.1 | async-start | bytes 4194304
  15.5 15.4 %collective-permute-start.3 = (bf16[96,1024]{1,0:T(8,128)(2,1)S(1)}, bf16[96,1024]{1,0:T(8,128)(2,1)S(1)}, u32[]{:S(2)}, u32[]{:S(2)}) collective-permute-start(bf16[96,1024]{1,0:T(8,128)(2,1)S(1)} %get-tuple-element.106.refs_2_), channel_id=1, source_target_pairs={{0,10},{1,8},{2,11},{3,9},{4,14},{5,12},{6,15},{7,13},{8,1},{9,3},... | collective-permute-start | bytes 589832 | tf_op jit(solution)/shard_map/ppermute | solution.py:374
  18.2 12.7 %collective-permute-start.4 = (bf16[96,1024]{1,0:T(8,128)(2,1)S(1)}, bf16[96,1024]{1,0:T(8,128)(2,1)S(1)}, u32[]{:S(2)}, u32[]{:S(2)}) collective-permute-start(bf16[96,1024]{1,0:T(8,128)(2,1)S(1)} %get-tuple-element.107.refs_3_), channel_id=1, source_target_pairs={{0,14},{1,12},{2,15},{3,13},{4,10},{5,8},{6,11},{7,9},{8,5},{9,7},... | collective-permute-start | bytes 589832 | tf_op jit(solution)/shard_map/ppermute | solution.py:374
  19.9 11.1 %copy-start.1 = (f32[2,1024]{1,0:T(2,128)S(1)}, f32[2,1024]{1,0:T(2,128)}, u32[]{:S(2)}) copy-start(f32[2,1024]{1,0:T(2,128)} %refs_4_.3) | copy-start | bytes 24580
  32.5 10.9 %collective-permute-start.6 = (bf16[384,1024]{1,0:T(8,128)(2,1)S(1)}, bf16[384,1024]{1,0:T(8,128)(2,1)S(1)}, u32[]{:S(2)}, u32[]{:S(2)}) collective-permute-start(bf16[384,1024]{1,0:T(8,128)(2,1)S(1)} %get-tuple-element.84.kv_ref), channel_id=1, source_target_pairs={{0,1},{1,0},{2,3},{3,2},{4,5},{5,4},{6,7},{7,6},{8,9},{9,8},{10,11... | collective-permute-start | bytes 2359304 | tf_op jit(solution)/shard_map/ppermute | solution.py:361
  32.6 16.9 %collective-permute-start.8 = (bf16[96,1024]{1,0:T(8,128)(2,1)S(1)}, bf16[96,1024]{1,0:T(8,128)(2,1)S(1)}, u32[]{:S(2)}, u32[]{:S(2)}) collective-permute-start(bf16[96,1024]{1,0:T(8,128)(2,1)S(1)} %get-tuple-element.98.refs_1_), channel_id=1, source_target_pairs={{0,4},{1,6},{2,5},{3,7},{4,0},{5,2},{6,1},{7,3},{8,15},{9,13},{10,... | collective-permute-start | bytes 589832 | tf_op jit(solution)/shard_map/ppermute | solution.py:374
  37.8 12.5 %collective-permute-start.10 = (bf16[96,1024]{1,0:T(8,128)(2,1)S(1)}, bf16[96,1024]{1,0:T(8,128)(2,1)S(1)}, u32[]{:S(2)}, u32[]{:S(2)}) collective-permute-start(bf16[96,1024]{1,0:T(8,128)(2,1)S(1)} %get-tuple-element.100.refs_3_), channel_id=1, source_target_pairs={{0,14},{1,12},{2,15},{3,13},{4,10},{5,8},{6,11},{7,9},{8,5},{9,7},... | collective-permute-start | bytes 589832 | tf_op jit(solution)/shard_map/ppermute | solution.py:374
  40.2 9.2 %collective-permute-start.7 = (bf16[96,1024]{1,0:T(8,128)(2,1)S(1)}, bf16[96,1024]{1,0:T(8,128)(2,1)S(1)}, u32[]{:S(2)}, u32[]{:S(2)}) collective-permute-start(bf16[96,1024]{1,0:T(8,128)(2,1)S(1)} %get-tuple-element.97.refs_0_), channel_id=1, source_target_pairs={{0,0},{1,2},{2,1},{3,3},{4,4},{5,6},{6,5},{7,7},{8,11},{9,9},{10,1... | collective-permute-start | bytes 589832 | tf_op jit(solution)/shard_map/ppermute | solution.py:374
  43.3 14.4 %collective-permute-start.9 = (bf16[96,1024]{1,0:T(8,128)(2,1)S(1)}, bf16[96,1024]{1,0:T(8,128)(2,1)S(1)}, u32[]{:S(2)}, u32[]{:S(2)}) collective-permute-start(bf16[96,1024]{1,0:T(8,128)(2,1)S(1)} %get-tuple-element.99.refs_2_), channel_id=1, source_target_pairs={{0,10},{1,8},{2,11},{3,9},{4,14},{5,12},{6,15},{7,13},{8,1},{9,3},... | collective-permute-start | bytes 589832 | tf_op jit(solution)/shard_map/ppermute | solution.py:374
  59.2 17.5 %copy-start = (bf16[2,512,1024]{2,1,0:T(8,128)(2,1)S(1)}, bf16[2,512,1024]{2,1,0:T(8,128)(2,1)}, u32[]{:S(2)}) copy-start(bf16[2,512,1024]{2,1,0:T(8,128)(2,1)} %w_ref.13) | copy-start | bytes 6291460
  59.2 8.7 %collective-permute-start.11 = (bf16[384,1024]{1,0:T(8,128)(2,1)S(1)}, bf16[384,1024]{1,0:T(8,128)(2,1)S(1)}, u32[]{:S(2)}, u32[]{:S(2)}) collective-permute-start(bf16[384,1024]{1,0:T(8,128)(2,1)S(1)} %get-tuple-element.95.kv_ref), channel_id=1, source_target_pairs={{0,1},{1,0},{2,3},{3,2},{4,5},{5,4},{6,7},{7,6},{8,9},{9,8},{10,11... | collective-permute-start | bytes 2359304 | tf_op jit(solution)/shard_map/ppermute | solution.py:361
  60.5 11.2 %collective-permute-start.16 = (bf16[96,512]{1,0:T(8,128)(2,1)S(1)}, bf16[96,512]{1,0:T(8,128)(2,1)S(1)}, u32[]{:S(2)}, u32[]{:S(2)}) collective-permute-start(bf16[96,512]{1,0:T(8,128)(2,1)S(1)} %get-tuple-element.85), channel_id=1, source_target_pairs={{0,0},{1,2},{2,1},{3,3},{4,4},{5,6},{6,5},{7,7},{8,11},{9,9},{10,1... | collective-permute-start | bytes 294920 | tf_op jit(solution)/shard_map/ppermute | solution.py:374
  63.0 6.4 %collective-permute-start.17 = (bf16[96,512]{1,0:T(8,128)(2,1)S(1)}, bf16[96,512]{1,0:T(8,128)(2,1)S(1)}, u32[]{:S(2)}, u32[]{:S(2)}) collective-permute-start(bf16[96,512]{1,0:T(8,128)(2,1)S(1)} %get-tuple-element.108), channel_id=1, source_target_pairs={{0,4},{1,6},{2,5},{3,7},{4,0},{5,2},{6,1},{7,3},{8,15},{9,13},{10,... | collective-permute-start | bytes 294920 | tf_op jit(solution)/shard_map/ppermute | solution.py:374
  63.1 11.0 %collective-permute-start.18 = (bf16[96,512]{1,0:T(8,128)(2,1)S(1)}, bf16[96,512]{1,0:T(8,128)(2,1)S(1)}, u32[]{:S(2)}, u32[]{:S(2)}) collective-permute-start(bf16[96,512]{1,0:T(8,128)(2,1)S(1)} %get-tuple-element.111), channel_id=1, source_target_pairs={{0,10},{1,8},{2,11},{3,9},{4,14},{5,12},{6,15},{7,13},{8,1},{9,3},... | collective-permute-start | bytes 294920 | tf_op jit(solution)/shard_map/ppermute | solution.py:374
  65.4 11.2 %collective-permute-start.19 = (bf16[96,512]{1,0:T(8,128)(2,1)S(1)}, bf16[96,512]{1,0:T(8,128)(2,1)S(1)}, u32[]{:S(2)}, u32[]{:S(2)}) collective-permute-start(bf16[96,512]{1,0:T(8,128)(2,1)S(1)} %get-tuple-element.112), channel_id=1, source_target_pairs={{0,14},{1,12},{2,15},{3,13},{4,10},{5,8},{6,11},{7,9},{8,5},{9,7},... | collective-permute-start | bytes 294920 | tf_op jit(solution)/shard_map/ppermute | solution.py:374
  69.4 9.3 %collective-permute-start.13 = (bf16[96,512]{1,0:T(8,128)(2,1)S(1)}, bf16[96,512]{1,0:T(8,128)(2,1)S(1)}, u32[]{:S(2)}, u32[]{:S(2)}) collective-permute-start(bf16[96,512]{1,0:T(8,128)(2,1)S(1)} %get-tuple-element.101), channel_id=1, source_target_pairs={{0,4},{1,6},{2,5},{3,7},{4,0},{5,2},{6,1},{7,3},{8,15},{9,13},{10,... | collective-permute-start | bytes 294920 | tf_op jit(solution)/shard_map/ppermute | solution.py:374
  69.5 11.5 %collective-permute-start.14 = (bf16[96,512]{1,0:T(8,128)(2,1)S(1)}, bf16[96,512]{1,0:T(8,128)(2,1)S(1)}, u32[]{:S(2)}, u32[]{:S(2)}) collective-permute-start(bf16[96,512]{1,0:T(8,128)(2,1)S(1)} %get-tuple-element.102), channel_id=1, source_target_pairs={{0,10},{1,8},{2,11},{3,9},{4,14},{5,12},{6,15},{7,13},{8,1},{9,3},... | collective-permute-start | bytes 294920 | tf_op jit(solution)/shard_map/ppermute | solution.py:374
  71.7 9.3 %collective-permute-start.15 = (bf16[96,512]{1,0:T(8,128)(2,1)S(1)}, bf16[96,512]{1,0:T(8,128)(2,1)S(1)}, u32[]{:S(2)}, u32[]{:S(2)}) collective-permute-start(bf16[96,512]{1,0:T(8,128)(2,1)S(1)} %get-tuple-element.103), channel_id=1, source_target_pairs={{0,14},{1,12},{2,15},{3,13},{4,10},{5,8},{6,11},{7,9},{8,5},{9,7},... | collective-permute-start | bytes 294920 | tf_op jit(solution)/shard_map/ppermute | solution.py:374
  74.2 6.8 %collective-permute-start.12 = (bf16[96,512]{1,0:T(8,128)(2,1)S(1)}, bf16[96,512]{1,0:T(8,128)(2,1)S(1)}, u32[]{:S(2)}, u32[]{:S(2)}) collective-permute-start(bf16[96,512]{1,0:T(8,128)(2,1)S(1)} %get-tuple-element.96), channel_id=1, source_target_pairs={{0,0},{1,2},{2,1},{3,3},{4,4},{5,6},{6,5},{7,7},{8,11},{9,9},{10,1... | collective-permute-start | bytes 294920 | tf_op jit(solution)/shard_map/ppermute | solution.py:374

commit v3 on v2

--- a/solution.py
+++ b/solution.py
@@ -191,21 +191,21 @@
     attend(q_ref, kv_ref, other_ref, spans, POSB, put)
 
 
-def finish_kernel(c, high, hi_ref, w_ref, *refs):
-    pieces, mixes = refs[:high], refs[high : 2 * high]
+def finish_kernel(c, ks, high, hi_ref, w_ref, *refs):
+    pieces, mixes = refs[: len(ks)], refs[len(ks) : 2 * len(ks)]
     out_ref, buf, sem = refs[-3:]
     _, rows, colb, feat = buf.shape
     per = rows * colb
     mixed = jnp.concatenate([ref[...] for ref in mixes], axis=0)
     update = jnp.dot(mixed, w_ref[...], preferred_element_type=jnp.float32)
     copies = []
-    for k in range(high):
-        total = pieces[k][...].astype(jnp.float32) + update[k * per : (k + 1) * per]
-        buf[k] = total.reshape(rows, colb, feat).astype(jnp.bfloat16)
+    for i, k in enumerate(ks):
+        total = pieces[i][...].astype(jnp.float32) + update[i * per : (i + 1) * per]
+        buf[i] = total.reshape(rows, colb, feat).astype(jnp.bfloat16)
         place = c * high + jnp.bitwise_xor(hi_ref[0], k)
         column = pl.multiple_of(place * colb, colb)
         copies.append(
-            pltpu.make_async_copy(buf.at[k], out_ref.at[:, pl.ds(column, colb), :], sem.at[k])
+            pltpu.make_async_copy(buf.at[i], out_ref.at[:, pl.ds(column, colb), :], sem.at[i])
         )
         copies[-1].start()
     for copy in copies:
@@ -340,21 +340,24 @@
             out_shape=[jax.ShapeDtypeStruct((each, inner), bf)] * high,
         )(q, kv, other)
 
-    def finish(c, hi, pieces, mixes, prior):
+    def finish(c, ks, hi, pieces, mixes, prior):
         extra_specs, extra = [], []
         if prior is not None:
             extra_specs, extra = [pl.BlockSpec(memory_space=pl.ANY)], [prior]
         return call(
-            functools.partial(finish_kernel, c, high),
-            work,
+            functools.partial(finish_kernel, c, ks, high),
+            work // 2,
             in_specs=[SMEM, pick(1, (inner, feat))]
-            + [whole(each, feat)] * high
-            + [whole(each, inner)] * high
+            + [whole(each, feat)] * len(ks)
+            + [whole(each, inner)] * len(ks)
             + extra_specs,
             out_specs=HBM,
             out_shape=jax.ShapeDtypeStruct((rows, cols, feat), bf),
-            scratch_shapes=[pltpu.VMEM(held, bf), pltpu.SemaphoreType.DMA((high,))],
-            input_output_aliases={2 * high + 2: 0} if extra else {},
+            scratch_shapes=[
+                pltpu.VMEM((len(ks), rows, COLB, feat), bf),
+                pltpu.SemaphoreType.DMA((len(ks),)),
+            ],
+            input_output_aliases={2 * len(ks) + 2: 0} if extra else {},
         )(hi, out_weights, *pieces, *mixes, *extra)
 
     def swap(a):
@@ -406,19 +409,20 @@
         other = swap(kv)
         if mixes is not None:
             mixes = after(mixes, q)
-            home[-1].update(exchange(mixes, heavy))
+            home[-1].update(exchange(mixes, light))
         mixes = timed(q, kv, other)
         last = mixes[0]
-        home.append(exchange(mixes, light))
+        home.append(exchange(mixes, heavy))
         if c + 1 < CHUNKS:
             hi = gate(after(hi, last))
             last = hi
-    home[-1].update(exchange(mixes, heavy))
+    home[-1].update(exchange(mixes, light))
     out = None
     for c in range(CHUNKS):
-        made = after([pieces[c][k] for k in range(high)], last)
-        mixes = [home[c][k] for k in range(high)]
-        out = finish(c, hi, made, mixes, out)
+        for ks in (light, heavy):
+            made = after([pieces[c][k] for k in ks], last)
+            mixes = [home[c][k] for k in ks]
+            out = finish(c, ks, hi, made, mixes, out)
     return out[None]
 
 

time: 83.4 us -> 86 us (1.031)
  the two profiles are of different devices: /device:TPU:1 before, /device:TPU:0 now
where the time goes in v3:
time: 86 us; the launch traced here: 85.7 us
  waiting for transfers between devices  32.5 us (38%)
  starting transfers between devices  27.2 us (32%)
  Pallas kernels  25.5 us (30%)
    ppermute x16, waiting for transfers between devices, permute(): return lax.ppermute(piece, ('tm', 'space'), route(k))  32.5 us
    ppermute x16, starting transfers between devices, permute(): return lax.ppermute(piece, ('tm', 'space'), route(k))  24.5 us
    pallas_call x4, Pallas kernels, finish(): call(functools.partial(finish_kernel, c, ks, high), work // 2, in_specs=[...  6.72 us
    pallas_call x4, Pallas kernels, height(): call(functools.partial(height_kernel, ks), 2 * work, in_specs=[SMEM, whol...  6.7 us
    pallas_call x1, Pallas kernels, load(): call(load_kernel, 2 * work, in_specs=[HBM, HBM, HBM], out_specs=[whole(*s...  3.73 us
    pallas_call x2, Pallas kernels, time_project(): call(time_project_kernel, 3 * work, in_specs=[whole(each, feat)] * high +...  3.09 us
    pallas_call x2, Pallas kernels, timed(): call(time_kernel, 2 * work, in_specs=qkv_in, out_specs=[whole(each, inner...  2.81 us
    ppermute x4, starting transfers between devices, swap(): return lax.ppermute(a, 'space', [(0, 1), (1, 0)])  2.67 us
  transfers between devices with their start and end apart: 20, of which 8 were waited for; matrix products, arithmetic and copies ran while one was open for 0% of the time, Pallas kernels for 20%

profile of v3, /device:TPU:0, one launch (start us, length us, event | category | flops | bytes accessed | tf_op | source)
XLA Modules:
  0.0 85.7 jit_solution(2898445491336733589)
XLA Ops:
  0.0 3.7 %shard_map.46 = (bf16[384,1024]{1,0:T(8,128)(2,1)S(1)}, bf16[384,1024]{1,0:T(8,128)(2,1)S(1)}, bf16[1024,1536]{1,0:T(8,128)(2,1)S(1)}, f32[2,1024]{1,0:T(2,128)S...) custom-call(bf16[12,64,1024]{2,1,0:T(8,128)(2,1)} %bitcast.5, f32[2,1024]{1,0:T(2,128)} %refs_4_.3, ...), custom_call_target="tpu_custom_call" | custom-call | flops 805306368 | bytes 1572864 | tf_op jit(solution)/shard_map/pallas_call | solution.py:273
  4.3 2.0 %shard_map.47 = (bf16[384,512]{1,0:T(8,128)(2,1)S(1)}, bf16[384,512]{1,0:T(8,128)(2,1)S(1)}, bf16[384,1024]{1,0:T(8,128)(2,1)S(1)}) custom-call(bf16[384,1024]{1,0:T(8,128)(2,1)S(1)} %get-tuple-element.61.first_ref, bf16[4,12,8,1024]{3,2,1,0:T(8,128)(2,1)S(1)} %get-tuple-element.62.x_ref, f32[2,1024]{1,0:T(2,128)S(1)} %get-tuple-element.63.gain_ref, ...), custom_call_target="tpu_custom_call" | custom-call | flops 1610612736 | bytes 1572864 | tf_op jit(solution)/shard_map/pallas_call | solution.py:287
  6.3 1.6 %shard_map.48 = (bf16[96,1024]{1,0:T(8,128)(2,1)S(1)}, bf16[96,1024]{1,0:T(8,128)(2,1)S(1)}) custom-call(s32[1]{0:T(128)} %bitcast.hi_ref.in_ref, bf16[4,12,8,1024]{3,2,1,0:T(8,128)(2,1)S(1)} %get-tuple-element.60.x_ref, bf16[384,512]{1,0:T(8,128)(2,1)S(1)} %get-tuple-element.70.q_ref, bf16[384,1024]{1,0:T(8,128)(2,1)S(1)} %get-tuple-element.68.kv_ref, ...), custom_call_target="tpu_custom_call" | custom-call | flops 805306368 | bytes 1572864 | tf_op jit(solution)/shard_map/pallas_call | solution.py:301
  8.0 1.8 %shard_map.49 = (bf16[96,1024]{1,0:T(8,128)(2,1)S(1)}, bf16[96,1024]{1,0:T(8,128)(2,1)S(1)}) custom-call(s32[1]{0:T(128)} %bitcast.hi_ref.in_ref, bf16[4,12,8,1024]{3,2,1,0:T(8,128)(2,1)S(1)} %get-tuple-element.60.x_ref, bf16[384,512]{1,0:T(8,128)(2,1)S(1)} %get-tuple-element.70.q_ref, bf16[384,1024]{1,0:T(8,128)(2,1)S(1)} %get-tuple-element.68.kv_ref, ...), custom_call_target="tpu_custom_call" | custom-call | flops 805306368 | bytes 1572864 | tf_op jit(solution)/shard_map/pallas_call | solution.py:301
  10.5 3.1 %collective-permute-start.2 = (bf16[96,1024]{1,0:T(8,128)(2,1)S(1)}, bf16[96,1024]{1,0:T(8,128)(2,1)S(1)}, u32[]{:S(2)}, u32[]{:S(2)}) collective-permute-start(bf16[96,1024]{1,0:T(8,128)(2,1)S(1)} %get-tuple-element.108.refs_0_), channel_id=1, source_target_pairs={{0,4},{1,6},{2,5},{3,7},{4,0},{5,2},{6,1},{7,3},{8,15},{9,13},{10,... | collective-permute-start | bytes 589832 | tf_op jit(solution)/shard_map/ppermute | solution.py:377
  13.6 3.5 %collective-permute-start.3 = (bf16[96,1024]{1,0:T(8,128)(2,1)S(1)}, bf16[96,1024]{1,0:T(8,128)(2,1)S(1)}, u32[]{:S(2)}, u32[]{:S(2)}) collective-permute-start(bf16[96,1024]{1,0:T(8,128)(2,1)S(1)} %get-tuple-element.105.refs_1_), channel_id=1, source_target_pairs={{0,10},{1,8},{2,11},{3,9},{4,14},{5,12},{6,15},{7,13},{8,1},{9,3},... | collective-permute-start | bytes 589832 | tf_op jit(solution)/shard_map/ppermute | solution.py:377
  17.1 1.6 %shard_map.50 = (bf16[96,1024]{1,0:T(8,128)(2,1)S(1)}, bf16[96,1024]{1,0:T(8,128)(2,1)S(1)}) custom-call(s32[1]{0:T(128)} %bitcast.hi_ref.in_ref, bf16[4,12,8,1024]{3,2,1,0:T(8,128)(2,1)S(1)} %get-tuple-element.62.x_ref, bf16[384,512]{1,0:T(8,128)(2,1)S(1)} %get-tuple-element.77.q_ref, bf16[384,1024]{1,0:T(8,128)(2,1)S(1)} %get-tuple-element.75.kv_ref, ...), custom_call_target="tpu_custom_call" | custom-call | flops 805306368 | bytes 1572864 | tf_op jit(solution)/shard_map/pallas_call | solution.py:301
  18.8 1.6 %shard_map.51 = (bf16[96,1024]{1,0:T(8,128)(2,1)S(1)}, bf16[96,1024]{1,0:T(8,128)(2,1)S(1)}) custom-call(s32[1]{0:T(128)} %bitcast.hi_ref.in_ref, bf16[4,12,8,1024]{3,2,1,0:T(8,128)(2,1)S(1)} %get-tuple-element.62.x_ref, bf16[384,512]{1,0:T(8,128)(2,1)S(1)} %get-tuple-element.77.q_ref, bf16[384,1024]{1,0:T(8,128)(2,1)S(1)} %get-tuple-element.75.kv_ref, ...), custom_call_target="tpu_custom_call" | custom-call | flops 805306368 | bytes 1572864 | tf_op jit(solution)/shard_map/pallas_call | solution.py:301
  20.4 2.0 %collective-permute-done.3.refs_2_ = bf16[96,1024]{1,0:T(8,128)(2,1)S(1)} collective-permute-done((bf16[96,1024]{1,0:T(8,128)(2,1)S(1)}, bf16[96,1024]{1,0:T(8,128)(2,1)S(1)}, u32[]{:S(2)}, u32[]{:S(2)}) %collective-permute-start.3) | collective-permute-done | bytes 196640 | tf_op jit(solution)/shard_map/ppermute | solution.py:377
  22.5 7.1 %collective-permute-done.4.refs_3_ = bf16[96,1024]{1,0:T(8,128)(2,1)S(1)} collective-permute-done((bf16[96,1024]{1,0:T(8,128)(2,1)S(1)}, bf16[96,1024]{1,0:T(8,128)(2,1)S(1)}, u32[]{:S(2)}, u32[]{:S(2)}) %collective-permute-start.4) | collective-permute-done | bytes 196640 | tf_op jit(solution)/shard_map/ppermute | solution.py:377
  29.5 1.5 %shard_map.52 = (bf16[384,512]{1,0:T(8,128)(2,1)S(1)}, bf16[384,1024]{1,0:T(8,128)(2,1)S(1)}) custom-call(bf16[96,1024]{1,0:T(8,128)(2,1)S(1)} %collective-permute-done.1.refs_0_, bf16[96,1024]{1,0:T(8,128)(2,1)S(1)} %collective-permute-done.2.refs_1_, bf16[96,1024]{1,0:T(8,128)(2,1)S(1)} %collective-permute-done.3.refs_2_, ...), custom_call_target="tpu_custom_call" | custom-call | flops 1207959552 | bytes 1572864 | tf_op jit(solution)/shard_map/pallas_call | solution.py:326
  31.1 2.0 %collective-permute-start.6 = (bf16[384,1024]{1,0:T(8,128)(2,1)S(1)}, bf16[384,1024]{1,0:T(8,128)(2,1)S(1)}, u32[]{:S(2)}, u32[]{:S(2)}) collective-permute-start(bf16[384,1024]{1,0:T(8,128)(2,1)S(1)} %get-tuple-element.84.kv_ref), channel_id=1, source_target_pairs={{0,1},{1,0},{2,3},{3,2},{4,5},{5,4},{6,7},{7,6},{8,9},{9,8},{10,11... | collective-permute-start | bytes 2359304 | tf_op jit(solution)/shard_map/ppermute | solution.py:364
  33.1 4.2 %collective-permute-start.8 = (bf16[96,1024]{1,0:T(8,128)(2,1)S(1)}, bf16[96,1024]{1,0:T(8,128)(2,1)S(1)}, u32[]{:S(2)}, u32[]{:S(2)}) collective-permute-start(bf16[96,1024]{1,0:T(8,128)(2,1)S(1)} %get-tuple-element.101.refs_0_), channel_id=1, source_target_pairs={{0,4},{1,6},{2,5},{3,7},{4,0},{5,2},{6,1},{7,3},{8,15},{9,13},{10,... | collective-permute-start | bytes 589832 | tf_op jit(solution)/shard_map/ppermute | solution.py:377
  37.2 3.3 %collective-permute-start.10 = (bf16[96,1024]{1,0:T(8,128)(2,1)S(1)}, bf16[96,1024]{1,0:T(8,128)(2,1)S(1)}, u32[]{:S(2)}, u32[]{:S(2)}) collective-permute-start(bf16[96,1024]{1,0:T(8,128)(2,1)S(1)} %get-tuple-element.97.refs_0_), channel_id=1, source_target_pairs={{0,14},{1,12},{2,15},{3,13},{4,10},{5,8},{6,11},{7,9},{8,5},{9,7},... | collective-permute-start | bytes 589832 | tf_op jit(solution)/shard_map/ppermute | solution.py:377
  43.5 6.8 %collective-permute-done.10.refs_3_ = bf16[96,1024]{1,0:T(8,128)(2,1)S(1)} collective-permute-done((bf16[96,1024]{1,0:T(8,128)(2,1)S(1)}, bf16[96,1024]{1,0:T(8,128)(2,1)S(1)}, u32[]{:S(2)}, u32[]{:S(2)}) %collective-permute-start.10) | collective-permute-done | bytes 196640 | tf_op jit(solution)/shard_map/ppermute | solution.py:377
  50.3 8.6 %collective-permute-done.9.refs_2_ = bf16[96,1024]{1,0:T(8,128)(2,1)S(1)} collective-permute-done((bf16[96,1024]{1,0:T(8,128)(2,1)S(1)}, bf16[96,1024]{1,0:T(8,128)(2,1)S(1)}, u32[]{:S(2)}, u32[]{:S(2)}) %collective-permute-start.9) | collective-permute-done | bytes 196640 | tf_op jit(solution)/shard_map/ppermute | solution.py:377
  60.5 2.0 %collective-permute-start.16 = (bf16[96,512]{1,0:T(8,128)(2,1)S(1)}, bf16[96,512]{1,0:T(8,128)(2,1)S(1)}, u32[]{:S(2)}, u32[]{:S(2)}) collective-permute-start(bf16[96,512]{1,0:T(8,128)(2,1)S(1)} %get-tuple-element.106), channel_id=1, source_target_pairs={{0,14},{1,12},{2,15},{3,13},{4,10},{5,8},{6,11},{7,9},{8,5},{9,7},... | collective-permute-start | bytes 294920 | tf_op jit(solution)/shard_map/ppermute | solution.py:377
  63.2 3.4 %collective-permute-start.17 = (bf16[96,512]{1,0:T(8,128)(2,1)S(1)}, bf16[96,512]{1,0:T(8,128)(2,1)S(1)}, u32[]{:S(2)}, u32[]{:S(2)}) collective-permute-start(bf16[96,512]{1,0:T(8,128)(2,1)S(1)} %get-tuple-element.107), channel_id=1, source_target_pairs={{0,10},{1,8},{2,11},{3,9},{4,14},{5,12},{6,15},{7,13},{8,1},{9,3},... | collective-permute-start | bytes 294920 | tf_op jit(solution)/shard_map/ppermute | solution.py:377
  69.3 1.9 %collective-permute-done.18.refs_2_ = bf16[96,512]{1,0:T(8,128)(2,1)S(1)} collective-permute-done((bf16[96,512]{1,0:T(8,128)(2,1)S(1)}, bf16[96,512]{1,0:T(8,128)(2,1)S(1)}, u32[]{:S(2)}, u32[]{:S(2)}) %collective-permute-start.18) | collective-permute-done | bytes 98336 | tf_op jit(solution)/shard_map/ppermute | solution.py:377
  73.2 1.7 %shard_map.56.refs_4_ = bf16[12,64,1024]{2,1,0:T(8,128)(2,1)} custom-call(s32[1]{0:T(128)} %gate.1.hi_ref, bf16[2,512,1024]{2,1,0:T(8,128)(2,1)S(1)} %copy-done, bf16[96,1024]{1,0:T(8,128)(2,1)S(1)} %get-tuple-element.108.refs_0_, bf16[96,1024]{1,0:T(8,128)(2,1)S(1)} %get-tuple-element.109.refs_1_, bf16[96,512]{1,0:T(8,128)(2,1)S(1)} %collective-permute-done.18.refs_2_, ...), custom_call_target="tpu_custom_call" | custom-call | flops 201326592 | bytes 1572864 | tf_op jit(solution)/shard_map/pallas_call | solution.py:347
  74.9 1.7 %shard_map.57.refs_4_ = bf16[12,64,1024]{2,1,0:T(8,128)(2,1)} custom-call(s32[1]{0:T(128)} %gate.1.hi_ref, bf16[2,512,1024]{2,1,0:T(8,128)(2,1)S(1)} %copy-done, bf16[96,1024]{1,0:T(8,128)(2,1)S(1)} %get-tuple-element.104.refs_0_, bf16[96,1024]{1,0:T(8,128)(2,1)S(1)} %get-tuple-element.105.refs_1_, ...), custom_call_target="tpu_custom_call", output_to_operand_aliasing={{}: (6, {})} | custom-call | flops 201326592 | bytes 1572864 | tf_op jit(solution)/shard_map/pallas_call | solution.py:347
  76.6 1.7 %shard_map.58.refs_4_ = bf16[12,64,1024]{2,1,0:T(8,128)(2,1)} custom-call(s32[1]{0:T(128)} %gate.1.hi_ref, bf16[2,512,1024]{2,1,0:T(8,128)(2,1)S(1)} %copy-done, bf16[96,1024]{1,0:T(8,128)(2,1)S(1)} %get-tuple-element.101.refs_0_, bf16[96,1024]{1,0:T(8,128)(2,1)S(1)} %get-tuple-element.102.refs_1_, ...), custom_call_target="tpu_custom_call", output_to_operand_aliasing={{}: (6, {})} | custom-call | flops 201326592 | bytes 1572864 | tf_op jit(solution)/shard_map/pallas_call | solution.py:347
  79.5 4.4 %collective-permute-done.13.refs_3_ = bf16[96,512]{1,0:T(8,128)(2,1)S(1)} collective-permute-done((bf16[96,512]{1,0:T(8,128)(2,1)S(1)}, bf16[96,512]{1,0:T(8,128)(2,1)S(1)}, u32[]{:S(2)}, u32[]{:S(2)}) %collective-permute-start.13) | collective-permute-done | bytes 98336 | tf_op jit(solution)/shard_map/ppermute | solution.py:377
  83.9 1.7 %shard_map.59 = bf16[12,64,1024]{2,1,0:T(8,128)(2,1)} custom-call(s32[1]{0:T(128)} %gate.1.hi_ref, bf16[2,512,1024]{2,1,0:T(8,128)(2,1)S(1)} %copy-done, bf16[96,1024]{1,0:T(8,128)(2,1)S(1)} %get-tuple-element.97.refs_0_, bf16[96,1024]{1,0:T(8,128)(2,1)S(1)} %get-tuple-element.98.refs_1_, ...), custom_call_target="tpu_custom_call", output_to_operand_aliasing={{}: (6, {})} | custom-call | flops 201326592 | bytes 1572864 | tf_op jit(solution)/shard_map/pallas_call | solution.py:347
  (40 shorter events, 12.4 us)
Async XLA Ops:
  3.7 2.6 %collective-permute-start = (bf16[384,1024]{1,0:T(8,128)(2,1)S(1)}, bf16[384,1024]{1,0:T(8,128)(2,1)S(1)}, u32[]{:S(2)}, u32[]{:S(2)}) collective-permute-start(bf16[384,1024]{1,0:T(8,128)(2,1)S(1)} %get-tuple-element.68.kv_ref), channel_id=1, source_target_pairs={{0,1},{1,0},{2,3},{3,2},{4,5},{5,4},{6,7},{7,6},{8,9},{9,8},{10,11... | collective-permute-start | bytes 2359304 | tf_op jit(solution)/shard_map/ppermute | solution.py:364
  6.3 10.9 %collective-permute-start.5 = (bf16[384,1024]{1,0:T(8,128)(2,1)S(1)}, bf16[384,1024]{1,0:T(8,128)(2,1)S(1)}, u32[]{:S(2)}, u32[]{:S(2)}) collective-permute-start(bf16[384,1024]{1,0:T(8,128)(2,1)S(1)} %get-tuple-element.75.kv_ref), channel_id=1, source_target_pairs={{0,1},{1,0},{2,3},{3,2},{4,5},{5,4},{6,7},{7,6},{8,9},{9,8},{10,11... | collective-permute-start | bytes 2359304 | tf_op jit(solution)/shard_map/ppermute | solution.py:364
  8.0 21.5 %slice-start = ((s8[6291456]{0:T(1024)(128)(4,1)}), s8[4194304]{0:T(1024)(128)(4,1)S(1)}, s32[]{:S(2)}) async-start(s8[6291456]{0:T(1024)(128)(4,1)} %bitcast.3), calls=%async_computation | async-start | bytes 8388608
  9.8 10.6 %collective-permute-start.1 = (bf16[96,1024]{1,0:T(8,128)(2,1)S(1)}, bf16[96,1024]{1,0:T(8,128)(2,1)S(1)}, u32[]{:S(2)}, u32[]{:S(2)}) collective-permute-start(bf16[96,1024]{1,0:T(8,128)(2,1)S(1)} %get-tuple-element.109.refs_1_), channel_id=1, source_target_pairs={{0,0},{1,2},{2,1},{3,3},{4,4},{5,6},{6,5},{7,7},{8,11},{9,9},{10,1... | collective-permute-start | bytes 589832 | tf_op jit(solution)/shard_map/ppermute | solution.py:377
  10.5 10.0 %collective-permute-start.2 = (bf16[96,1024]{1,0:T(8,128)(2,1)S(1)}, bf16[96,1024]{1,0:T(8,128)(2,1)S(1)}, u32[]{:S(2)}, u32[]{:S(2)}) collective-permute-start(bf16[96,1024]{1,0:T(8,128)(2,1)S(1)} %get-tuple-element.108.refs_0_), channel_id=1, source_target_pairs={{0,4},{1,6},{2,5},{3,7},{4,0},{5,2},{6,1},{7,3},{8,15},{9,13},{10,... | collective-permute-start | bytes 589832 | tf_op jit(solution)/shard_map/ppermute | solution.py:377
  13.6 15.9 %slice-start.1 = ((s8[6291456]{0:T(1024)(128)(4,1)}), s8[2097152]{0:T(1024)(128)(4,1)S(1)}, s32[]{:S(2)}) async-start(s8[6291456]{0:T(1024)(128)(4,1)} %bitcast.3), calls=%async_computation.1 | async-start | bytes 4194304
  13.6 8.9 %collective-permute-start.3 = (bf16[96,1024]{1,0:T(8,128)(2,1)S(1)}, bf16[96,1024]{1,0:T(8,128)(2,1)S(1)}, u32[]{:S(2)}, u32[]{:S(2)}) collective-permute-start(bf16[96,1024]{1,0:T(8,128)(2,1)S(1)} %get-tuple-element.105.refs_1_), channel_id=1, source_target_pairs={{0,10},{1,8},{2,11},{3,9},{4,14},{5,12},{6,15},{7,13},{8,1},{9,3},... | collective-permute-start | bytes 589832 | tf_op jit(solution)/shard_map/ppermute | solution.py:377
  17.1 12.4 %collective-permute-start.4 = (bf16[96,1024]{1,0:T(8,128)(2,1)S(1)}, bf16[96,1024]{1,0:T(8,128)(2,1)S(1)}, u32[]{:S(2)}, u32[]{:S(2)}) collective-permute-start(bf16[96,1024]{1,0:T(8,128)(2,1)S(1)} %get-tuple-element.104.refs_0_), channel_id=1, source_target_pairs={{0,14},{1,12},{2,15},{3,13},{4,10},{5,8},{6,11},{7,9},{8,5},{9,7},... | collective-permute-start | bytes 589832 | tf_op jit(solution)/shard_map/ppermute | solution.py:377
  18.8 10.8 %copy-start.1 = (f32[2,1024]{1,0:T(2,128)S(1)}, f32[2,1024]{1,0:T(2,128)}, u32[]{:S(2)}) copy-start(f32[2,1024]{1,0:T(2,128)} %refs_4_.3) | copy-start | bytes 24580
  31.1 10.4 %collective-permute-start.6 = (bf16[384,1024]{1,0:T(8,128)(2,1)S(1)}, bf16[384,1024]{1,0:T(8,128)(2,1)S(1)}, u32[]{:S(2)}, u32[]{:S(2)}) collective-permute-start(bf16[384,1024]{1,0:T(8,128)(2,1)S(1)} %get-tuple-element.84.kv_ref), channel_id=1, source_target_pairs={{0,1},{1,0},{2,3},{3,2},{4,5},{5,4},{6,7},{7,6},{8,9},{9,8},{10,11... | collective-permute-start | bytes 2359304 | tf_op jit(solution)/shard_map/ppermute | solution.py:364
  33.1 10.4 %collective-permute-start.8 = (bf16[96,1024]{1,0:T(8,128)(2,1)S(1)}, bf16[96,1024]{1,0:T(8,128)(2,1)S(1)}, u32[]{:S(2)}, u32[]{:S(2)}) collective-permute-start(bf16[96,1024]{1,0:T(8,128)(2,1)S(1)} %get-tuple-element.101.refs_0_), channel_id=1, source_target_pairs={{0,4},{1,6},{2,5},{3,7},{4,0},{5,2},{6,1},{7,3},{8,15},{9,13},{10,... | collective-permute-start | bytes 589832 | tf_op jit(solution)/shard_map/ppermute | solution.py:377
  37.2 13.0 %collective-permute-start.10 = (bf16[96,1024]{1,0:T(8,128)(2,1)S(1)}, bf16[96,1024]{1,0:T(8,128)(2,1)S(1)}, u32[]{:S(2)}, u32[]{:S(2)}) collective-permute-start(bf16[96,1024]{1,0:T(8,128)(2,1)S(1)} %get-tuple-element.97.refs_0_), channel_id=1, source_target_pairs={{0,14},{1,12},{2,15},{3,13},{4,10},{5,8},{6,11},{7,9},{8,5},{9,7},... | collective-permute-start | bytes 589832 | tf_op jit(solution)/shard_map/ppermute | solution.py:377
  40.6 2.9 %collective-permute-start.7 = (bf16[96,1024]{1,0:T(8,128)(2,1)S(1)}, bf16[96,1024]{1,0:T(8,128)(2,1)S(1)}, u32[]{:S(2)}, u32[]{:S(2)}) collective-permute-start(bf16[96,1024]{1,0:T(8,128)(2,1)S(1)} %get-tuple-element.102.refs_1_), channel_id=1, source_target_pairs={{0,0},{1,2},{2,1},{3,3},{4,4},{5,6},{6,5},{7,7},{8,11},{9,9},{10,1... | collective-permute-start | bytes 589832 | tf_op jit(solution)/shard_map/ppermute | solution.py:377
  41.4 17.4 %collective-permute-start.9 = (bf16[96,1024]{1,0:T(8,128)(2,1)S(1)}, bf16[96,1024]{1,0:T(8,128)(2,1)S(1)}, u32[]{:S(2)}, u32[]{:S(2)}) collective-permute-start(bf16[96,1024]{1,0:T(8,128)(2,1)S(1)} %get-tuple-element.98.refs_1_), channel_id=1, source_target_pairs={{0,10},{1,8},{2,11},{3,9},{4,14},{5,12},{6,15},{7,13},{8,1},{9,3},... | collective-permute-start | bytes 589832 | tf_op jit(solution)/shard_map/ppermute | solution.py:377
  60.4 12.8 %copy-start = (bf16[2,512,1024]{2,1,0:T(8,128)(2,1)S(1)}, bf16[2,512,1024]{2,1,0:T(8,128)(2,1)}, u32[]{:S(2)}) copy-start(bf16[2,512,1024]{2,1,0:T(8,128)(2,1)} %w_ref.17) | copy-start | bytes 6291460
  60.4 6.2 %collective-permute-start.11 = (bf16[384,1024]{1,0:T(8,128)(2,1)S(1)}, bf16[384,1024]{1,0:T(8,128)(2,1)S(1)}, u32[]{:S(2)}, u32[]{:S(2)}) collective-permute-start(bf16[384,1024]{1,0:T(8,128)(2,1)S(1)} %get-tuple-element.95.kv_ref), channel_id=1, source_target_pairs={{0,1},{1,0},{2,3},{3,2},{4,5},{5,4},{6,7},{7,6},{8,9},{9,8},{10,11... | collective-permute-start | bytes 2359304 | tf_op jit(solution)/shard_map/ppermute | solution.py:364
  60.5 8.1 %collective-permute-start.16 = (bf16[96,512]{1,0:T(8,128)(2,1)S(1)}, bf16[96,512]{1,0:T(8,128)(2,1)S(1)}, u32[]{:S(2)}, u32[]{:S(2)}) collective-permute-start(bf16[96,512]{1,0:T(8,128)(2,1)S(1)} %get-tuple-element.106), channel_id=1, source_target_pairs={{0,14},{1,12},{2,15},{3,13},{4,10},{5,8},{6,11},{7,9},{8,5},{9,7},... | collective-permute-start | bytes 294920 | tf_op jit(solution)/shard_map/ppermute | solution.py:377
  62.6 8.6 %collective-permute-start.18 = (bf16[96,512]{1,0:T(8,128)(2,1)S(1)}, bf16[96,512]{1,0:T(8,128)(2,1)S(1)}, u32[]{:S(2)}, u32[]{:S(2)}) collective-permute-start(bf16[96,512]{1,0:T(8,128)(2,1)S(1)} %get-tuple-element.111), channel_id=1, source_target_pairs={{0,4},{1,6},{2,5},{3,7},{4,0},{5,2},{6,1},{7,3},{8,15},{9,13},{10,... | collective-permute-start | bytes 294920 | tf_op jit(solution)/shard_map/ppermute | solution.py:377
  62.6 10.0 %collective-permute-start.19 = (bf16[96,512]{1,0:T(8,128)(2,1)S(1)}, bf16[96,512]{1,0:T(8,128)(2,1)S(1)}, u32[]{:S(2)}, u32[]{:S(2)}) collective-permute-start(bf16[96,512]{1,0:T(8,128)(2,1)S(1)} %get-tuple-element.112), channel_id=1, source_target_pairs={{0,0},{1,2},{2,1},{3,3},{4,4},{5,6},{6,5},{7,7},{8,11},{9,9},{10,1... | collective-permute-start | bytes 294920 | tf_op jit(solution)/shard_map/ppermute | solution.py:377
  63.2 11.7 %collective-permute-start.17 = (bf16[96,512]{1,0:T(8,128)(2,1)S(1)}, bf16[96,512]{1,0:T(8,128)(2,1)S(1)}, u32[]{:S(2)}, u32[]{:S(2)}) collective-permute-start(bf16[96,512]{1,0:T(8,128)(2,1)S(1)} %get-tuple-element.107), channel_id=1, source_target_pairs={{0,10},{1,8},{2,11},{3,9},{4,14},{5,12},{6,15},{7,13},{8,1},{9,3},... | collective-permute-start | bytes 294920 | tf_op jit(solution)/shard_map/ppermute | solution.py:377
  68.0 8.6 %collective-permute-start.14 = (bf16[96,512]{1,0:T(8,128)(2,1)S(1)}, bf16[96,512]{1,0:T(8,128)(2,1)S(1)}, u32[]{:S(2)}, u32[]{:S(2)}) collective-permute-start(bf16[96,512]{1,0:T(8,128)(2,1)S(1)} %get-tuple-element.103), channel_id=1, source_target_pairs={{0,4},{1,6},{2,5},{3,7},{4,0},{5,2},{6,1},{7,3},{8,15},{9,13},{10,... | collective-permute-start | bytes 294920 | tf_op jit(solution)/shard_map/ppermute | solution.py:377
  68.6 8.0 %collective-permute-start.15 = (bf16[96,512]{1,0:T(8,128)(2,1)S(1)}, bf16[96,512]{1,0:T(8,128)(2,1)S(1)}, u32[]{:S(2)}, u32[]{:S(2)}) collective-permute-start(bf16[96,512]{1,0:T(8,128)(2,1)S(1)} %get-tuple-element.96), channel_id=1, source_target_pairs={{0,0},{1,2},{2,1},{3,3},{4,4},{5,6},{6,5},{7,7},{8,11},{9,9},{10,1... | collective-permute-start | bytes 294920 | tf_op jit(solution)/shard_map/ppermute | solution.py:377
  71.2 8.3 %collective-permute-start.12 = (bf16[96,512]{1,0:T(8,128)(2,1)S(1)}, bf16[96,512]{1,0:T(8,128)(2,1)S(1)}, u32[]{:S(2)}, u32[]{:S(2)}) collective-permute-start(bf16[96,512]{1,0:T(8,128)(2,1)S(1)} %get-tuple-element.99), channel_id=1, source_target_pairs={{0,14},{1,12},{2,15},{3,13},{4,10},{5,8},{6,11},{7,9},{8,5},{9,7},... | collective-permute-start | bytes 294920 | tf_op jit(solution)/shard_map/ppermute | solution.py:377
  72.6 11.3 %collective-permute-start.13 = (bf16[96,512]{1,0:T(8,128)(2,1)S(1)}, bf16[96,512]{1,0:T(8,128)(2,1)S(1)}, u32[]{:S(2)}, u32[]{:S(2)}) collective-permute-start(bf16[96,512]{1,0:T(8,128)(2,1)S(1)} %get-tuple-element.100), channel_id=1, source_target_pairs={{0,10},{1,8},{2,11},{3,9},{4,14},{5,12},{6,15},{7,13},{8,1},{9,3},... | collective-permute-start | bytes 294920 | tf_op jit(solution)/shard_map/ppermute | solution.py:377

commit v4 on v3

--- a/solution.py
+++ b/solution.py
@@ -177,29 +177,37 @@
     out_ref[0] = in_ref[0]
 
 
-def time_kernel(q_ref, kv_ref, other_ref, *mix_refs):
-    each = mix_refs[0].shape[0]
+def time_kernel(held, q_ref, kv_ref, other_ref, *refs):
+    held_refs, mix_refs = refs[:held], refs[held:]
+    each = q_ref.shape[0] // len(mix_refs)
+    bases = [0 if ref.shape[0] == each else each for ref in mix_refs]
     spans = [
         [(k * each + p, POSB) for k in range(len(mix_refs))] for p in range(0, each, POSB)
     ]
+    for ref, held_ref in zip(mix_refs, held_refs):
+        ref[:each, :] = held_ref[...]
 
     def put(span, lo, out):
         at = span[0][0]
         for k, ref in enumerate(mix_refs):
-            ref[at : at + POSB, lo : lo + out.shape[1]] = out[k * POSB : (k + 1) * POSB]
+            row = bases[k] + at
+            ref[row : row + POSB, lo : lo + out.shape[1]] = out[k * POSB : (k + 1) * POSB]
 
     attend(q_ref, kv_ref, other_ref, spans, POSB, put)
 
 
-def finish_kernel(c, ks, high, hi_ref, w_ref, *refs):
-    pieces, mixes = refs[: len(ks)], refs[len(ks) : 2 * len(ks)]
+def finish_kernel(items, mixed, high, hi_ref, w_ref, *refs):
+    pieces, mixes = refs[: len(items)], refs[len(items) : len(items) + mixed]
     out_ref, buf, sem = refs[-3:]
     _, rows, colb, feat = buf.shape
     per = rows * colb
-    mixed = jnp.concatenate([ref[...] for ref in mixes], axis=0)
-    update = jnp.dot(mixed, w_ref[...], preferred_element_type=jnp.float32)
+    update = jnp.dot(
+        jnp.concatenate([ref[...] for ref in mixes], axis=0),
+        w_ref[...],
+        preferred_element_type=jnp.float32,
+    )
     copies = []
-    for i, k in enumerate(ks):
+    for i, (c, k) in enumerate(items):
         total = pieces[i][...].astype(jnp.float32) + update[i * per : (i + 1) * per]
         buf[i] = total.reshape(rows, colb, feat).astype(jnp.bfloat16)
         place = c * high + jnp.bitwise_xor(hi_ref[0], k)
@@ -264,11 +272,11 @@
     def after(values, earlier):
         return lax.optimization_barrier((values, earlier))[0]
 
-    held = (blocks, rows, COLB, feat)
+    tile = (blocks, rows, COLB, feat)
 
     def load(x):
         shapes = [(count, 2 * inner), (count, feat), (feat, 3 * inner), gains.shape]
-        shapes += [held] * CHUNKS
+        shapes += [tile] * CHUNKS
         kinds = [bf, bf, bf, gains.dtype] + [bf] * CHUNKS
         return call(
             load_kernel,
@@ -289,7 +297,7 @@
             4 * work,
             in_specs=[
                 whole(count, feat),
-                whole(*held),
+                whole(*tile),
                 whole(*gains.shape),
                 whole(feat, 3 * inner),
             ],
@@ -301,7 +309,7 @@
         return call(
             functools.partial(height_kernel, ks),
             2 * work,
-            in_specs=[SMEM, whole(*held)] + qkv_in + [HBM],
+            in_specs=[SMEM, whole(*tile)] + qkv_in + [HBM],
             out_specs=[whole(each, feat)] * len(ks),
             out_shape=[jax.ShapeDtypeStruct((each, feat), bf)] * len(ks),
             scratch_shapes=[
@@ -331,33 +339,34 @@
             **qkv_out,
         )(*pieces, gains, qkv_weights)
 
-    def timed(q, kv, other):
+    def timed(q, kv, other, held):
+        sizes = [each * (1 + (k < len(held))) for k in range(high)]
         return call(
-            time_kernel,
+            functools.partial(time_kernel, len(held)),
             2 * work,
-            in_specs=qkv_in,
-            out_specs=[whole(each, inner)] * high,
-            out_shape=[jax.ShapeDtypeStruct((each, inner), bf)] * high,
-        )(q, kv, other)
-
-    def finish(c, ks, hi, pieces, mixes, prior):
+            in_specs=qkv_in + [whole(each, inner)] * len(held),
+            out_specs=[whole(size, inner) for size in sizes],
+            out_shape=[jax.ShapeDtypeStruct((size, inner), bf) for size in sizes],
+        )(q, kv, other, *held)
+
+    def finish(items, hi, pieces, mixes, prior):
         extra_specs, extra = [], []
         if prior is not None:
             extra_specs, extra = [pl.BlockSpec(memory_space=pl.ANY)], [prior]
         return call(
-            functools.partial(finish_kernel, c, ks, high),
-            work // 2,
+            functools.partial(finish_kernel, items, len(mixes), high),
+            work * len(items) // high,
             in_specs=[SMEM, pick(1, (inner, feat))]
-            + [whole(each, feat)] * len(ks)
-            + [whole(each, inner)] * len(ks)
+            + [whole(each, feat)] * len(items)
+            + [whole(*mix.shape) for mix in mixes]
             + extra_specs,
             out_specs=HBM,
             out_shape=jax.ShapeDtypeStruct((rows, cols, feat), bf),
             scratch_shapes=[
-                pltpu.VMEM((len(ks), rows, COLB, feat), bf),
-                pltpu.SemaphoreType.DMA((len(ks),)),
+                pltpu.VMEM((len(items), rows, COLB, feat), bf),
+                pltpu.SemaphoreType.DMA((len(items),)),
             ],
-            input_output_aliases={2 * len(ks) + 2: 0} if extra else {},
+            input_output_aliases={len(items) + len(mixes) + 2: 0} if extra else {},
         )(hi, out_weights, *pieces, *mixes, *extra)
 
     def swap(a):
@@ -387,7 +396,7 @@
     q0, q1, kv1 = second(first, xs[1], gain, weight)
     others.append(swap(kv1))
     queries, keys = [q0, q1], [kv, kv1]
-    pieces, arrived, home = [], [], []
+    pieces, arrived = [], []
     last = q1
     for c in range(CHUNKS):
         made, got = {}, {}
@@ -402,27 +411,27 @@
             got.update(exchange(ready, ks))
         pieces.append(made)
         arrived.append(got)
-    mixes = None
+    held, home = [], []
     for c in range(CHUNKS):
         got = [arrived[c][k] for k in range(high)]
         q, kv = time_project(after(got, last))
-        other = swap(kv)
-        if mixes is not None:
-            mixes = after(mixes, q)
-            home[-1].update(exchange(mixes, light))
-        mixes = timed(q, kv, other)
-        last = mixes[0]
+        mixes = timed(q, kv, swap(kv), held)
+        last = mixes[-1]
         home.append(exchange(mixes, heavy))
+        held = mixes[:half]
         if c + 1 < CHUNKS:
             hi = gate(after(hi, last))
             last = hi
-    home[-1].update(exchange(mixes, light))
-    out = None
-    for c in range(CHUNKS):
-        for ks in (light, heavy):
-            made = after([pieces[c][k] for k in ks], last)
-            mixes = [home[c][k] for k in ks]
-            out = finish(c, ks, hi, made, mixes, out)
+    shared = exchange(held, light)
+
+    def close(items, mixes, prior):
+        made = after([pieces[c][k] for c, k in items], last)
+        return finish(items, hi, made, mixes, prior)
+
+    out = close([(0, k) for k in heavy], [home[0][k] for k in heavy], None)
+    items = [(c, k) for k in light for c in range(CHUNKS)]
+    out = close(items, [shared[k] for k in light], out)
+    out = close([(1, k) for k in heavy], [home[1][k] for k in heavy], out)
     return out[None]
 
 

time: 86 us -> 87.9 us (1.022)
  the two profiles are of different devices: /device:TPU:0 before, /device:TPU:1 now
where the time goes in v4:
time: 87.9 us; the launch traced here: 87.6 us
  waiting for transfers between devices  32.8 us (37%)
  starting transfers between devices  30.1 us (34%)
  Pallas kernels  24.4 us (28%)
    ppermute x14, waiting for transfers between devices, permute(): return lax.ppermute(piece, ('tm', 'space'), route(k))  30.9 us
    ppermute x14, starting transfers between devices, permute(): return lax.ppermute(piece, ('tm', 'space'), route(k))  28.2 us
    pallas_call x4, Pallas kernels, height(): call(functools.partial(height_kernel, ks), 2 * work, in_specs=[SMEM, whol...  6.7 us
    pallas_call x3, Pallas kernels, finish(): call(functools.partial(finish_kernel, items, len(mixes), high), work * le...  5.55 us
    pallas_call x1, Pallas kernels, load(): call(load_kernel, 2 * work, in_specs=[HBM, HBM, HBM], out_specs=[whole(*s...  3.73 us
    pallas_call x2, Pallas kernels, time_project(): call(time_project_kernel, 3 * work, in_specs=[whole(each, feat)] * high +...  3.08 us
    pallas_call x2, Pallas kernels, timed(): call(functools.partial(time_kernel, len(held)), 2 * work, in_specs=qkv_in...  2.82 us
    pallas_call x1, Pallas kernels, second(): call(second_kernel, 4 * work, in_specs=[whole(count, feat), whole(*tile),...  1.95 us
  transfers between devices with their start and end apart: 18, of which 8 were waited for; matrix products, arithmetic and copies ran while one was open for 0% of the time, Pallas kernels for 16%

profile of v4, /device:TPU:1, one launch (start us, length us, event | category | flops | bytes accessed | tf_op | source)
XLA Modules:
  0.0 87.6 jit_solution(6253694319863030581)
XLA Ops:
  0.0 3.7 %shard_map.46 = (bf16[384,1024]{1,0:T(8,128)(2,1)S(1)}, bf16[384,1024]{1,0:T(8,128)(2,1)S(1)}, bf16[1024,1536]{1,0:T(8,128)(2,1)S(1)}, f32[2,1024]{1,0:T(2,128)S...) custom-call(bf16[12,64,1024]{2,1,0:T(8,128)(2,1)} %bitcast.5, f32[2,1024]{1,0:T(2,128)} %refs_4_.3, ...), custom_call_target="tpu_custom_call" | custom-call | flops 805306368 | bytes 1572864 | tf_op jit(solution)/shard_map/pallas_call | solution.py:281
  3.8 2.0 %shard_map.47 = (bf16[384,512]{1,0:T(8,128)(2,1)S(1)}, bf16[384,512]{1,0:T(8,128)(2,1)S(1)}, bf16[384,1024]{1,0:T(8,128)(2,1)S(1)}) custom-call(bf16[384,1024]{1,0:T(8,128)(2,1)S(1)} %get-tuple-element.59.first_ref, bf16[4,12,8,1024]{3,2,1,0:T(8,128)(2,1)S(1)} %get-tuple-element.60.x_ref, f32[2,1024]{1,0:T(2,128)S(1)} %get-tuple-element.61.gain_ref, ...), custom_call_target="tpu_custom_call" | custom-call | flops 1610612736 | bytes 1572864 | tf_op jit(solution)/shard_map/pallas_call | solution.py:295
  6.3 1.6 %shard_map.48 = (bf16[96,1024]{1,0:T(8,128)(2,1)S(1)}, bf16[96,1024]{1,0:T(8,128)(2,1)S(1)}) custom-call(s32[1]{0:T(128)} %bitcast.hi_ref.in_ref, bf16[4,12,8,1024]{3,2,1,0:T(8,128)(2,1)S(1)} %get-tuple-element.58.x_ref, bf16[384,512]{1,0:T(8,128)(2,1)S(1)} %get-tuple-element.68.q_ref, bf16[384,1024]{1,0:T(8,128)(2,1)S(1)} %get-tuple-element.66.kv_ref, ...), custom_call_target="tpu_custom_call" | custom-call | flops 805306368 | bytes 1572864 | tf_op jit(solution)/shard_map/pallas_call | solution.py:309
  8.0 1.8 %shard_map.49 = (bf16[96,1024]{1,0:T(8,128)(2,1)S(1)}, bf16[96,1024]{1,0:T(8,128)(2,1)S(1)}) custom-call(s32[1]{0:T(128)} %bitcast.hi_ref.in_ref, bf16[4,12,8,1024]{3,2,1,0:T(8,128)(2,1)S(1)} %get-tuple-element.58.x_ref, bf16[384,512]{1,0:T(8,128)(2,1)S(1)} %get-tuple-element.68.q_ref, bf16[384,1024]{1,0:T(8,128)(2,1)S(1)} %get-tuple-element.66.kv_ref, ...), custom_call_target="tpu_custom_call" | custom-call | flops 805306368 | bytes 1572864 | tf_op jit(solution)/shard_map/pallas_call | solution.py:309
  9.8 4.5 %collective-permute-start.1 = (bf16[96,1024]{1,0:T(8,128)(2,1)S(1)}, bf16[96,1024]{1,0:T(8,128)(2,1)S(1)}, u32[]{:S(2)}, u32[]{:S(2)}) collective-permute-start(bf16[96,1024]{1,0:T(8,128)(2,1)S(1)} %get-tuple-element.102.refs_2_), channel_id=1, source_target_pairs={{0,0},{1,2},{2,1},{3,3},{4,4},{5,6},{6,5},{7,7},{8,11},{9,9},{10,1... | collective-permute-start | bytes 589832 | tf_op jit(solution)/shard_map/ppermute | solution.py:386
  15.5 2.7 %collective-permute-start.3 = (bf16[96,1024]{1,0:T(8,128)(2,1)S(1)}, bf16[96,1024]{1,0:T(8,128)(2,1)S(1)}, u32[]{:S(2)}, u32[]{:S(2)}) collective-permute-start(bf16[96,1024]{1,0:T(8,128)(2,1)S(1)} %get-tuple-element.107.refs_1_), channel_id=1, source_target_pairs={{0,10},{1,8},{2,11},{3,9},{4,14},{5,12},{6,15},{7,13},{8,1},{9,3},... | collective-permute-start | bytes 589832 | tf_op jit(solution)/shard_map/ppermute | solution.py:386
  18.2 1.6 %shard_map.50 = (bf16[96,1024]{1,0:T(8,128)(2,1)S(1)}, bf16[96,1024]{1,0:T(8,128)(2,1)S(1)}) custom-call(s32[1]{0:T(128)} %bitcast.hi_ref.in_ref, bf16[4,12,8,1024]{3,2,1,0:T(8,128)(2,1)S(1)} %get-tuple-element.60.x_ref, bf16[384,512]{1,0:T(8,128)(2,1)S(1)} %get-tuple-element.75.q_ref, bf16[384,1024]{1,0:T(8,128)(2,1)S(1)} %get-tuple-element.73.kv_ref, ...), custom_call_target="tpu_custom_call" | custom-call | flops 805306368 | bytes 1572864 | tf_op jit(solution)/shard_map/pallas_call | solution.py:309
  19.9 1.6 %shard_map.51 = (bf16[96,1024]{1,0:T(8,128)(2,1)S(1)}, bf16[96,1024]{1,0:T(8,128)(2,1)S(1)}) custom-call(s32[1]{0:T(128)} %bitcast.hi_ref.in_ref, bf16[4,12,8,1024]{3,2,1,0:T(8,128)(2,1)S(1)} %get-tuple-element.60.x_ref, bf16[384,512]{1,0:T(8,128)(2,1)S(1)} %get-tuple-element.75.q_ref, bf16[384,1024]{1,0:T(8,128)(2,1)S(1)} %get-tuple-element.73.kv_ref, ...), custom_call_target="tpu_custom_call" | custom-call | flops 805306368 | bytes 1572864 | tf_op jit(solution)/shard_map/pallas_call | solution.py:309
  21.5 1.7 %collective-permute-done.2.refs_1_ = bf16[96,1024]{1,0:T(8,128)(2,1)S(1)} collective-permute-done((bf16[96,1024]{1,0:T(8,128)(2,1)S(1)}, bf16[96,1024]{1,0:T(8,128)(2,1)S(1)}, u32[]{:S(2)}, u32[]{:S(2)}) %collective-permute-start.2) | collective-permute-done | bytes 196640 | tf_op jit(solution)/shard_map/ppermute | solution.py:386
  23.3 7.6 %collective-permute-done.3.refs_2_ = bf16[96,1024]{1,0:T(8,128)(2,1)S(1)} collective-permute-done((bf16[96,1024]{1,0:T(8,128)(2,1)S(1)}, bf16[96,1024]{1,0:T(8,128)(2,1)S(1)}, u32[]{:S(2)}, u32[]{:S(2)}) %collective-permute-start.3) | collective-permute-done | bytes 196640 | tf_op jit(solution)/shard_map/ppermute | solution.py:386
  30.9 1.5 %shard_map.52 = (bf16[384,512]{1,0:T(8,128)(2,1)S(1)}, bf16[384,1024]{1,0:T(8,128)(2,1)S(1)}) custom-call(bf16[96,1024]{1,0:T(8,128)(2,1)S(1)} %collective-permute-done.1.refs_0_, bf16[96,1024]{1,0:T(8,128)(2,1)S(1)} %collective-permute-done.2.refs_1_, bf16[96,1024]{1,0:T(8,128)(2,1)S(1)} %collective-permute-done.3.refs_2_, ...), custom_call_target="tpu_custom_call" | custom-call | flops 1207959552 | bytes 1572864 | tf_op jit(solution)/shard_map/pallas_call | solution.py:334
  32.6 5.2 %collective-permute-start.8 = (bf16[96,1024]{1,0:T(8,128)(2,1)S(1)}, bf16[96,1024]{1,0:T(8,128)(2,1)S(1)}, u32[]{:S(2)}, u32[]{:S(2)}) collective-permute-start(bf16[96,1024]{1,0:T(8,128)(2,1)S(1)} %get-tuple-element.101.refs_1_), channel_id=1, source_target_pairs={{0,4},{1,6},{2,5},{3,7},{4,0},{5,2},{6,1},{7,3},{8,15},{9,13},{10,... | collective-permute-start | bytes 589832 | tf_op jit(solution)/shard_map/ppermute | solution.py:386
  37.8 2.5 %collective-permute-start.10 = (bf16[96,1024]{1,0:T(8,128)(2,1)S(1)}, bf16[96,1024]{1,0:T(8,128)(2,1)S(1)}, u32[]{:S(2)}, u32[]{:S(2)}) collective-permute-start(bf16[96,1024]{1,0:T(8,128)(2,1)S(1)} %get-tuple-element.97.refs_0_), channel_id=1, source_target_pairs={{0,14},{1,12},{2,15},{3,13},{4,10},{5,8},{6,11},{7,9},{8,5},{9,7},... | collective-permute-start | bytes 589832 | tf_op jit(solution)/shard_map/ppermute | solution.py:386
  40.2 3.3 %collective-permute-start.7 = (bf16[96,1024]{1,0:T(8,128)(2,1)S(1)}, bf16[96,1024]{1,0:T(8,128)(2,1)S(1)}, u32[]{:S(2)}, u32[]{:S(2)}) collective-permute-start(bf16[96,1024]{1,0:T(8,128)(2,1)S(1)} %get-tuple-element.103.refs_3_), channel_id=1, source_target_pairs={{0,0},{1,2},{2,1},{3,3},{4,4},{5,6},{6,5},{7,7},{8,11},{9,9},{10,1... | collective-permute-start | bytes 589832 | tf_op jit(solution)/shard_map/ppermute | solution.py:386
  45.5 4.0 %collective-permute-done.7.refs_0_ = bf16[96,1024]{1,0:T(8,128)(2,1)S(1)} collective-permute-done((bf16[96,1024]{1,0:T(8,128)(2,1)S(1)}, bf16[96,1024]{1,0:T(8,128)(2,1)S(1)}, u32[]{:S(2)}, u32[]{:S(2)}) %collective-permute-start.7) | collective-permute-done | bytes 196640 | tf_op jit(solution)/shard_map/ppermute | solution.py:386
  50.2 7.5 %collective-permute-done.9.refs_2_ = bf16[96,1024]{1,0:T(8,128)(2,1)S(1)} collective-permute-done((bf16[96,1024]{1,0:T(8,128)(2,1)S(1)}, bf16[96,1024]{1,0:T(8,128)(2,1)S(1)}, u32[]{:S(2)}, u32[]{:S(2)}) %collective-permute-start.9) | collective-permute-done | bytes 196640 | tf_op jit(solution)/shard_map/ppermute | solution.py:386
  60.5 1.9 %collective-permute-done.11.other_ref = bf16[384,1024]{1,0:T(8,128)(2,1)S(1)} collective-permute-done((bf16[384,1024]{1,0:T(8,128)(2,1)S(1)}, bf16[384,1024]{1,0:T(8,128)(2,1)S(1)}, u32[]{:S(2)}, u32[]{:S(2)}) %collective-permute-start.11) | collective-permute-done | bytes 786464 | tf_op jit(solution)/shard_map/ppermute | solution.py:373
  63.9 2.5 %collective-permute-start.15 = (bf16[192,512]{1,0:T(8,128)(2,1)S(1)}, bf16[192,512]{1,0:T(8,128)(2,1)S(1)}, u32[]{:S(2)}, u32[]{:S(2)}) collective-permute-start(bf16[192,512]{1,0:T(8,128)(2,1)S(1)} %get-tuple-element.105), channel_id=1, source_target_pairs={{0,0},{1,2},{2,1},{3,3},{4,4},{5,6},{6,5},{7,7},{8,11},{9,9},{10,1... | collective-permute-start | bytes 589832 | tf_op jit(solution)/shard_map/ppermute | solution.py:386
  66.5 2.2 %collective-permute-start.17 = (bf16[96,512]{1,0:T(8,128)(2,1)S(1)}, bf16[96,512]{1,0:T(8,128)(2,1)S(1)}, u32[]{:S(2)}, u32[]{:S(2)}) collective-permute-start(bf16[96,512]{1,0:T(8,128)(2,1)S(1)} %get-tuple-element.108), channel_id=1, source_target_pairs={{0,10},{1,8},{2,11},{3,9},{4,14},{5,12},{6,15},{7,13},{8,1},{9,3},... | collective-permute-start | bytes 294920 | tf_op jit(solution)/shard_map/ppermute | solution.py:386
  68.6 2.5 %collective-permute-start.16 = (bf16[96,512]{1,0:T(8,128)(2,1)S(1)}, bf16[96,512]{1,0:T(8,128)(2,1)S(1)}, u32[]{:S(2)}, u32[]{:S(2)}) collective-permute-start(bf16[96,512]{1,0:T(8,128)(2,1)S(1)} %get-tuple-element.83), channel_id=1, source_target_pairs={{0,14},{1,12},{2,15},{3,13},{4,10},{5,8},{6,11},{7,9},{8,5},{9,7},... | collective-permute-start | bytes 294920 | tf_op jit(solution)/shard_map/ppermute | solution.py:386
  71.2 8.7 %collective-permute-done.17.refs_3_ = bf16[96,512]{1,0:T(8,128)(2,1)S(1)} collective-permute-done((bf16[96,512]{1,0:T(8,128)(2,1)S(1)}, bf16[96,512]{1,0:T(8,128)(2,1)S(1)}, u32[]{:S(2)}, u32[]{:S(2)}) %collective-permute-start.17) | collective-permute-done | bytes 98336 | tf_op jit(solution)/shard_map/ppermute | solution.py:386
  81.4 1.7 %shard_map.56.refs_6_ = bf16[12,64,1024]{2,1,0:T(8,128)(2,1)} custom-call(s32[1]{0:T(128)} %gate.1.hi_ref, bf16[2,512,1024]{2,1,0:T(8,128)(2,1)S(1)} %copy-done, bf16[96,1024]{1,0:T(8,128)(2,1)S(1)} %get-tuple-element.106.refs_0_, bf16[96,1024]{1,0:T(8,128)(2,1)S(1)} %get-tuple-element.107.refs_1_, bf16[96,512]{1,0:T(8,128)(2,1)S(1)} %collective-permute-done.16.refs_2_, ...), custom_call_target="tpu_custom_call" | custom-call | flops 201326592 | bytes 1572864 | tf_op jit(solution)/shard_map/pallas_call | solution.py:356
  83.2 2.1 %shard_map.57.refs_4_ = bf16[12,64,1024]{2,1,0:T(8,128)(2,1)} custom-call(s32[1]{0:T(128)} %gate.1.hi_ref, bf16[2,512,1024]{2,1,0:T(8,128)(2,1)S(1)} %copy-done, bf16[96,1024]{1,0:T(8,128)(2,1)S(1)} %get-tuple-element.100.refs_0_, bf16[96,1024]{1,0:T(8,128)(2,1)S(1)} %get-tuple-element.101.refs_1_, ...), custom_call_target="tpu_custom_call", output_to_operand_aliasing={{}: (8, {})} | custom-call | flops 402653184 | bytes 1572864 | tf_op jit(solution)/shard_map/pallas_call | solution.py:356
  85.7 1.7 %shard_map.58 = bf16[12,64,1024]{2,1,0:T(8,128)(2,1)} custom-call(s32[1]{0:T(128)} %gate.1.hi_ref, bf16[2,512,1024]{2,1,0:T(8,128)(2,1)S(1)} %copy-done, bf16[96,1024]{1,0:T(8,128)(2,1)S(1)} %get-tuple-element.97.refs_0_, bf16[96,1024]{1,0:T(8,128)(2,1)S(1)} %get-tuple-element.98.refs_1_, ...), custom_call_target="tpu_custom_call", output_to_operand_aliasing={{}: (6, {})} | custom-call | flops 201326592 | bytes 1572864 | tf_op jit(solution)/shard_map/pallas_call | solution.py:356
  (35 shorter events, 10.9 us)
Async XLA Ops:
  3.7 2.6 %collective-permute-start = (bf16[384,1024]{1,0:T(8,128)(2,1)S(1)}, bf16[384,1024]{1,0:T(8,128)(2,1)S(1)}, u32[]{:S(2)}, u32[]{:S(2)}) collective-permute-start(bf16[384,1024]{1,0:T(8,128)(2,1)S(1)} %get-tuple-element.66.kv_ref), channel_id=1, source_target_pairs={{0,1},{1,0},{2,3},{3,2},{4,5},{5,4},{6,7},{7,6},{8,9},{9,8},{10,11... | collective-permute-start | bytes 2359304 | tf_op jit(solution)/shard_map/ppermute | solution.py:373
  5.8 12.5 %collective-permute-start.5 = (bf16[384,1024]{1,0:T(8,128)(2,1)S(1)}, bf16[384,1024]{1,0:T(8,128)(2,1)S(1)}, u32[]{:S(2)}, u32[]{:S(2)}) collective-permute-start(bf16[384,1024]{1,0:T(8,128)(2,1)S(1)} %get-tuple-element.73.kv_ref), channel_id=1, source_target_pairs={{0,1},{1,0},{2,3},{3,2},{4,5},{5,4},{6,7},{7,6},{8,9},{9,8},{10,11... | collective-permute-start | bytes 2359304 | tf_op jit(solution)/shard_map/ppermute | solution.py:373
  8.0 22.9 %slice-start = ((s8[6291456]{0:T(1024)(128)(4,1)}), s8[4194304]{0:T(1024)(128)(4,1)S(1)}, s32[]{:S(2)}) async-start(s8[6291456]{0:T(1024)(128)(4,1)} %bitcast.3), calls=%async_computation | async-start | bytes 8388608
  9.8 11.7 %collective-permute-start.1 = (bf16[96,1024]{1,0:T(8,128)(2,1)S(1)}, bf16[96,1024]{1,0:T(8,128)(2,1)S(1)}, u32[]{:S(2)}, u32[]{:S(2)}) collective-permute-start(bf16[96,1024]{1,0:T(8,128)(2,1)S(1)} %get-tuple-element.102.refs_2_), channel_id=1, source_target_pairs={{0,0},{1,2},{2,1},{3,3},{4,4},{5,6},{6,5},{7,7},{8,11},{9,9},{10,1... | collective-permute-start | bytes 589832 | tf_op jit(solution)/shard_map/ppermute | solution.py:386
  14.3 9.0 %collective-permute-start.2 = (bf16[96,1024]{1,0:T(8,128)(2,1)S(1)}, bf16[96,1024]{1,0:T(8,128)(2,1)S(1)}, u32[]{:S(2)}, u32[]{:S(2)}) collective-permute-start(bf16[96,1024]{1,0:T(8,128)(2,1)S(1)} %get-tuple-element.100.refs_0_), channel_id=1, source_target_pairs={{0,4},{1,6},{2,5},{3,7},{4,0},{5,2},{6,1},{7,3},{8,15},{9,13},{10,... | collective-permute-start | bytes 589832 | tf_op jit(solution)/shard_map/ppermute | solution.py:386
  15.5 15.4 %slice-start.1 = ((s8[6291456]{0:T(1024)(128)(4,1)}), s8[2097152]{0:T(1024)(128)(4,1)S(1)}, s32[]{:S(2)}) async-start(s8[6291456]{0:T(1024)(128)(4,1)} %bitcast.3), calls=%async_computation.1 | async-start | bytes 4194304
  15.5 15.4 %collective-permute-start.3 = (bf16[96,1024]{1,0:T(8,128)(2,1)S(1)}, bf16[96,1024]{1,0:T(8,128)(2,1)S(1)}, u32[]{:S(2)}, u32[]{:S(2)}) collective-permute-start(bf16[96,1024]{1,0:T(8,128)(2,1)S(1)} %get-tuple-element.107.refs_1_), channel_id=1, source_target_pairs={{0,10},{1,8},{2,11},{3,9},{4,14},{5,12},{6,15},{7,13},{8,1},{9,3},... | collective-permute-start | bytes 589832 | tf_op jit(solution)/shard_map/ppermute | solution.py:386
  18.2 12.7 %collective-permute-start.4 = (bf16[96,1024]{1,0:T(8,128)(2,1)S(1)}, bf16[96,1024]{1,0:T(8,128)(2,1)S(1)}, u32[]{:S(2)}, u32[]{:S(2)}) collective-permute-start(bf16[96,1024]{1,0:T(8,128)(2,1)S(1)} %get-tuple-element.106.refs_0_), channel_id=1, source_target_pairs={{0,14},{1,12},{2,15},{3,13},{4,10},{5,8},{6,11},{7,9},{8,5},{9,7},... | collective-permute-start | bytes 589832 | tf_op jit(solution)/shard_map/ppermute | solution.py:386
  19.9 11.1 %copy-start.1 = (f32[2,1024]{1,0:T(2,128)S(1)}, f32[2,1024]{1,0:T(2,128)}, u32[]{:S(2)}) copy-start(f32[2,1024]{1,0:T(2,128)} %refs_4_.3) | copy-start | bytes 24580
  32.5 11.1 %collective-permute-start.6 = (bf16[384,1024]{1,0:T(8,128)(2,1)S(1)}, bf16[384,1024]{1,0:T(8,128)(2,1)S(1)}, u32[]{:S(2)}, u32[]{:S(2)}) collective-permute-start(bf16[384,1024]{1,0:T(8,128)(2,1)S(1)} %get-tuple-element.82.kv_ref), channel_id=1, source_target_pairs={{0,1},{1,0},{2,3},{3,2},{4,5},{5,4},{6,7},{7,6},{8,9},{9,8},{10,11... | collective-permute-start | bytes 2359304 | tf_op jit(solution)/shard_map/ppermute | solution.py:373
  32.6 16.9 %collective-permute-start.8 = (bf16[96,1024]{1,0:T(8,128)(2,1)S(1)}, bf16[96,1024]{1,0:T(8,128)(2,1)S(1)}, u32[]{:S(2)}, u32[]{:S(2)}) collective-permute-start(bf16[96,1024]{1,0:T(8,128)(2,1)S(1)} %get-tuple-element.101.refs_1_), channel_id=1, source_target_pairs={{0,4},{1,6},{2,5},{3,7},{4,0},{5,2},{6,1},{7,3},{8,15},{9,13},{10,... | collective-permute-start | bytes 589832 | tf_op jit(solution)/shard_map/ppermute | solution.py:386
  37.8 12.5 %collective-permute-start.10 = (bf16[96,1024]{1,0:T(8,128)(2,1)S(1)}, bf16[96,1024]{1,0:T(8,128)(2,1)S(1)}, u32[]{:S(2)}, u32[]{:S(2)}) collective-permute-start(bf16[96,1024]{1,0:T(8,128)(2,1)S(1)} %get-tuple-element.97.refs_0_), channel_id=1, source_target_pairs={{0,14},{1,12},{2,15},{3,13},{4,10},{5,8},{6,11},{7,9},{8,5},{9,7},... | collective-permute-start | bytes 589832 | tf_op jit(solution)/shard_map/ppermute | solution.py:386
  40.2 9.3 %collective-permute-start.7 = (bf16[96,1024]{1,0:T(8,128)(2,1)S(1)}, bf16[96,1024]{1,0:T(8,128)(2,1)S(1)}, u32[]{:S(2)}, u32[]{:S(2)}) collective-permute-start(bf16[96,1024]{1,0:T(8,128)(2,1)S(1)} %get-tuple-element.103.refs_3_), channel_id=1, source_target_pairs={{0,0},{1,2},{2,1},{3,3},{4,4},{5,6},{6,5},{7,7},{8,11},{9,9},{10,1... | collective-permute-start | bytes 589832 | tf_op jit(solution)/shard_map/ppermute | solution.py:386
  43.5 14.3 %collective-permute-start.9 = (bf16[96,1024]{1,0:T(8,128)(2,1)S(1)}, bf16[96,1024]{1,0:T(8,128)(2,1)S(1)}, u32[]{:S(2)}, u32[]{:S(2)}) collective-permute-start(bf16[96,1024]{1,0:T(8,128)(2,1)S(1)} %get-tuple-element.98.refs_1_), channel_id=1, source_target_pairs={{0,10},{1,8},{2,11},{3,9},{4,14},{5,12},{6,15},{7,13},{8,1},{9,3},... | collective-permute-start | bytes 589832 | tf_op jit(solution)/shard_map/ppermute | solution.py:386
  59.3 22.1 %copy-start = (bf16[2,512,1024]{2,1,0:T(8,128)(2,1)S(1)}, bf16[2,512,1024]{2,1,0:T(8,128)(2,1)}, u32[]{:S(2)}) copy-start(bf16[2,512,1024]{2,1,0:T(8,128)(2,1)} %w_ref.15) | copy-start | bytes 6291460
  59.3 3.1 %collective-permute-start.11 = (bf16[384,1024]{1,0:T(8,128)(2,1)S(1)}, bf16[384,1024]{1,0:T(8,128)(2,1)S(1)}, u32[]{:S(2)}, u32[]{:S(2)}) collective-permute-start(bf16[384,1024]{1,0:T(8,128)(2,1)S(1)} %get-tuple-element.93.kv_ref), channel_id=1, source_target_pairs={{0,1},{1,0},{2,3},{3,2},{4,5},{5,4},{6,7},{7,6},{8,9},{9,8},{10,11... | collective-permute-start | bytes 2359304 | tf_op jit(solution)/shard_map/ppermute | solution.py:373
  63.8 19.3 %collective-permute-start.14 = (bf16[192,512]{1,0:T(8,128)(2,1)S(1)}, bf16[192,512]{1,0:T(8,128)(2,1)S(1)}, u32[]{:S(2)}, u32[]{:S(2)}) collective-permute-start(bf16[192,512]{1,0:T(8,128)(2,1)S(1)} %get-tuple-element.104), channel_id=1, source_target_pairs={{0,4},{1,6},{2,5},{3,7},{4,0},{5,2},{6,1},{7,3},{8,15},{9,13},{10,... | collective-permute-start | bytes 589832 | tf_op jit(solution)/shard_map/ppermute | solution.py:386
  63.9 19.2 %collective-permute-start.15 = (bf16[192,512]{1,0:T(8,128)(2,1)S(1)}, bf16[192,512]{1,0:T(8,128)(2,1)S(1)}, u32[]{:S(2)}, u32[]{:S(2)}) collective-permute-start(bf16[192,512]{1,0:T(8,128)(2,1)S(1)} %get-tuple-element.105), channel_id=1, source_target_pairs={{0,0},{1,2},{2,1},{3,3},{4,4},{5,6},{6,5},{7,7},{8,11},{9,9},{10,1... | collective-permute-start | bytes 589832 | tf_op jit(solution)/shard_map/ppermute | solution.py:386
  66.5 13.4 %collective-permute-start.17 = (bf16[96,512]{1,0:T(8,128)(2,1)S(1)}, bf16[96,512]{1,0:T(8,128)(2,1)S(1)}, u32[]{:S(2)}, u32[]{:S(2)}) collective-permute-start(bf16[96,512]{1,0:T(8,128)(2,1)S(1)} %get-tuple-element.108), channel_id=1, source_target_pairs={{0,10},{1,8},{2,11},{3,9},{4,14},{5,12},{6,15},{7,13},{8,1},{9,3},... | collective-permute-start | bytes 294920 | tf_op jit(solution)/shard_map/ppermute | solution.py:386
  68.6 12.8 %collective-permute-start.16 = (bf16[96,512]{1,0:T(8,128)(2,1)S(1)}, bf16[96,512]{1,0:T(8,128)(2,1)S(1)}, u32[]{:S(2)}, u32[]{:S(2)}) collective-permute-start(bf16[96,512]{1,0:T(8,128)(2,1)S(1)} %get-tuple-element.83), channel_id=1, source_target_pairs={{0,14},{1,12},{2,15},{3,13},{4,10},{5,8},{6,11},{7,9},{8,5},{9,7},... | collective-permute-start | bytes 294920 | tf_op jit(solution)/shard_map/ppermute | solution.py:386
  71.2 14.1 %collective-permute-start.13 = (bf16[96,512]{1,0:T(8,128)(2,1)S(1)}, bf16[96,512]{1,0:T(8,128)(2,1)S(1)}, u32[]{:S(2)}, u32[]{:S(2)}) collective-permute-start(bf16[96,512]{1,0:T(8,128)(2,1)S(1)} %get-tuple-element.99), channel_id=1, source_target_pairs={{0,10},{1,8},{2,11},{3,9},{4,14},{5,12},{6,15},{7,13},{8,1},{9,3},... | collective-permute-start | bytes 294920 | tf_op jit(solution)/shard_map/ppermute | solution.py:386
  79.9 5.8 %collective-permute-start.12 = (bf16[96,512]{1,0:T(8,128)(2,1)S(1)}, bf16[96,512]{1,0:T(8,128)(2,1)S(1)}, u32[]{:S(2)}, u32[]{:S(2)}) collective-permute-start(bf16[96,512]{1,0:T(8,128)(2,1)S(1)} %get-tuple-element.96), channel_id=1, source_target_pairs={{0,14},{1,12},{2,15},{3,13},{4,10},{5,8},{6,11},{7,9},{8,5},{9,7},... | collective-permute-start | bytes 294920 | tf_op jit(solution)/shard_map/ppermute | solution.py:386

commit v5 on v4

v5 whole, which is shorter than its diff:
```python
import functools

import jax
import jax.numpy as jnp
from jax import lax
from jax.experimental import pallas as pl
from jax.experimental.pallas import tpu as pltpu
from jax.sharding import PartitionSpec as P


HEAD = 64
EPS = 1e-06
QUAD = 4
CHUNKS = 2
COLB = 8
SPLIT = 2
LATE = ()
POSB = 16
NEG = -1e30
VMEM_BYTES = 16 * 1024 * 1024


def params():
    return pltpu.CompilerParams(vmem_limit_bytes=VMEM_BYTES)


def normalise(stream, gain):
    scale = lax.rsqrt(jnp.mean(stream * stream, axis=-1, keepdims=True) + EPS)
    return (stream * scale * gain).astype(jnp.bfloat16)


def group_bias(keys, group):
    left = lax.broadcasted_iota(jnp.int32, (1, group, keys), 1)
    right = lax.broadcasted_iota(jnp.int32, (1, group, keys), 2) % group
    return jnp.where(left == right, 0.0, NEG)


def attend_quad(query, key, value, bias):
    rows, width = query.shape
    keys = key.shape[0]
    lanes = lax.broadcasted_iota(jnp.int32, (rows, width), 1) // HEAD
    heads = width // HEAD
    zero = jnp.zeros_like(query)
    stacked = jnp.concatenate([jnp.where(lanes == h, query, zero) for h in range(heads)], axis=0)
    scores = lax.dot_general(
        stacked, key, (((1,), (1,)), ((), ())), preferred_element_type=jnp.float32
    )
    scores = scores.reshape(heads * rows // bias.shape[1], bias.shape[1], keys) + bias
    raised = jnp.exp(scores - jnp.max(scores, axis=-1, keepdims=True))
    total = jnp.sum(raised, axis=-1, keepdims=True).reshape(heads * rows, 1)
    raised = raised.reshape(heads * rows, keys).astype(jnp.bfloat16)
    mixed = jnp.dot(raised, value, preferred_element_type=jnp.float32) * (1.0 / total)
    out = mixed[:rows]
    for h in range(1, heads):
        out = jnp.where(lanes == h, mixed[h * rows : (h + 1) * rows], out)
    return out.astype(jnp.bfloat16)


def join(parts):
    return parts[0] if len(parts) == 1 else jnp.concatenate(parts, axis=0)


def project_keys(normed, w_ref, kv_ref):
    inner = kv_ref.shape[1] // 2
    kv_ref[...] = jnp.dot(
        normed, w_ref[:, inner:], preferred_element_type=jnp.float32
    ).astype(jnp.bfloat16)


def project_queries(normed, w_ref, q_ref):
    q_ref[...] = jnp.dot(
        normed, w_ref[:, : q_ref.shape[1]], preferred_element_type=jnp.float32
    ).astype(jnp.bfloat16) * jnp.bfloat16(HEAD**-0.5)


def position():
    return lax.axis_index("tm") // 2


def load_kernel(order, x_ref, gain_ref, w_ref, kv_ref, normed_ref, w_out, gain_out, *refs):
    x_outs, (x_sem, w_sem, gain_sem) = refs[:CHUNKS], refs[CHUNKS:]
    blocks, rows, colb, feat = x_outs[0].shape
    inner = kv_ref.shape[1] // 2
    per = rows * colb
    first = kv_ref.shape[0] // per
    loads = []
    for c in range(CHUNKS):
        for i, k in enumerate(order):
            column = pl.multiple_of((c * blocks + jnp.bitwise_xor(position(), k)) * colb, colb)
            loads.append(
                pltpu.make_async_copy(
                    x_ref.at[:, pl.ds(column, colb), :], x_outs[c].at[i], x_sem.at[c * blocks + i]
                )
            )
    step = feat // SPLIT
    fetches = [
        pltpu.make_async_copy(
            w_ref.at[0, pl.ds(i * step, step), :], w_out.at[pl.ds(i * step, step), :], w_sem.at[i]
        )
        for i in range(SPLIT)
    ]
    gain_load = pltpu.make_async_copy(gain_ref, gain_out, gain_sem)
    for copy in [gain_load] + loads[:first] + fetches + loads[first:]:
        copy.start()
    gain_load.wait()
    for i in range(first):
        loads[i].wait()
        stream = x_outs[0][i].astype(jnp.float32).reshape(per, feat)
        normed_ref[i * per : (i + 1) * per, :] = normalise(stream, gain_out[0:1, :])
    total = None
    for i, fetch in enumerate(fetches):
        fetch.wait()
        span = slice(i * step, (i + 1) * step)
        part = jnp.dot(
            normed_ref[:, span], w_out[span, inner:], preferred_element_type=jnp.float32
        )
        total = part if total is None else total + part
    kv_ref[...] = total.astype(jnp.bfloat16)
    for load in loads[first:]:
        load.wait()


def queries_kernel(normed_ref, w_ref, q_ref):
    project_queries(normed_ref[...], w_ref, q_ref)


def project_kernel(first, x_ref, gain_ref, w_ref, q_ref, kv_ref):
    blocks, rows, colb, feat = x_ref.shape
    stream = x_ref[first:].astype(jnp.float32).reshape((blocks - first) * rows * colb, feat)
    normed = normalise(stream, gain_ref[0:1, :])
    project_keys(normed, w_ref, kv_ref)
    project_queries(normed, w_ref, q_ref)


def height_kernel(tile, start, x_ref, q_ref, kv_ref, other_ref, w_ref, *refs):
    mix_ref, w_buf, w_sem = refs[-3:]
    _, rows, colb, feat = x_ref.shape
    per = rows * colb
    fetch = pltpu.make_async_copy(w_ref.at[0], w_buf, w_sem)
    fetch.start()
    inner = q_ref.shape[1]
    width = QUAD * HEAD
    bias = group_bias(2 * per, colb)
    zero = lax.axis_index("space") // lax.axis_size("space")
    for i in range(len(refs) - 3):
        span = pl.ds(pl.multiple_of((zero + i) * per, per) + start, per)
        for lo in range(0, inner, width):
            here, there = slice(lo, lo + width), slice(inner + lo, inner + lo + width)
            key = join([kv_ref[span, here], other_ref[span, here]])
            value = join([kv_ref[span, there], other_ref[span, there]])
            mix_ref[i * per : (i + 1) * per, here] = attend_quad(
                q_ref[span, here], key, value, bias
            )
    fetch.wait()
    update = jnp.dot(mix_ref[...], w_buf[...], preferred_element_type=jnp.float32)
    for i in range(len(refs) - 3):
        stream = x_ref[tile + i].astype(jnp.float32).reshape(per, feat)
        refs[i][...] = (stream + update[i * per : (i + 1) * per]).astype(jnp.bfloat16)


def time_project_kernel(*refs):
    gain_ref, w_ref, q_ref, kv_ref = refs[-4:]
    normed = join([normalise(ref[...].astype(jnp.float32), gain_ref[1:2, :]) for ref in refs[:-4]])
    project_keys(normed, w_ref, kv_ref)
    project_queries(normed, w_ref, q_ref)


def gate_kernel(in_ref, out_ref):
    out_ref[0] = 0


def time_kernel(groups, *refs):
    count = 3 * len(groups)
    sources, mix_refs = refs[:count], refs[count:]
    each, inner = mix_refs[0].shape
    width = QUAD * HEAD
    bias = group_bias(2 * len(mix_refs) * POSB, POSB)
    flat = [(g, i, k) for g, group in enumerate(groups) for i, k in enumerate(group)]

    def rows(which, p, lo):
        return [
            sources[3 * g + which][i * each + p : i * each + p + POSB, lo : lo + width]
            for g, i, _ in flat
        ]

    for p in range(0, each, POSB):
        for lo in range(0, inner, width):
            key = join(rows(1, p, lo) + rows(2, p, lo))
            value = join(rows(1, p, inner + lo) + rows(2, p, inner + lo))
            out = attend_quad(join(rows(0, p, lo)), key, value, bias)
            for n, (_, _, k) in enumerate(flat):
                mix_refs[k][p : p + POSB, lo : lo + width] = out[n * POSB : (n + 1) * POSB]


def finish_kernel(items, mixed, high, w_ref, *refs):
    pieces, mixes = refs[: len(items)], refs[len(items) : len(items) + mixed]
    out_ref, buf, sem = refs[-3:]
    _, rows, colb, feat = buf.shape
    per = rows * colb
    update = jnp.dot(
        jnp.concatenate([ref[...] for ref in mixes], axis=0),
        w_ref[...],
        preferred_element_type=jnp.float32,
    )
    copies = []
    for i, (c, k) in enumerate(items):
        total = pieces[i][...].astype(jnp.float32) + update[i * per : (i + 1) * per]
        buf[i] = total.reshape(rows, colb, feat).astype(jnp.bfloat16)
        place = c * high + jnp.bitwise_xor(position(), k)
        column = pl.multiple_of(place * colb, colb)
        copies.append(
            pltpu.make_async_copy(buf.at[i], out_ref.at[:, pl.ds(column, colb), :], sem.at[i])
        )
        copies[-1].start()
    for copy in copies:
        copy.wait()


SMEM = pl.BlockSpec(memory_space=pltpu.SMEM)
HBM = pl.BlockSpec(memory_space=pltpu.HBM)


def cost(flops, moved):
    return pl.CostEstimate(flops=int(flops), bytes_accessed=int(moved), transcendentals=0)


def fast(tokens, gains, qkv_weights, out_weights):
    high = lax.axis_size("tm") // 2
    half = high // 2
    order = list(range(high - 1, -1, -1))
    rows, cols, feat = tokens.shape[1:]
    inner = out_weights.shape[1]
    wide = cols // CHUNKS
    blocks = wide // COLB
    count = rows * wide
    each = count // high
    bf = jnp.bfloat16
    x = pltpu.with_memory_space_constraint(tokens[0], pltpu.HBM)
    gains_far = pltpu.with_memory_space_constraint(gains, pltpu.HBM)
    qkv_far = pltpu.with_memory_space_constraint(qkv_weights, pltpu.HBM)
    out_far = pltpu.with_memory_space_constraint(out_weights, pltpu.HBM)

    def pick(i, n):
        return pl.BlockSpec((None,) + n, lambda _: (i,) + (0,) * len(n))

    def whole(*shape):
        return pl.BlockSpec(shape, lambda _: (0,) * len(shape))

    def call(kernel, flops, **rest):
        return pl.pallas_call(
            kernel,
            grid=(1,),
            compiler_params=params(),
            cost_estimate=cost(flops, 4 * count * feat),
            **rest,
        )

    tile = (blocks, rows, COLB, feat)
    work = 2 * count * feat * inner // high

    def made(n, width):
        return jax.ShapeDtypeStruct((n * each, width), bf)

    def full(array):
        return whole(*array.shape)

    def load(x):
        shapes = [(half * each, 2 * inner), (half * each, feat), (feat, 3 * inner), gains.shape]
        shapes += [tile] * CHUNKS
        kinds = [bf, bf, bf, gains.dtype] + [bf] * CHUNKS
        return call(
            functools.partial(load_kernel, order),
            2 * half * work,
            in_specs=[HBM, HBM, HBM],
            out_specs=[whole(*shape) for shape in shapes],
            out_shape=[jax.ShapeDtypeStruct(*pair) for pair in zip(shapes, kinds)],
            scratch_shapes=[
                pltpu.SemaphoreType.DMA((blocks * CHUNKS,)),
                pltpu.SemaphoreType.DMA((SPLIT,)),
                pltpu.SemaphoreType.DMA,
            ],
        )(x, gains_far, qkv_far)

    def ask(normed, weight):
        out = made(half, inner)
        return call(
            queries_kernel,
            half * work,
            in_specs=[full(normed), full(weight)],
            out_specs=full(out),
            out_shape=out,
        )(normed, weight)

    def project(first, x, gain, weight):
        outs = [made(high - first, inner), made(high - first, 2 * inner)]
        return call(
            functools.partial(project_kernel, first),
            3 * (high - first) * work,
            in_specs=[full(x), full(gain), full(weight)],
            out_specs=[full(out) for out in outs],
            out_shape=outs,
        )(x, gain, weight)

    def height(at, start, x, q, kv, other):
        outs = [made(1, feat)] * half
        return call(
            functools.partial(height_kernel, at, start),
            2 * half * work,
            in_specs=[full(x), full(q), full(kv), full(other), HBM],
            out_specs=[full(out) for out in outs],
            out_shape=outs,
            scratch_shapes=[
                pltpu.VMEM((half * each, inner), bf),
                pltpu.VMEM((inner, feat), bf),
                pltpu.SemaphoreType.DMA,
            ],
        )(x, q, kv, other, out_far)

    def gate(value):
        return pl.pallas_call(
            gate_kernel,
            in_specs=[pl.BlockSpec(memory_space=pl.ANY)],
            out_specs=SMEM,
            out_shape=jax.ShapeDtypeStruct((1,), jnp.int32),
            compiler_params=params(),
            cost_estimate=cost(1, 8),
            name="gate",
        )(value)

    def time_project(pieces):
        n = len(pieces)
        outs = [made(n, inner), made(n, 2 * inner)]
        return call(
            time_project_kernel,
            3 * n * work,
            in_specs=[full(piece) for piece in pieces]
            + [full(gains), pick(1, (feat, 3 * inner))],
            out_specs=[full(out) for out in outs],
            out_shape=outs,
        )(*pieces, gains, qkv_weights)

    def timed(groups, *sources):
        outs = [made(1, inner)] * high
        return call(
            functools.partial(time_kernel, groups),
            2 * high * work,
            in_specs=[full(source) for source in sources],
            out_specs=[full(out) for out in outs],
            out_shape=outs,
        )(*sources)

    def finish(items, pieces, mixes, extra):
        return call(
            functools.partial(finish_kernel, items, len(mixes), high),
            work * len(items),
            in_specs=[pick(1, (inner, feat))]
            + [whole(each, feat)] * len(items)
            + [whole(*mix.shape) for mix in mixes]
            + [pl.BlockSpec(memory_space=pl.ANY)] * len(extra),
            out_specs=HBM,
            out_shape=jax.ShapeDtypeStruct((rows, cols, feat), bf),
            scratch_shapes=[
                pltpu.VMEM((len(items), rows, COLB, feat), bf),
                pltpu.SemaphoreType.DMA((len(items),)),
            ],
            input_output_aliases={
                1 + len(items) + len(mixes): 0 for a in extra if a.ndim == 3
            },
        )(out_weights, *pieces, *mixes, *extra)

    def after(values, earlier):
        return lax.optimization_barrier((values, earlier))[0]

    def swap(a):
        return lax.ppermute(a, "space", [(0, 1), (1, 0)])

    def route(k):
        pairs = []
        for z in range(high):
            for lo in range(2):
                for s in range(2):
                    there = z ^ k
                    to = (there * 2 + (s ^ (there >= half))) * 2 + (lo ^ (z >= half))
                    pairs.append(((z * 2 + lo) * 2 + s, to))
        return pairs

    def permute(piece, k):
        return lax.ppermute(piece, ("tm", "space"), route(k))

    def exchange(pieces, ks):
        return {k: permute(pieces[k], k) for k in ks}

    heavy, light = order[:half], order[half:]
    kv, normed, weight, gain, *xs = load(x)
    other = swap(kv)
    q = ask(normed, weight)
    outs = height(0, 0, xs[0], q, kv, other)
    pieces = [dict(zip(heavy, outs)), {}]
    arrived = [exchange(pieces[0], heavy), {}]
    q, kv = project(half, after(xs[0], outs[0]), gain, weight)
    other = swap(kv)
    q1, kv1 = project(0, after(xs[1], q), gain, weight)
    other1 = swap(kv1)
    outs = height(half, 0, xs[0], after(q, q1), kv, other)
    pieces[0].update(zip(light, outs))
    arrived[0].update(exchange(pieces[0], light))
    for name, ks, n in (("far", heavy, 0), ("near", light, half)):
        q1 = after(q1, outs[0])
        outs = height(n, n * each, xs[1], q1, kv1, other1)
        pieces[1].update(zip(ks, outs))
        ready = dict(pieces[1])
        if name == "far":
            ready[half] = after(ready[half], arrived[0][half])
        arrived[1].update(exchange(ready, ks))
    last = outs[0]
    plans = [[order], [[k for k in order if k != half], [half]]]
    home, gates = [], []
    for c in range(CHUNKS):
        sources = []
        for n, group in enumerate(plans[c]):
            got = after([arrived[c][k] for k in group], last)
            q, kv = time_project(got)
            sources += [q, kv, swap(kv)]
            last = q
            if c and not n and LATE:
                home[-1].update(exchange(after(mixes, q), LATE))
        mixes = timed(plans[c], *sources)
        last = mixes[0]
        home.append(exchange(mixes, [k for k in order if c or k not in LATE]))
        if c + 1 < CHUNKS:
            last = gate(last)
            gates.append(last)
    out = gates
    for c in range(CHUNKS):
        items = [(c, k) for k in order]
        held = after([pieces[c][k] for k in order], last)
        out = [finish(items, held, [home[c][k] for k in order], out)]
    return out[0][None]


def attend_plain(stream, gain, qkv_weight, out_weight):
    groups, length, _ = stream.shape
    inner = out_weight.shape[0]
    heads = inner // HEAD
    wide = stream.astype(jnp.float32)
    normed = normalise(wide, gain)
    projected = jnp.einsum(
        "glf,fe->gle", normed, qkv_weight, preferred_element_type=jnp.float32
    ).astype(jnp.bfloat16)
    q, k, v = jnp.split(projected.reshape(groups, length, 3 * heads, HEAD), 3, axis=2)
    scores = jnp.einsum("gqhd,gkhd->ghqk", q, k, preferred_element_type=jnp.float32) * HEAD**-0.5
    weights = jax.nn.softmax(scores, axis=-1).astype(jnp.bfloat16)
    mixture = jnp.einsum("ghqk,gkhd->gqhd", weights, v, preferred_element_type=jnp.float32)
    mixture = mixture.astype(jnp.bfloat16).reshape(groups, length, inner)
    update = jnp.einsum("gle,ef->glf", mixture, out_weight, preferred_element_type=jnp.float32)
    return (wide + update).astype(jnp.bfloat16)


def plain(tokens, gains, qkv_weights, out_weights):
    frames = lax.axis_size("tm")
    local = lax.all_to_all(tokens[0], "space", split_axis=1, concat_axis=0, tiled=True)
    height_n, wide, feat = local.shape
    by_column = jnp.transpose(local, (1, 0, 2))
    done = attend_plain(by_column, gains[0], qkv_weights[0], out_weights[0])
    flat = done.reshape(frames, wide * height_n // frames, feat)
    by_frame = lax.all_to_all(flat, "tm", split_axis=0, concat_axis=0, tiled=True)
    done = attend_plain(
        jnp.transpose(by_frame, (1, 0, 2)), gains[1], qkv_weights[1], out_weights[1]
    )
    back = lax.all_to_all(
        jnp.transpose(done, (1, 0, 2)), "tm", split_axis=0, concat_axis=0, tiled=True
    )
    by_row = jnp.transpose(back.reshape(wide, height_n, feat), (1, 0, 2))
    return lax.all_to_all(by_row, "space", split_axis=0, concat_axis=1, tiled=True)[None]


def solution(mesh):
    frames, pair = mesh.shape["tm"], mesh.shape["space"]
    high = frames // 2

    def shards(tokens, gains, qkv_weights, out_weights):
        _, rows, cols, feat = tokens.shape
        inner = out_weights.shape[1]
        count = rows * cols // CHUNKS
        fits = (
            pair == 2
            and frames == 2 * high
            and high > 1
            and high & (high - 1) == 0
            and cols == CHUNKS * COLB * high
            and count % (high * POSB) == 0
            and inner % (QUAD * HEAD) == 0
            and feat % 128 == 0
        )
        body = fast if fits else plain
        return body(tokens, gains, qkv_weights, out_weights)

    return jax.shard_map(
        shards,
        mesh=mesh,
        in_specs=(P(("grp", "tm"), "space", None, None), P(), P(), P()),
        out_specs=P(("grp", "tm"), "space", None, None),
        check_vma=False,
    )
```

time: 87.9 us -> 84.6 us (0.962)
  waiting for transfers between devices: 32.8 us -> 25.2 us
  starting transfers between devices: 30.1 us -> 35.4 us
  Pallas kernels: 24.4 us -> 22.8 us
    ppermute x14 -> x16, waiting for transfers between devices: 30.9 us -> 23.9 us  [permute(): return lax.ppermute(piece, ('tm', 'space'), route(k))]
    ppermute x14 -> x16, starting transfers between devices: 28.2 us -> 30.9 us  [permute(): return lax.ppermute(piece, ('tm', 'space'), route(k))]
    ppermute x4 -> x6, starting transfers between devices: 1.88 us -> 4.5 us  [swap(): return lax.ppermute(a, 'space', [(0, 1), (1, 0)])]
    pallas_call x3 -> x2, Pallas kernels: 5.55 us -> 3.46 us  [finish(): call(functools.partial(finish_kernel, items, len(mixes), high), work * le...]
    ppermute x4 -> x6, waiting for transfers between devices: 1.92 us -> 1.33 us  [swap(): return lax.ppermute(a, 'space', [(0, 1), (1, 0)])]
    pallas_call x11 -> x14, Pallas kernels: 18.8 us -> 19.3 us  [the longest x4 6.73 us: height(): call(functools.partial(height_kernel, at, start), 2 * half * work, in_spe...]
  transfers between devices with their start and end apart: 18 -> 22, of which waited for: 8 -> 8; matrix products, arithmetic and copies ran while one was open for 0% -> 0% of each run, Pallas kernels for 16% -> 14%
where the time goes in v5:
time: 84.6 us; the launch traced here: 83.8 us
  starting transfers between devices  35.4 us (42%)
  waiting for transfers between devices  25.2 us (30%)
  Pallas kernels  22.8 us (27%)
    ppermute x16, starting transfers between devices, permute(): return lax.ppermute(piece, ('tm', 'space'), route(k))  30.9 us
    ppermute x16, waiting for transfers between devices, permute(): return lax.ppermute(piece, ('tm', 'space'), route(k))  23.9 us
    pallas_call x4, Pallas kernels, height(): call(functools.partial(height_kernel, at, start), 2 * half * work, in_spe...  6.73 us
    ppermute x6, starting transfers between devices, swap(): return lax.ppermute(a, 'space', [(0, 1), (1, 0)])  4.5 us
    pallas_call x2, Pallas kernels, finish(): call(functools.partial(finish_kernel, items, len(mixes), high), work * le...  3.46 us
    pallas_call x3, Pallas kernels, time_project(): call(time_project_kernel, 3 * n * work, in_specs=[full(piece) for piece i...  3.46 us
    pallas_call x1, Pallas kernels, load(): call(functools.partial(load_kernel, order), 2 * half * work, in_specs=[HB...  2.99 us
    pallas_call x2, Pallas kernels, timed(): call(functools.partial(time_kernel, groups), 2 * high * work, in_specs=[f...  2.82 us
  transfers between devices with their start and end apart: 22, of which 8 were waited for; matrix products, arithmetic and copies ran while one was open for 0% of the time, Pallas kernels for 14%

profile of v5, /device:TPU:1, one launch (start us, length us, event | category | flops | bytes accessed | tf_op | source)
XLA Modules:
  0.0 83.8 jit_solution(8938045893385932075)
XLA Ops:
  0.0 3.0 %shard_map.46 = (bf16[192,1024]{1,0:T(8,128)(2,1)S(1)}, bf16[192,1024]{1,0:T(8,128)(2,1)S(1)}, bf16[1024,1536]{1,0:T(8,128)(2,1)S(1)}, f32[2,1024]{1,0:T(2,128)S...) custom-call(bf16[12,64,1024]{2,1,0:T(8,128)(2,1)} %bitcast.4, f32[2,1024]{1,0:T(2,128)} %refs_1_.1, ...), custom_call_target="tpu_custom_call" | custom-call | flops 402653184 | bytes 1572864 | tf_op jit(solution)/shard_map/pallas_call | solution.py:271
  4.8 1.6 %shard_map.48 = (bf16[96,1024]{1,0:T(8,128)(2,1)S(1)}, bf16[96,1024]{1,0:T(8,128)(2,1)S(1)}) custom-call(bf16[4,12,8,1024]{3,2,1,0:T(8,128)(2,1)S(1)} %get-tuple-element.65.x_ref, bf16[192,512]{1,0:T(8,128)(2,1)S(1)} %shard_map.47.q_ref, bf16[192,1024]{1,0:T(8,128)(2,1)S(1)} %get-tuple-element.63.kv_ref, ...), custom_call_target="tpu_custom_call" | custom-call | flops 402653184 | bytes 1572864 | tf_op jit(solution)/shard_map/pallas_call | solution.py:306
  7.3 1.5 %shard_map.50 = (bf16[384,512]{1,0:T(8,128)(2,1)S(1)}, bf16[384,1024]{1,0:T(8,128)(2,1)S(1)}) custom-call(bf16[4,12,8,1024]{3,2,1,0:T(8,128)(2,1)S(1)} %get-tuple-element.68.x_ref, f32[2,1024]{1,0:T(2,128)S(1)} %get-tuple-element.66.gain_ref, bf16[1024,1536]{1,0:T(8,128)(2,1)S(1)} %get-tuple-element.62.w_ref), custom_call_target="tpu_custom_call" | custom-call | flops 1207959552 | bytes 1572864 | tf_op jit(solution)/shard_map/pallas_call | solution.py:296
  9.4 4.7 %collective-permute-start.6 = (bf16[96,1024]{1,0:T(8,128)(2,1)S(1)}, bf16[96,1024]{1,0:T(8,128)(2,1)S(1)}, u32[]{:S(2)}, u32[]{:S(2)}) collective-permute-start(bf16[96,1024]{1,0:T(8,128)(2,1)S(1)} %get-tuple-element.106.refs_0_), channel_id=1, source_target_pairs={{0,14},{1,12},{2,15},{3,13},{4,10},{5,8},{6,11},{7,9},{8,5},{9,7},... | collective-permute-start | bytes 589832 | tf_op jit(solution)/shard_map/ppermute | solution.py:388
  14.2 1.8 %shard_map.51 = (bf16[96,1024]{1,0:T(8,128)(2,1)S(1)}, bf16[96,1024]{1,0:T(8,128)(2,1)S(1)}) custom-call(bf16[4,12,8,1024]{3,2,1,0:T(8,128)(2,1)S(1)} %get-tuple-element.65.x_ref, bf16[192,512]{1,0:T(8,128)(2,1)S(1)} %get-tuple-element.70.q_ref, bf16[192,1024]{1,0:T(8,128)(2,1)S(1)} %get-tuple-element.71.kv_ref, ...), custom_call_target="tpu_custom_call" | custom-call | flops 402653184 | bytes 1572864 | tf_op jit(solution)/shard_map/pallas_call | solution.py:306
  16.0 1.5 %collective-permute-start.8 = (bf16[96,1024]{1,0:T(8,128)(2,1)S(1)}, bf16[96,1024]{1,0:T(8,128)(2,1)S(1)}, u32[]{:S(2)}, u32[]{:S(2)}) collective-permute-start(bf16[96,1024]{1,0:T(8,128)(2,1)S(1)} %get-tuple-element.108.refs_2_), channel_id=1, source_target_pairs={{0,4},{1,6},{2,5},{3,7},{4,0},{5,2},{6,1},{7,3},{8,15},{9,13},{10,... | collective-permute-start | bytes 589832 | tf_op jit(solution)/shard_map/ppermute | solution.py:388
  17.4 2.4 %collective-permute-start.9 = (bf16[96,1024]{1,0:T(8,128)(2,1)S(1)}, bf16[96,1024]{1,0:T(8,128)(2,1)S(1)}, u32[]{:S(2)}, u32[]{:S(2)}) collective-permute-start(bf16[96,1024]{1,0:T(8,128)(2,1)S(1)} %get-tuple-element.109.refs_3_), channel_id=1, source_target_pairs={{0,0},{1,2},{2,1},{3,3},{4,4},{5,6},{6,5},{7,7},{8,11},{9,9},{10,1... | collective-permute-start | bytes 589832 | tf_op jit(solution)/shard_map/ppermute | solution.py:388
  19.8 1.6 %shard_map.52 = (bf16[96,1024]{1,0:T(8,128)(2,1)S(1)}, bf16[96,1024]{1,0:T(8,128)(2,1)S(1)}) custom-call(bf16[4,12,8,1024]{3,2,1,0:T(8,128)(2,1)S(1)} %get-tuple-element.68.x_ref, bf16[384,512]{1,0:T(8,128)(2,1)S(1)} %get-tuple-element.77.q_ref, bf16[384,1024]{1,0:T(8,128)(2,1)S(1)} %get-tuple-element.74.kv_ref, ...), custom_call_target="tpu_custom_call" | custom-call | flops 402653184 | bytes 1572864 | tf_op jit(solution)/shard_map/pallas_call | solution.py:306
  21.5 1.6 %shard_map.53 = (bf16[96,1024]{1,0:T(8,128)(2,1)S(1)}, bf16[96,1024]{1,0:T(8,128)(2,1)S(1)}) custom-call(bf16[4,12,8,1024]{3,2,1,0:T(8,128)(2,1)S(1)} %get-tuple-element.68.x_ref, bf16[384,512]{1,0:T(8,128)(2,1)S(1)} %get-tuple-element.77.q_ref, bf16[384,1024]{1,0:T(8,128)(2,1)S(1)} %get-tuple-element.74.kv_ref, ...), custom_call_target="tpu_custom_call" | custom-call | flops 402653184 | bytes 1572864 | tf_op jit(solution)/shard_map/pallas_call | solution.py:306
  23.1 8.2 %collective-permute-done.7.refs_1_ = bf16[96,1024]{1,0:T(8,128)(2,1)S(1)} collective-permute-done((bf16[96,1024]{1,0:T(8,128)(2,1)S(1)}, bf16[96,1024]{1,0:T(8,128)(2,1)S(1)}, u32[]{:S(2)}, u32[]{:S(2)}) %collective-permute-start.7) | collective-permute-done | bytes 196640 | tf_op jit(solution)/shard_map/ppermute | solution.py:388
  31.4 1.6 %shard_map.54 = (bf16[384,512]{1,0:T(8,128)(2,1)S(1)}, bf16[384,1024]{1,0:T(8,128)(2,1)S(1)}) custom-call(bf16[96,1024]{1,0:T(8,128)(2,1)S(1)} %collective-permute-done.6.refs_0_, bf16[96,1024]{1,0:T(8,128)(2,1)S(1)} %collective-permute-done.7.refs_1_, bf16[96,1024]{1,0:T(8,128)(2,1)S(1)} %collective-permute-done.8.refs_2_, ...), custom_call_target="tpu_custom_call" | custom-call | flops 1207959552 | bytes 1572864 | tf_op jit(solution)/shard_map/pallas_call | solution.py:333
  33.0 1.4 %collective-permute-start.10 = (bf16[384,1024]{1,0:T(8,128)(2,1)S(1)}, bf16[384,1024]{1,0:T(8,128)(2,1)S(1)}, u32[]{:S(2)}, u32[]{:S(2)}) collective-permute-start(bf16[384,1024]{1,0:T(8,128)(2,1)S(1)} %get-tuple-element.87.refs_1_), channel_id=1, source_target_pairs={{0,1},{1,0},{2,3},{3,2},{4,5},{5,4},{6,7},{7,6},{8,9},{9,8},{10,11... | collective-permute-start | bytes 2359304 | tf_op jit(solution)/shard_map/ppermute | solution.py:375
  34.4 2.4 %collective-permute-start.5 = (bf16[96,1024]{1,0:T(8,128)(2,1)S(1)}, bf16[96,1024]{1,0:T(8,128)(2,1)S(1)}, u32[]{:S(2)}, u32[]{:S(2)}) collective-permute-start(bf16[96,1024]{1,0:T(8,128)(2,1)S(1)} %get-tuple-element.102.refs_3_), channel_id=1, source_target_pairs={{0,0},{1,2},{2,1},{3,3},{4,4},{5,6},{6,5},{7,7},{8,11},{9,9},{10,1... | collective-permute-start | bytes 589832 | tf_op jit(solution)/shard_map/ppermute | solution.py:388
  36.8 2.7 %collective-permute-start.3 = (bf16[96,1024]{1,0:T(8,128)(2,1)S(1)}, bf16[96,1024]{1,0:T(8,128)(2,1)S(1)}, u32[]{:S(2)}, u32[]{:S(2)}) collective-permute-start(bf16[96,1024]{1,0:T(8,128)(2,1)S(1)} %get-tuple-element.99.refs_0_), channel_id=1, source_target_pairs={{0,14},{1,12},{2,15},{3,13},{4,10},{5,8},{6,11},{7,9},{8,5},{9,7},... | collective-permute-start | bytes 589832 | tf_op jit(solution)/shard_map/ppermute | solution.py:388
  41.4 2.9 %collective-permute-done.5.refs_2_ = bf16[96,1024]{1,0:T(8,128)(2,1)S(1)} collective-permute-done((bf16[96,1024]{1,0:T(8,128)(2,1)S(1)}, bf16[96,1024]{1,0:T(8,128)(2,1)S(1)}, u32[]{:S(2)}, u32[]{:S(2)}) %collective-permute-start.5) | collective-permute-done | bytes 196640 | tf_op jit(solution)/shard_map/ppermute | solution.py:388
  46.0 1.8 %collective-permute-start.11 = (bf16[288,1024]{1,0:T(8,128)(2,1)S(1)}, bf16[288,1024]{1,0:T(8,128)(2,1)S(1)}, u32[]{:S(2)}, u32[]{:S(2)}) collective-permute-start(bf16[288,1024]{1,0:T(8,128)(2,1)S(1)} %get-tuple-element.93.refs_1_), channel_id=1, source_target_pairs={{0,1},{1,0},{2,3},{3,2},{4,5},{5,4},{6,7},{7,6},{8,9},{9,8},{10,11... | collective-permute-start | bytes 1769480 | tf_op jit(solution)/shard_map/ppermute | solution.py:375
  47.8 3.7 %collective-permute-start.12 = (bf16[96,1024]{1,0:T(8,128)(2,1)S(1)}, bf16[96,1024]{1,0:T(8,128)(2,1)S(1)}, u32[]{:S(2)}, u32[]{:S(2)}) collective-permute-start(bf16[96,1024]{1,0:T(8,128)(2,1)S(1)} %get-tuple-element.100.refs_1_), channel_id=1, source_target_pairs={{0,10},{1,8},{2,11},{3,9},{4,14},{5,12},{6,15},{7,13},{8,1},{9,3},... | collective-permute-start | bytes 589832 | tf_op jit(solution)/shard_map/ppermute | solution.py:388
  51.5 9.7 %collective-permute-done.12.refs_0_ = bf16[96,1024]{1,0:T(8,128)(2,1)S(1)} collective-permute-done((bf16[96,1024]{1,0:T(8,128)(2,1)S(1)}, bf16[96,1024]{1,0:T(8,128)(2,1)S(1)}, u32[]{:S(2)}, u32[]{:S(2)}) %collective-permute-start.12) | collective-permute-done | bytes 196640 | tf_op jit(solution)/shard_map/ppermute | solution.py:388
  63.7 2.8 %collective-permute-start.20 = (bf16[96,512]{1,0:T(8,128)(2,1)S(1)}, bf16[96,512]{1,0:T(8,128)(2,1)S(1)}, u32[]{:S(2)}, u32[]{:S(2)}) collective-permute-start(bf16[96,512]{1,0:T(8,128)(2,1)S(1)} %get-tuple-element.112), channel_id=1, source_target_pairs={{0,4},{1,6},{2,5},{3,7},{4,0},{5,2},{6,1},{7,3},{8,15},{9,13},{10,... | collective-permute-start | bytes 294920 | tf_op jit(solution)/shard_map/ppermute | solution.py:388
  66.6 3.2 %collective-permute-start.21 = (bf16[96,512]{1,0:T(8,128)(2,1)S(1)}, bf16[96,512]{1,0:T(8,128)(2,1)S(1)}, u32[]{:S(2)}, u32[]{:S(2)}) collective-permute-start(bf16[96,512]{1,0:T(8,128)(2,1)S(1)} %get-tuple-element.88.in_ref), channel_id=1, source_target_pairs={{0,0},{1,2},{2,1},{3,3},{4,4},{5,6},{6,5},{7,7},{8,11},{9,9},{10,1... | collective-permute-start | bytes 294920 | tf_op jit(solution)/shard_map/ppermute | solution.py:388
  73.2 2.0 %collective-permute-start.16 = (bf16[96,512]{1,0:T(8,128)(2,1)S(1)}, bf16[96,512]{1,0:T(8,128)(2,1)S(1)}, u32[]{:S(2)}, u32[]{:S(2)}) collective-permute-start(bf16[96,512]{1,0:T(8,128)(2,1)S(1)} %get-tuple-element.105), channel_id=1, source_target_pairs={{0,4},{1,6},{2,5},{3,7},{4,0},{5,2},{6,1},{7,3},{8,15},{9,13},{10,... | collective-permute-start | bytes 294920 | tf_op jit(solution)/shard_map/ppermute | solution.py:388
  75.3 3.2 %collective-permute-start.17 = (bf16[96,512]{1,0:T(8,128)(2,1)S(1)}, bf16[96,512]{1,0:T(8,128)(2,1)S(1)}, u32[]{:S(2)}, u32[]{:S(2)}) collective-permute-start(bf16[96,512]{1,0:T(8,128)(2,1)S(1)} %get-tuple-element.98), channel_id=1, source_target_pairs={{0,0},{1,2},{2,1},{3,3},{4,4},{5,6},{6,5},{7,7},{8,11},{9,9},{10,1... | collective-permute-start | bytes 294920 | tf_op jit(solution)/shard_map/ppermute | solution.py:388
  78.5 2.0 %shard_map.59.refs_8_ = bf16[12,64,1024]{2,1,0:T(8,128)(2,1)} custom-call(bf16[2,512,1024]{2,1,0:T(8,128)(2,1)S(1)} %copy-done, bf16[96,1024]{1,0:T(8,128)(2,1)S(1)} %get-tuple-element.106.refs_0_, bf16[96,1024]{1,0:T(8,128)(2,1)S(1)} %get-tuple-element.107.refs_1_, bf16[96,1024]{1,0:T(8,128)(2,1)S(1)} %get-tuple-element.108.refs_2_, ...), custom_call_target="tpu_custom_call" | custom-call | flops 402653184 | bytes 1572864 | tf_op jit(solution)/shard_map/pallas_call | solution.py:353
  82.3 1.4 %shard_map.60 = bf16[12,64,1024]{2,1,0:T(8,128)(2,1)} custom-call(bf16[2,512,1024]{2,1,0:T(8,128)(2,1)S(1)} %copy-done, bf16[96,1024]{1,0:T(8,128)(2,1)S(1)} %get-tuple-element.99.refs_0_, bf16[96,1024]{1,0:T(8,128)(2,1)S(1)} %get-tuple-element.100.refs_1_, bf16[96,1024]{1,0:T(8,128)(2,1)S(1)} %get-tuple-element.101.refs_2_, ...), custom_call_target="tpu_custom_call", output_to_operand_aliasing={{}: (9, {})} | custom-call | flops 402653184 | bytes 1572864 | tf_op jit(solution)/shard_map/pallas_call | solution.py:353
  (45 shorter events, 14.6 us)
Async XLA Ops:
  3.0 1.8 %collective-permute-start = (bf16[192,1024]{1,0:T(8,128)(2,1)S(1)}, bf16[192,1024]{1,0:T(8,128)(2,1)S(1)}, u32[]{:S(2)}, u32[]{:S(2)}) collective-permute-start(bf16[192,1024]{1,0:T(8,128)(2,1)S(1)} %get-tuple-element.63.kv_ref), channel_id=1, source_target_pairs={{0,1},{1,0},{2,3},{3,2},{4,5},{5,4},{6,7},{7,6},{8,9},{9,8},{10,11... | collective-permute-start | bytes 1179656 | tf_op jit(solution)/shard_map/ppermute | solution.py:375
  8.9 10.9 %collective-permute-start.2 = (bf16[384,1024]{1,0:T(8,128)(2,1)S(1)}, bf16[384,1024]{1,0:T(8,128)(2,1)S(1)}, u32[]{:S(2)}, u32[]{:S(2)}) collective-permute-start(bf16[384,1024]{1,0:T(8,128)(2,1)S(1)} %get-tuple-element.74.kv_ref), channel_id=1, source_target_pairs={{0,1},{1,0},{2,3},{3,2},{4,5},{5,4},{6,7},{7,6},{8,9},{9,8},{10,11... | collective-permute-start | bytes 2359304 | tf_op jit(solution)/shard_map/ppermute | solution.py:375
  9.1 5.1 %collective-permute-start.1 = (bf16[192,1024]{1,0:T(8,128)(2,1)S(1)}, bf16[192,1024]{1,0:T(8,128)(2,1)S(1)}, u32[]{:S(2)}, u32[]{:S(2)}) collective-permute-start(bf16[192,1024]{1,0:T(8,128)(2,1)S(1)} %get-tuple-element.71.kv_ref), channel_id=1, source_target_pairs={{0,1},{1,0},{2,3},{3,2},{4,5},{5,4},{6,7},{7,6},{8,9},{9,8},{10,11... | collective-permute-start | bytes 1179656 | tf_op jit(solution)/shard_map/ppermute | solution.py:375
  9.4 21.9 %collective-permute-start.6 = (bf16[96,1024]{1,0:T(8,128)(2,1)S(1)}, bf16[96,1024]{1,0:T(8,128)(2,1)S(1)}, u32[]{:S(2)}, u32[]{:S(2)}) collective-permute-start(bf16[96,1024]{1,0:T(8,128)(2,1)S(1)} %get-tuple-element.106.refs_0_), channel_id=1, source_target_pairs={{0,14},{1,12},{2,15},{3,13},{4,10},{5,8},{6,11},{7,9},{8,5},{9,7},... | collective-permute-start | bytes 589832 | tf_op jit(solution)/shard_map/ppermute | solution.py:388
  14.1 17.2 %collective-permute-start.7 = (bf16[96,1024]{1,0:T(8,128)(2,1)S(1)}, bf16[96,1024]{1,0:T(8,128)(2,1)S(1)}, u32[]{:S(2)}, u32[]{:S(2)}) collective-permute-start(bf16[96,1024]{1,0:T(8,128)(2,1)S(1)} %get-tuple-element.107.refs_1_), channel_id=1, source_target_pairs={{0,10},{1,8},{2,11},{3,9},{4,14},{5,12},{6,15},{7,13},{8,1},{9,3},... | collective-permute-start | bytes 589832 | tf_op jit(solution)/shard_map/ppermute | solution.py:388
  14.2 17.2 %slice-start = ((s8[6291456]{0:T(1024)(128)(4,1)}), s8[4194304]{0:T(1024)(128)(4,1)S(1)}, s32[]{:S(2)}) async-start(s8[6291456]{0:T(1024)(128)(4,1)} %bitcast.2), calls=%async_computation | async-start | bytes 8388608
  16.0 15.4 %collective-permute-start.8 = (bf16[96,1024]{1,0:T(8,128)(2,1)S(1)}, bf16[96,1024]{1,0:T(8,128)(2,1)S(1)}, u32[]{:S(2)}, u32[]{:S(2)}) collective-permute-start(bf16[96,1024]{1,0:T(8,128)(2,1)S(1)} %get-tuple-element.108.refs_2_), channel_id=1, source_target_pairs={{0,4},{1,6},{2,5},{3,7},{4,0},{5,2},{6,1},{7,3},{8,15},{9,13},{10,... | collective-permute-start | bytes 589832 | tf_op jit(solution)/shard_map/ppermute | solution.py:388
  17.4 13.9 %collective-permute-start.9 = (bf16[96,1024]{1,0:T(8,128)(2,1)S(1)}, bf16[96,1024]{1,0:T(8,128)(2,1)S(1)}, u32[]{:S(2)}, u32[]{:S(2)}) collective-permute-start(bf16[96,1024]{1,0:T(8,128)(2,1)S(1)} %get-tuple-element.109.refs_3_), channel_id=1, source_target_pairs={{0,0},{1,2},{2,1},{3,3},{4,4},{5,6},{6,5},{7,7},{8,11},{9,9},{10,1... | collective-permute-start | bytes 589832 | tf_op jit(solution)/shard_map/ppermute | solution.py:388
  33.0 6.4 %collective-permute-start.10 = (bf16[384,1024]{1,0:T(8,128)(2,1)S(1)}, bf16[384,1024]{1,0:T(8,128)(2,1)S(1)}, u32[]{:S(2)}, u32[]{:S(2)}) collective-permute-start(bf16[384,1024]{1,0:T(8,128)(2,1)S(1)} %get-tuple-element.87.refs_1_), channel_id=1, source_target_pairs={{0,1},{1,0},{2,3},{3,2},{4,5},{5,4},{6,7},{7,6},{8,9},{9,8},{10,11... | collective-permute-start | bytes 2359304 | tf_op jit(solution)/shard_map/ppermute | solution.py:375
  34.4 7.0 %collective-permute-start.4 = (bf16[96,1024]{1,0:T(8,128)(2,1)S(1)}, bf16[96,1024]{1,0:T(8,128)(2,1)S(1)}, u32[]{:S(2)}, u32[]{:S(2)}) collective-permute-start(bf16[96,1024]{1,0:T(8,128)(2,1)S(1)} %get-tuple-element.101.refs_2_), channel_id=1, source_target_pairs={{0,4},{1,6},{2,5},{3,7},{4,0},{5,2},{6,1},{7,3},{8,15},{9,13},{10,... | collective-permute-start | bytes 589832 | tf_op jit(solution)/shard_map/ppermute | solution.py:388
  34.4 9.9 %collective-permute-start.5 = (bf16[96,1024]{1,0:T(8,128)(2,1)S(1)}, bf16[96,1024]{1,0:T(8,128)(2,1)S(1)}, u32[]{:S(2)}, u32[]{:S(2)}) collective-permute-start(bf16[96,1024]{1,0:T(8,128)(2,1)S(1)} %get-tuple-element.102.refs_3_), channel_id=1, source_target_pairs={{0,0},{1,2},{2,1},{3,3},{4,4},{5,6},{6,5},{7,7},{8,11},{9,9},{10,1... | collective-permute-start | bytes 589832 | tf_op jit(solution)/shard_map/ppermute | solution.py:388
  36.8 8.0 %collective-permute-start.3 = (bf16[96,1024]{1,0:T(8,128)(2,1)S(1)}, bf16[96,1024]{1,0:T(8,128)(2,1)S(1)}, u32[]{:S(2)}, u32[]{:S(2)}) collective-permute-start(bf16[96,1024]{1,0:T(8,128)(2,1)S(1)} %get-tuple-element.99.refs_0_), channel_id=1, source_target_pairs={{0,14},{1,12},{2,15},{3,13},{4,10},{5,8},{6,11},{7,9},{8,5},{9,7},... | collective-permute-start | bytes 589832 | tf_op jit(solution)/shard_map/ppermute | solution.py:388
  46.0 23.8 %collective-permute-start.11 = (bf16[288,1024]{1,0:T(8,128)(2,1)S(1)}, bf16[288,1024]{1,0:T(8,128)(2,1)S(1)}, u32[]{:S(2)}, u32[]{:S(2)}) collective-permute-start(bf16[288,1024]{1,0:T(8,128)(2,1)S(1)} %get-tuple-element.93.refs_1_), channel_id=1, source_target_pairs={{0,1},{1,0},{2,3},{3,2},{4,5},{5,4},{6,7},{7,6},{8,9},{9,8},{10,11... | collective-permute-start | bytes 1769480 | tf_op jit(solution)/shard_map/ppermute | solution.py:375
  47.8 13.4 %collective-permute-start.12 = (bf16[96,1024]{1,0:T(8,128)(2,1)S(1)}, bf16[96,1024]{1,0:T(8,128)(2,1)S(1)}, u32[]{:S(2)}, u32[]{:S(2)}) collective-permute-start(bf16[96,1024]{1,0:T(8,128)(2,1)S(1)} %get-tuple-element.100.refs_1_), channel_id=1, source_target_pairs={{0,10},{1,8},{2,11},{3,9},{4,14},{5,12},{6,15},{7,13},{8,1},{9,3},... | collective-permute-start | bytes 589832 | tf_op jit(solution)/shard_map/ppermute | solution.py:388
  61.9 16.6 %copy-start = (bf16[2,512,1024]{2,1,0:T(8,128)(2,1)S(1)}, bf16[2,512,1024]{2,1,0:T(8,128)(2,1)}, u32[]{:S(2)}) copy-start(bf16[2,512,1024]{2,1,0:T(8,128)(2,1)} %w_ref.13) | copy-start | bytes 6291460
  61.9 4.6 %collective-permute-start.13 = (bf16[96,1024]{1,0:T(8,128)(2,1)S(1)}, bf16[96,1024]{1,0:T(8,128)(2,1)S(1)}, u32[]{:S(2)}, u32[]{:S(2)}) collective-permute-start(bf16[96,1024]{1,0:T(8,128)(2,1)S(1)} %get-tuple-element.97.refs_4_), channel_id=1, source_target_pairs={{0,1},{1,0},{2,3},{3,2},{4,5},{5,4},{6,7},{7,6},{8,9},{9,8},{10,11... | collective-permute-start | bytes 589832 | tf_op jit(solution)/shard_map/ppermute | solution.py:375
  62.6 9.8 %collective-permute-start.18 = (bf16[96,512]{1,0:T(8,128)(2,1)S(1)}, bf16[96,512]{1,0:T(8,128)(2,1)S(1)}, u32[]{:S(2)}, u32[]{:S(2)}) collective-permute-start(bf16[96,512]{1,0:T(8,128)(2,1)S(1)} %get-tuple-element.110), channel_id=1, source_target_pairs={{0,14},{1,12},{2,15},{3,13},{4,10},{5,8},{6,11},{7,9},{8,5},{9,7},... | collective-permute-start | bytes 294920 | tf_op jit(solution)/shard_map/ppermute | solution.py:388
  63.7 9.5 %collective-permute-start.19 = (bf16[96,512]{1,0:T(8,128)(2,1)S(1)}, bf16[96,512]{1,0:T(8,128)(2,1)S(1)}, u32[]{:S(2)}, u32[]{:S(2)}) collective-permute-start(bf16[96,512]{1,0:T(8,128)(2,1)S(1)} %get-tuple-element.111), channel_id=1, source_target_pairs={{0,10},{1,8},{2,11},{3,9},{4,14},{5,12},{6,15},{7,13},{8,1},{9,3},... | collective-permute-start | bytes 294920 | tf_op jit(solution)/shard_map/ppermute | solution.py:388
  63.7 11.5 %collective-permute-start.20 = (bf16[96,512]{1,0:T(8,128)(2,1)S(1)}, bf16[96,512]{1,0:T(8,128)(2,1)S(1)}, u32[]{:S(2)}, u32[]{:S(2)}) collective-permute-start(bf16[96,512]{1,0:T(8,128)(2,1)S(1)} %get-tuple-element.112), channel_id=1, source_target_pairs={{0,4},{1,6},{2,5},{3,7},{4,0},{5,2},{6,1},{7,3},{8,15},{9,13},{10,... | collective-permute-start | bytes 294920 | tf_op jit(solution)/shard_map/ppermute | solution.py:388
  66.6 11.9 %collective-permute-start.21 = (bf16[96,512]{1,0:T(8,128)(2,1)S(1)}, bf16[96,512]{1,0:T(8,128)(2,1)S(1)}, u32[]{:S(2)}, u32[]{:S(2)}) collective-permute-start(bf16[96,512]{1,0:T(8,128)(2,1)S(1)} %get-tuple-element.88.in_ref), channel_id=1, source_target_pairs={{0,0},{1,2},{2,1},{3,3},{4,4},{5,6},{6,5},{7,7},{8,11},{9,9},{10,1... | collective-permute-start | bytes 294920 | tf_op jit(solution)/shard_map/ppermute | solution.py:388
  71.2 9.3 %collective-permute-start.14 = (bf16[96,512]{1,0:T(8,128)(2,1)S(1)}, bf16[96,512]{1,0:T(8,128)(2,1)S(1)}, u32[]{:S(2)}, u32[]{:S(2)}) collective-permute-start(bf16[96,512]{1,0:T(8,128)(2,1)S(1)} %get-tuple-element.103), channel_id=1, source_target_pairs={{0,14},{1,12},{2,15},{3,13},{4,10},{5,8},{6,11},{7,9},{8,5},{9,7},... | collective-permute-start | bytes 294920 | tf_op jit(solution)/shard_map/ppermute | solution.py:388
  72.4 9.3 %collective-permute-start.15 = (bf16[96,512]{1,0:T(8,128)(2,1)S(1)}, bf16[96,512]{1,0:T(8,128)(2,1)S(1)}, u32[]{:S(2)}, u32[]{:S(2)}) collective-permute-start(bf16[96,512]{1,0:T(8,128)(2,1)S(1)} %get-tuple-element.104), channel_id=1, source_target_pairs={{0,10},{1,8},{2,11},{3,9},{4,14},{5,12},{6,15},{7,13},{8,1},{9,3},... | collective-permute-start | bytes 294920 | tf_op jit(solution)/shard_map/ppermute | solution.py:388
  73.2 8.4 %collective-permute-start.16 = (bf16[96,512]{1,0:T(8,128)(2,1)S(1)}, bf16[96,512]{1,0:T(8,128)(2,1)S(1)}, u32[]{:S(2)}, u32[]{:S(2)}) collective-permute-start(bf16[96,512]{1,0:T(8,128)(2,1)S(1)} %get-tuple-element.105), channel_id=1, source_target_pairs={{0,4},{1,6},{2,5},{3,7},{4,0},{5,2},{6,1},{7,3},{8,15},{9,13},{10,... | collective-permute-start | bytes 294920 | tf_op jit(solution)/shard_map/ppermute | solution.py:388
  75.3 7.0 %collective-permute-start.17 = (bf16[96,512]{1,0:T(8,128)(2,1)S(1)}, bf16[96,512]{1,0:T(8,128)(2,1)S(1)}, u32[]{:S(2)}, u32[]{:S(2)}) collective-permute-start(bf16[96,512]{1,0:T(8,128)(2,1)S(1)} %get-tuple-element.98), channel_id=1, source_target_pairs={{0,0},{1,2},{2,1},{3,3},{4,4},{5,6},{6,5},{7,7},{8,11},{9,9},{10,1... | collective-permute-start | bytes 294920 | tf_op jit(solution)/shard_map/ppermute | solution.py:388
  (2 other events, 23.9 us)

commit v6 on v5

--- a/solution.py
+++ b/solution.py
@@ -14,7 +14,6 @@
 CHUNKS = 2
 COLB = 8
 SPLIT = 2
-LATE = ()
 POSB = 16
 NEG = -1e30
 VMEM_BYTES = 16 * 1024 * 1024
@@ -60,76 +59,81 @@
     return parts[0] if len(parts) == 1 else jnp.concatenate(parts, axis=0)
 
 
-def project_keys(normed, w_ref, kv_ref):
-    inner = kv_ref.shape[1] // 2
-    kv_ref[...] = jnp.dot(
-        normed, w_ref[:, inner:], preferred_element_type=jnp.float32
-    ).astype(jnp.bfloat16)
-
-
-def project_queries(normed, w_ref, q_ref):
-    q_ref[...] = jnp.dot(
-        normed, w_ref[:, : q_ref.shape[1]], preferred_element_type=jnp.float32
-    ).astype(jnp.bfloat16) * jnp.bfloat16(HEAD**-0.5)
+def project_keys(normed, weight, kv_ref):
+    kv_ref[...] = jnp.dot(normed, weight, preferred_element_type=jnp.float32).astype(jnp.bfloat16)
+
+
+def project_queries(normed, weight, q_ref):
+    q_ref[...] = jnp.dot(normed, weight, preferred_element_type=jnp.float32).astype(
+        jnp.bfloat16
+    ) * jnp.bfloat16(HEAD**-0.5)
 
 
 def position():
     return lax.axis_index("tm") // 2
 
 
-def load_kernel(order, x_ref, gain_ref, w_ref, kv_ref, normed_ref, w_out, gain_out, *refs):
-    x_outs, (x_sem, w_sem, gain_sem) = refs[:CHUNKS], refs[CHUNKS:]
-    blocks, rows, colb, feat = x_outs[0].shape
-    inner = kv_ref.shape[1] // 2
+def token_loads(c, ks, high, x_ref, x_out, sem):
+    colb = x_out.shape[2]
+    loads = []
+    for i, k in enumerate(ks):
+        column = pl.multiple_of((c * high + jnp.bitwise_xor(position(), k)) * colb, colb)
+        loads.append(
+            pltpu.make_async_copy(x_ref.at[:, pl.ds(column, colb), :], x_out.at[i], sem.at[i])
+        )
+    return loads
+
+
+def load_kernel(ks, high, x_ref, gain_ref, w_ref, kv_ref, normed_ref, w_out, gain_out, *refs):
+    x_out, x_sem, w_sem, gain_sem = refs
+    _, rows, colb, feat = x_out.shape
+    width = kv_ref.shape[1]
     per = rows * colb
-    first = kv_ref.shape[0] // per
-    loads = []
-    for c in range(CHUNKS):
-        for i, k in enumerate(order):
-            column = pl.multiple_of((c * blocks + jnp.bitwise_xor(position(), k)) * colb, colb)
-            loads.append(
-                pltpu.make_async_copy(
-                    x_ref.at[:, pl.ds(column, colb), :], x_outs[c].at[i], x_sem.at[c * blocks + i]
-                )
-            )
+    loads = token_loads(0, ks, high, x_ref, x_out, x_sem)
     step = feat // SPLIT
     fetches = [
         pltpu.make_async_copy(
-            w_ref.at[0, pl.ds(i * step, step), :], w_out.at[pl.ds(i * step, step), :], w_sem.at[i]
+            w_ref.at[0, pl.ds(i * step, step), pl.ds(width // 2, width)],
+            w_out.at[pl.ds(i * step, step), :],
+            w_sem.at[i],
         )
         for i in range(SPLIT)
     ]
     gain_load = pltpu.make_async_copy(gain_ref, gain_out, gain_sem)
-    for copy in [gain_load] + loads[:first] + fetches + loads[first:]:
+    for copy in [gain_load] + loads + fetches:
         copy.start()
     gain_load.wait()
-    for i in range(first):
-        loads[i].wait()
-        stream = x_outs[0][i].astype(jnp.float32).reshape(per, feat)
+    for i, load in enumerate(loads):
+        load.wait()
+        stream = x_out[i].astype(jnp.float32).reshape(per, feat)
         normed_ref[i * per : (i + 1) * per, :] = normalise(stream, gain_out[0:1, :])
     total = None
     for i, fetch in enumerate(fetches):
         fetch.wait()
         span = slice(i * step, (i + 1) * step)
-        part = jnp.dot(
-            normed_ref[:, span], w_out[span, inner:], preferred_element_type=jnp.float32
-        )
+        part = jnp.dot(normed_ref[:, span], w_out[span, :], preferred_element_type=jnp.float32)
         total = part if total is None else total + part
     kv_ref[...] = total.astype(jnp.bfloat16)
-    for load in loads[first:]:
+
+
+def ask_kernel(normed_ref, w_ref, q_ref, w_out, sem):
+    fetch = pltpu.make_async_copy(w_ref.at[0, :, pl.ds(0, q_ref.shape[1])], w_out, sem)
+    fetch.start()
+    fetch.wait()
+    project_queries(normed_ref[...], w_out[...], q_ref)
+
+
+def project_kernel(c, ks, high, x_ref, gain_ref, keys_ref, queries_ref, q_ref, kv_ref, x_out, sem):
+    count, rows, colb, feat = x_out.shape
+    loads = token_loads(c, ks, high, x_ref, x_out, sem)
+    for load in loads:
+        load.start()
+    for load in loads:
         load.wait()
-
-
-def queries_kernel(normed_ref, w_ref, q_ref):
-    project_queries(normed_ref[...], w_ref, q_ref)
-
-
-def project_kernel(first, x_ref, gain_ref, w_ref, q_ref, kv_ref):
-    blocks, rows, colb, feat = x_ref.shape
-    stream = x_ref[first:].astype(jnp.float32).reshape((blocks - first) * rows * colb, feat)
+    stream = x_out[...].astype(jnp.float32).reshape(count * rows * colb, feat)
     normed = normalise(stream, gain_ref[0:1, :])
-    project_keys(normed, w_ref, kv_ref)
-    project_queries(normed, w_ref, q_ref)
+    project_keys(normed, keys_ref[...], kv_ref)
+    project_queries(normed, queries_ref[...], q_ref)
 
 
 def height_kernel(tile, start, x_ref, q_ref, kv_ref, other_ref, w_ref, *refs):
@@ -161,35 +165,38 @@
 def time_project_kernel(*refs):
     gain_ref, w_ref, q_ref, kv_ref = refs[-4:]
     normed = join([normalise(ref[...].astype(jnp.float32), gain_ref[1:2, :]) for ref in refs[:-4]])
-    project_keys(normed, w_ref, kv_ref)
-    project_queries(normed, w_ref, q_ref)
+    inner = q_ref.shape[1]
+    project_keys(normed, w_ref[:, inner:], kv_ref)
+    project_queries(normed, w_ref[:, :inner], q_ref)
 
 
 def gate_kernel(in_ref, out_ref):
     out_ref[0] = 0
 
 
-def time_kernel(groups, *refs):
+def time_kernel(groups, ks, *refs):
     count = 3 * len(groups)
     sources, mix_refs = refs[:count], refs[count:]
     each, inner = mix_refs[0].shape
     width = QUAD * HEAD
-    bias = group_bias(2 * len(mix_refs) * POSB, POSB)
     flat = [(g, i, k) for g, group in enumerate(groups) for i, k in enumerate(group)]
 
-    def rows(which, p, lo):
+    bias = group_bias(2 * len(flat) * POSB, POSB)
+
+    def rows(which, p, lo, chosen=flat):
         return [
             sources[3 * g + which][i * each + p : i * each + p + POSB, lo : lo + width]
-            for g, i, _ in flat
+            for g, i, _ in chosen
         ]
 
     for p in range(0, each, POSB):
         for lo in range(0, inner, width):
             key = join(rows(1, p, lo) + rows(2, p, lo))
             value = join(rows(1, p, inner + lo) + rows(2, p, inner + lo))
-            out = attend_quad(join(rows(0, p, lo)), key, value, bias)
-            for n, (_, _, k) in enumerate(flat):
-                mix_refs[k][p : p + POSB, lo : lo + width] = out[n * POSB : (n + 1) * POSB]
+            asking = [entry for k in ks for entry in flat if entry[2] == k]
+            out = attend_quad(join(rows(0, p, lo, asking)), key, value, bias)
+            for n, ref in enumerate(mix_refs):
+                ref[p : p + POSB, lo : lo + width] = out[n * POSB : (n + 1) * POSB]
 
 
 def finish_kernel(items, mixed, high, w_ref, *refs):
@@ -228,10 +235,10 @@
     high = lax.axis_size("tm") // 2
     half = high // 2
     order = list(range(high - 1, -1, -1))
+    heavy, light = order[:half], order[half:]
     rows, cols, feat = tokens.shape[1:]
     inner = out_weights.shape[1]
     wide = cols // CHUNKS
-    blocks = wide // COLB
     count = rows * wide
     each = count // high
     bf = jnp.bfloat16
@@ -255,7 +262,6 @@
             **rest,
         )
 
-    tile = (blocks, rows, COLB, feat)
     work = 2 * count * feat * inner // high
 
     def made(n, width):
@@ -264,53 +270,63 @@
     def full(array):
         return whole(*array.shape)
 
+    def tiles(n):
+        return jax.ShapeDtypeStruct((n, rows, COLB, feat), bf)
+
     def load(x):
-        shapes = [(half * each, 2 * inner), (half * each, feat), (feat, 3 * inner), gains.shape]
-        shapes += [tile] * CHUNKS
-        kinds = [bf, bf, bf, gains.dtype] + [bf] * CHUNKS
-        return call(
-            functools.partial(load_kernel, order),
+        outs = [
+            made(half, 2 * inner),
+            made(half, feat),
+            jax.ShapeDtypeStruct((feat, 2 * inner), bf),
+            jax.ShapeDtypeStruct(gains.shape, gains.dtype),
+            tiles(half),
+        ]
+        return call(
+            functools.partial(load_kernel, heavy, high),
             2 * half * work,
             in_specs=[HBM, HBM, HBM],
-            out_specs=[whole(*shape) for shape in shapes],
-            out_shape=[jax.ShapeDtypeStruct(*pair) for pair in zip(shapes, kinds)],
+            out_specs=[full(out) for out in outs],
+            out_shape=outs,
             scratch_shapes=[
-                pltpu.SemaphoreType.DMA((blocks * CHUNKS,)),
+                pltpu.SemaphoreType.DMA((half,)),
                 pltpu.SemaphoreType.DMA((SPLIT,)),
                 pltpu.SemaphoreType.DMA,
             ],
         )(x, gains_far, qkv_far)
 
-    def ask(normed, weight):
-        out = made(half, inner)
-        return call(
-            queries_kernel,
+    def ask(normed):
+        outs = [made(half, inner), jax.ShapeDtypeStruct((feat, inner), bf)]
+        return call(
+            ask_kernel,
             half * work,
-            in_specs=[full(normed), full(weight)],
-            out_specs=full(out),
-            out_shape=out,
-        )(normed, weight)
-
-    def project(first, x, gain, weight):
-        outs = [made(high - first, inner), made(high - first, 2 * inner)]
-        return call(
-            functools.partial(project_kernel, first),
-            3 * (high - first) * work,
-            in_specs=[full(x), full(gain), full(weight)],
+            in_specs=[full(normed), HBM],
             out_specs=[full(out) for out in outs],
             out_shape=outs,
-        )(x, gain, weight)
-
-    def height(at, start, x, q, kv, other):
-        outs = [made(1, feat)] * half
-        return call(
-            functools.partial(height_kernel, at, start),
-            2 * half * work,
+            scratch_shapes=[pltpu.SemaphoreType.DMA],
+        )(normed, qkv_far)
+
+    def project(c, ks, x, gain, keys, queries):
+        n = len(ks)
+        outs = [made(n, inner), made(n, 2 * inner), tiles(n)]
+        return call(
+            functools.partial(project_kernel, c, ks, high),
+            3 * n * work,
+            in_specs=[HBM, full(gain), full(keys), full(queries)],
+            out_specs=[full(out) for out in outs],
+            out_shape=outs,
+            scratch_shapes=[pltpu.SemaphoreType.DMA((n,))],
+        )(x, gain, keys, queries)
+
+    def height(n, at, x, q, kv, other):
+        outs = [made(1, feat)] * n
+        return call(
+            functools.partial(height_kernel, at, at * each),
+            2 * n * work,
             in_specs=[full(x), full(q), full(kv), full(other), HBM],
             out_specs=[full(out) for out in outs],
             out_shape=outs,
             scratch_shapes=[
-                pltpu.VMEM((half * each, inner), bf),
+                pltpu.VMEM((n * each, inner), bf),
                 pltpu.VMEM((inner, feat), bf),
                 pltpu.SemaphoreType.DMA,
             ],
@@ -339,11 +355,11 @@
             out_shape=outs,
         )(*pieces, gains, qkv_weights)
 
-    def timed(groups, *sources):
-        outs = [made(1, inner)] * high
-        return call(
-            functools.partial(time_kernel, groups),
-            2 * high * work,
+    def timed(groups, ks, *sources):
+        outs = [made(1, inner)] * len(ks)
+        return call(
+            functools.partial(time_kernel, groups, ks),
+            2 * len(ks) * work,
             in_specs=[full(source) for source in sources],
             out_specs=[full(out) for out in outs],
             out_shape=outs,
@@ -390,43 +406,39 @@
     def exchange(pieces, ks):
         return {k: permute(pieces[k], k) for k in ks}
 
-    heavy, light = order[:half], order[half:]
-    kv, normed, weight, gain, *xs = load(x)
+    kv, normed, keys, gain, tile = load(x)
     other = swap(kv)
-    q = ask(normed, weight)
-    outs = height(0, 0, xs[0], q, kv, other)
-    pieces = [dict(zip(heavy, outs)), {}]
-    arrived = [exchange(pieces[0], heavy), {}]
-    q, kv = project(half, after(xs[0], outs[0]), gain, weight)
+    q, queries = ask(normed)
+    pieces, arrived = [{}, {}], [{}, {}]
+    outs = height(half, 0, tile, q, kv, other)
+    pieces[0].update(zip(heavy, outs))
+    arrived[0].update(exchange(pieces[0], heavy))
+    q, kv, tile = project(0, light, after(x, outs[0]), gain, keys, queries)
     other = swap(kv)
-    q1, kv1 = project(0, after(xs[1], q), gain, weight)
+    q1, kv1, tile1 = project(1, order, after(x, q), gain, keys, queries)
     other1 = swap(kv1)
-    outs = height(half, 0, xs[0], after(q, q1), kv, other)
+    outs = height(half, 0, tile, after(q, q1), kv, other)
     pieces[0].update(zip(light, outs))
     arrived[0].update(exchange(pieces[0], light))
-    for name, ks, n in (("far", heavy, 0), ("near", light, half)):
+    for ks, at in ((heavy, 0), (light, half)):
         q1 = after(q1, outs[0])
-        outs = height(n, n * each, xs[1], q1, kv1, other1)
+        outs = height(half, at, tile1, q1, kv1, other1)
         pieces[1].update(zip(ks, outs))
         ready = dict(pieces[1])
-        if name == "far":
-            ready[half] = after(ready[half], arrived[0][half])
         arrived[1].update(exchange(ready, ks))
     last = outs[0]
-    plans = [[order], [[k for k in order if k != half], [half]]]
+    groups = [[order], [[k for k in order if k != half], [half]]]
     home, gates = [], []
     for c in range(CHUNKS):
         sources = []
-        for n, group in enumerate(plans[c]):
+        for group in groups[c]:
             got = after([arrived[c][k] for k in group], last)
             q, kv = time_project(got)
             sources += [q, kv, swap(kv)]
             last = q
-            if c and not n and LATE:
-                home[-1].update(exchange(after(mixes, q), LATE))
-        mixes = timed(plans[c], *sources)
+        mixes = timed(groups[c], order, *sources)
         last = mixes[0]
-        home.append(exchange(mixes, [k for k in order if c or k not in LATE]))
+        home.append(exchange(dict(zip(order, mixes)), order))
         if c + 1 < CHUNKS:
             last = gate(last)
             gates.append(last)

time: 84.6 us -> 86.5 us (1.022)
  Pallas kernels: 22.8 us -> 26.1 us
    pallas_call x10, Pallas kernels: 15.3 us -> 18.7 us  [the longest x4 6.88 us: height(): call(functools.partial(height_kernel, at, at * each), 2 * n * work, in_sp...]
    ppermute x6, waiting for transfers between devices: 1.33 us -> 0.09 us  [swap(): return lax.ppermute(a, 'space', [(0, 1), (1, 0)])]
  transfers between devices with their start and end apart: 22 -> 22, of which waited for: 8 -> 8; matrix products, arithmetic and copies ran while one was open for 0% -> 0% of each run, Pallas kernels for 14% -> 15%
where the time goes in v6:
time: 86.5 us; the launch traced here: 85.7 us
  starting transfers between devices  34.7 us (40%)
  Pallas kernels  26.1 us (30%)
  waiting for transfers between devices  24.4 us (28%)
    ppermute x16, starting transfers between devices, permute(): return lax.ppermute(piece, ('tm', 'space'), route(k))  30.8 us
    ppermute x16, waiting for transfers between devices, permute(): return lax.ppermute(piece, ('tm', 'space'), route(k))  24.3 us
    pallas_call x4, Pallas kernels, height(): call(functools.partial(height_kernel, at, at * each), 2 * n * work, in_sp...  6.88 us
    pallas_call x2, Pallas kernels, project(): call(functools.partial(project_kernel, c, ks, high), 3 * n * work, in_spe...  4.8 us
    ppermute x6, starting transfers between devices, swap(): return lax.ppermute(a, 'space', [(0, 1), (1, 0)])  3.88 us
    pallas_call x3, Pallas kernels, time_project(): call(time_project_kernel, 3 * n * work, in_specs=[full(piece) for piece i...  3.45 us
    pallas_call x2, Pallas kernels, finish(): call(functools.partial(finish_kernel, items, len(mixes), high), work * le...  3.45 us
    pallas_call x2, Pallas kernels, timed(): call(functools.partial(time_kernel, groups, ks), 2 * len(ks) * work, in_s...  2.82 us
  transfers between devices with their start and end apart: 22, of which 8 were waited for; matrix products, arithmetic and copies ran while one was open for 0% of the time, Pallas kernels for 15%

profile of v6, /device:TPU:1, one launch (start us, length us, event | category | flops | bytes accessed | tf_op | source)
XLA Modules:
  0.0 85.7 jit_solution(13986618586954133074)
XLA Ops:
  0.0 2.6 %shard_map.46 = (bf16[192,1024]{1,0:T(8,128)(2,1)S(1)}, bf16[192,1024]{1,0:T(8,128)(2,1)S(1)}, bf16[1024,1024]{1,0:T(8,128)(2,1)S(1)}, f32[2,1024]{1,0:T(2,128)S(1)}, bf16[2,12,8,1024]{3,2,1,0:T(8,128)(2,1)S(1)}) custom-call(bf16[12,64,1024]{2,1,0:T(8,128)(2,1)} %bitcast.4, f32[2,1024]{1,0:T(2,128)} %refs_1_.1, bf16[2,1024,1536]{2,1,0:T(8,128)(2,1)} %refs_2_.1), custom_call_target="tpu_custom_call" | custom-call | flops 402653184 | bytes 1572864 | tf_op jit(solution)/shard_map/pallas_call | solution.py:284
  2.7 1.6 %shard_map.47 = (bf16[192,512]{1,0:T(8,128)(2,1)S(1)}, bf16[1024,512]{1,0:T(8,128)(2,1)S(1)}) custom-call(bf16[192,1024]{1,0:T(8,128)(2,1)S(1)} %get-tuple-element.62.normed_ref, bf16[2,1024,1536]{2,1,0:T(8,128)(2,1)} %refs_2_.1), custom_call_target="tpu_custom_call" | custom-call | flops 201326592 | bytes 1572864 | tf_op jit(solution)/shard_map/pallas_call | solution.py:299
  4.4 1.6 %shard_map.48 = (bf16[96,1024]{1,0:T(8,128)(2,1)S(1)}, bf16[96,1024]{1,0:T(8,128)(2,1)S(1)}) custom-call(bf16[2,12,8,1024]{3,2,1,0:T(8,128)(2,1)S(1)} %get-tuple-element.61.x_ref, bf16[192,512]{1,0:T(8,128)(2,1)S(1)} %get-tuple-element.63.q_ref, bf16[192,1024]{1,0:T(8,128)(2,1)S(1)} %get-tuple-element.64.kv_ref, ...), custom_call_target="tpu_custom_call" | custom-call | flops 402653184 | bytes 1572864 | tf_op jit(solution)/shard_map/pallas_call | solution.py:322
  6.0 1.9 %shard_map.49 = (bf16[192,512]{1,0:T(8,128)(2,1)S(1)}, bf16[192,1024]{1,0:T(8,128)(2,1)S(1)}, bf16[2,12,8,1024]{3,2,1,0:T(8,128)(2,1)S(1)}) custom-call(bf16[12,64,1024]{2,1,0:T(8,128)(2,1)} %bitcast.5, f32[2,1024]{1,0:T(2,128)S(1)} %get-tuple-element.67.gain_ref, bf16[1024,1024]{1,0:T(8,128)(2,1)S(1)} %get-tuple-element.68.keys_ref, ...), custom_call_target="tpu_custom_call" | custom-call | flops 603979776 | bytes 1572864 | tf_op jit(solution)/shard_map/pallas_call | solution.py:311
  8.0 2.9 %shard_map.50 = (bf16[384,512]{1,0:T(8,128)(2,1)S(1)}, bf16[384,1024]{1,0:T(8,128)(2,1)S(1)}, bf16[4,12,8,1024]{3,2,1,0:T(8,128)(2,1)S(1)}) custom-call(bf16[12,64,1024]{2,1,0:T(8,128)(2,1)} %bitcast.6, f32[2,1024]{1,0:T(2,128)S(1)} %get-tuple-element.67.gain_ref, bf16[1024,1024]{1,0:T(8,128)(2,1)S(1)} %get-tuple-element.68.keys_ref, ...), custom_call_target="tpu_custom_call" | custom-call | flops 1207959552 | bytes 1572864 | tf_op jit(solution)/shard_map/pallas_call | solution.py:311
  11.4 4.7 %collective-permute-start.6 = (bf16[96,1024]{1,0:T(8,128)(2,1)S(1)}, bf16[96,1024]{1,0:T(8,128)(2,1)S(1)}, u32[]{:S(2)}, u32[]{:S(2)}) collective-permute-start(bf16[96,1024]{1,0:T(8,128)(2,1)S(1)} %get-tuple-element.110.refs_0_), channel_id=1, source_target_pairs={{0,14},{1,12},{2,15},{3,13},{4,10},{5,8},{6,11},{7,9},{8,5},{9,7},... | collective-permute-start | bytes 589832 | tf_op jit(solution)/shard_map/ppermute | solution.py:404
  16.1 1.8 %shard_map.51 = (bf16[96,1024]{1,0:T(8,128)(2,1)S(1)}, bf16[96,1024]{1,0:T(8,128)(2,1)S(1)}) custom-call(bf16[2,12,8,1024]{3,2,1,0:T(8,128)(2,1)S(1)} %get-tuple-element.74.x_ref, bf16[192,512]{1,0:T(8,128)(2,1)S(1)} %get-tuple-element.75.q_ref, bf16[192,1024]{1,0:T(8,128)(2,1)S(1)} %get-tuple-element.76.kv_ref, ...), custom_call_target="tpu_custom_call" | custom-call | flops 402653184 | bytes 1572864 | tf_op jit(solution)/shard_map/pallas_call | solution.py:322
  17.9 1.6 %collective-permute-start.8 = (bf16[96,1024]{1,0:T(8,128)(2,1)S(1)}, bf16[96,1024]{1,0:T(8,128)(2,1)S(1)}, u32[]{:S(2)}, u32[]{:S(2)}) collective-permute-start(bf16[96,1024]{1,0:T(8,128)(2,1)S(1)} %get-tuple-element.112.refs_2_), channel_id=1, source_target_pairs={{0,4},{1,6},{2,5},{3,7},{4,0},{5,2},{6,1},{7,3},{8,15},{9,13},{10,... | collective-permute-start | bytes 589832 | tf_op jit(solution)/shard_map/ppermute | solution.py:404
  19.5 2.2 %collective-permute-start.9 = (bf16[96,1024]{1,0:T(8,128)(2,1)S(1)}, bf16[96,1024]{1,0:T(8,128)(2,1)S(1)}, u32[]{:S(2)}, u32[]{:S(2)}) collective-permute-start(bf16[96,1024]{1,0:T(8,128)(2,1)S(1)} %get-tuple-element.113.refs_3_), channel_id=1, source_target_pairs={{0,0},{1,2},{2,1},{3,3},{4,4},{5,6},{6,5},{7,7},{8,11},{9,9},{10,1... | collective-permute-start | bytes 589832 | tf_op jit(solution)/shard_map/ppermute | solution.py:404
  21.7 1.8 %shard_map.52 = (bf16[96,1024]{1,0:T(8,128)(2,1)S(1)}, bf16[96,1024]{1,0:T(8,128)(2,1)S(1)}) custom-call(bf16[4,12,8,1024]{3,2,1,0:T(8,128)(2,1)S(1)} %get-tuple-element.72.x_ref, bf16[384,512]{1,0:T(8,128)(2,1)S(1)} %get-tuple-element.82.q_ref, bf16[384,1024]{1,0:T(8,128)(2,1)S(1)} %get-tuple-element.79.kv_ref, ...), custom_call_target="tpu_custom_call" | custom-call | flops 402653184 | bytes 1572864 | tf_op jit(solution)/shard_map/pallas_call | solution.py:322
  23.5 1.6 %shard_map.53 = (bf16[96,1024]{1,0:T(8,128)(2,1)S(1)}, bf16[96,1024]{1,0:T(8,128)(2,1)S(1)}) custom-call(bf16[4,12,8,1024]{3,2,1,0:T(8,128)(2,1)S(1)} %get-tuple-element.72.x_ref, bf16[384,512]{1,0:T(8,128)(2,1)S(1)} %get-tuple-element.82.q_ref, bf16[384,1024]{1,0:T(8,128)(2,1)S(1)} %get-tuple-element.79.kv_ref, ...), custom_call_target="tpu_custom_call" | custom-call | flops 402653184 | bytes 1572864 | tf_op jit(solution)/shard_map/pallas_call | solution.py:322
  25.2 8.4 %collective-permute-done.7.refs_1_ = bf16[96,1024]{1,0:T(8,128)(2,1)S(1)} collective-permute-done((bf16[96,1024]{1,0:T(8,128)(2,1)S(1)}, bf16[96,1024]{1,0:T(8,128)(2,1)S(1)}, u32[]{:S(2)}, u32[]{:S(2)}) %collective-permute-start.7) | collective-permute-done | bytes 196640 | tf_op jit(solution)/shard_map/ppermute | solution.py:404
  33.6 1.5 %shard_map.54 = (bf16[384,512]{1,0:T(8,128)(2,1)S(1)}, bf16[384,1024]{1,0:T(8,128)(2,1)S(1)}) custom-call(bf16[96,1024]{1,0:T(8,128)(2,1)S(1)} %collective-permute-done.6.refs_0_, bf16[96,1024]{1,0:T(8,128)(2,1)S(1)} %collective-permute-done.7.refs_1_, bf16[96,1024]{1,0:T(8,128)(2,1)S(1)} %collective-permute-done.8.refs_2_, ...), custom_call_target="tpu_custom_call" | custom-call | flops 1207959552 | bytes 1572864 | tf_op jit(solution)/shard_map/pallas_call | solution.py:349
  36.4 2.6 %collective-permute-start.5 = (bf16[96,1024]{1,0:T(8,128)(2,1)S(1)}, bf16[96,1024]{1,0:T(8,128)(2,1)S(1)}, u32[]{:S(2)}, u32[]{:S(2)}) collective-permute-start(bf16[96,1024]{1,0:T(8,128)(2,1)S(1)} %get-tuple-element.106.refs_3_), channel_id=1, source_target_pairs={{0,0},{1,2},{2,1},{3,3},{4,4},{5,6},{6,5},{7,7},{8,11},{9,9},{10,1... | collective-permute-start | bytes 589832 | tf_op jit(solution)/shard_map/ppermute | solution.py:404
  39.0 2.4 %collective-permute-start.3 = (bf16[96,1024]{1,0:T(8,128)(2,1)S(1)}, bf16[96,1024]{1,0:T(8,128)(2,1)S(1)}, u32[]{:S(2)}, u32[]{:S(2)}) collective-permute-start(bf16[96,1024]{1,0:T(8,128)(2,1)S(1)} %get-tuple-element.103.refs_0_), channel_id=1, source_target_pairs={{0,14},{1,12},{2,15},{3,13},{4,10},{5,8},{6,11},{7,9},{8,5},{9,7},... | collective-permute-start | bytes 589832 | tf_op jit(solution)/shard_map/ppermute | solution.py:404
  43.3 3.3 %collective-permute-done.5.refs_2_ = bf16[96,1024]{1,0:T(8,128)(2,1)S(1)} collective-permute-done((bf16[96,1024]{1,0:T(8,128)(2,1)S(1)}, bf16[96,1024]{1,0:T(8,128)(2,1)S(1)}, u32[]{:S(2)}, u32[]{:S(2)}) %collective-permute-start.5) | collective-permute-done | bytes 196640 | tf_op jit(solution)/shard_map/ppermute | solution.py:404
  48.2 1.5 %collective-permute-start.11 = (bf16[288,1024]{1,0:T(8,128)(2,1)S(1)}, bf16[288,1024]{1,0:T(8,128)(2,1)S(1)}, u32[]{:S(2)}, u32[]{:S(2)}) collective-permute-start(bf16[288,1024]{1,0:T(8,128)(2,1)S(1)} %get-tuple-element.98.refs_1_), channel_id=1, source_target_pairs={{0,1},{1,0},{2,3},{3,2},{4,5},{5,4},{6,7},{7,6},{8,9},{9,8},{10,11... | collective-permute-start | bytes 1769480 | tf_op jit(solution)/shard_map/ppermute | solution.py:391
  49.7 3.7 %collective-permute-start.12 = (bf16[96,1024]{1,0:T(8,128)(2,1)S(1)}, bf16[96,1024]{1,0:T(8,128)(2,1)S(1)}, u32[]{:S(2)}, u32[]{:S(2)}) collective-permute-start(bf16[96,1024]{1,0:T(8,128)(2,1)S(1)} %get-tuple-element.104.refs_1_), channel_id=1, source_target_pairs={{0,10},{1,8},{2,11},{3,9},{4,14},{5,12},{6,15},{7,13},{8,1},{9,3},... | collective-permute-start | bytes 589832 | tf_op jit(solution)/shard_map/ppermute | solution.py:404
  53.4 9.7 %collective-permute-done.12.refs_0_ = bf16[96,1024]{1,0:T(8,128)(2,1)S(1)} collective-permute-done((bf16[96,1024]{1,0:T(8,128)(2,1)S(1)}, bf16[96,1024]{1,0:T(8,128)(2,1)S(1)}, u32[]{:S(2)}, u32[]{:S(2)}) %collective-permute-start.12) | collective-permute-done | bytes 196640 | tf_op jit(solution)/shard_map/ppermute | solution.py:404
  65.7 2.8 %collective-permute-start.20 = (bf16[96,512]{1,0:T(8,128)(2,1)S(1)}, bf16[96,512]{1,0:T(8,128)(2,1)S(1)}, u32[]{:S(2)}, u32[]{:S(2)}) collective-permute-start(bf16[96,512]{1,0:T(8,128)(2,1)S(1)} %get-tuple-element.115), channel_id=1, source_target_pairs={{0,4},{1,6},{2,5},{3,7},{4,0},{5,2},{6,1},{7,3},{8,15},{9,13},{10,... | collective-permute-start | bytes 294920 | tf_op jit(solution)/shard_map/ppermute | solution.py:404
  68.5 3.1 %collective-permute-start.21 = (bf16[96,512]{1,0:T(8,128)(2,1)S(1)}, bf16[96,512]{1,0:T(8,128)(2,1)S(1)}, u32[]{:S(2)}, u32[]{:S(2)}) collective-permute-start(bf16[96,512]{1,0:T(8,128)(2,1)S(1)} %get-tuple-element.116), channel_id=1, source_target_pairs={{0,0},{1,2},{2,1},{3,3},{4,4},{5,6},{6,5},{7,7},{8,11},{9,9},{10,1... | collective-permute-start | bytes 294920 | tf_op jit(solution)/shard_map/ppermute | solution.py:404
  75.2 2.0 %collective-permute-start.16 = (bf16[96,512]{1,0:T(8,128)(2,1)S(1)}, bf16[96,512]{1,0:T(8,128)(2,1)S(1)}, u32[]{:S(2)}, u32[]{:S(2)}) collective-permute-start(bf16[96,512]{1,0:T(8,128)(2,1)S(1)} %get-tuple-element.108), channel_id=1, source_target_pairs={{0,4},{1,6},{2,5},{3,7},{4,0},{5,2},{6,1},{7,3},{8,15},{9,13},{10,... | collective-permute-start | bytes 294920 | tf_op jit(solution)/shard_map/ppermute | solution.py:404
  77.2 3.1 %collective-permute-start.17 = (bf16[96,512]{1,0:T(8,128)(2,1)S(1)}, bf16[96,512]{1,0:T(8,128)(2,1)S(1)}, u32[]{:S(2)}, u32[]{:S(2)}) collective-permute-start(bf16[96,512]{1,0:T(8,128)(2,1)S(1)} %get-tuple-element.109), channel_id=1, source_target_pairs={{0,0},{1,2},{2,1},{3,3},{4,4},{5,6},{6,5},{7,7},{8,11},{9,9},{10,1... | collective-permute-start | bytes 294920 | tf_op jit(solution)/shard_map/ppermute | solution.py:404
  80.3 2.0 %shard_map.59.refs_8_ = bf16[12,64,1024]{2,1,0:T(8,128)(2,1)} custom-call(bf16[2,512,1024]{2,1,0:T(8,128)(2,1)S(1)} %copy-done, bf16[96,1024]{1,0:T(8,128)(2,1)S(1)} %get-tuple-element.110.refs_0_, bf16[96,1024]{1,0:T(8,128)(2,1)S(1)} %get-tuple-element.111.refs_1_, bf16[96,1024]{1,0:T(8,128)(2,1)S(1)} %get-tuple-element.112.refs_2_, ...), custom_call_target="tpu_custom_call" | custom-call | flops 402653184 | bytes 1572864 | tf_op jit(solution)/shard_map/pallas_call | solution.py:369
  (45 shorter events, 14.8 us)
Async XLA Ops:
  2.6 1.8 %collective-permute-start = (bf16[192,1024]{1,0:T(8,128)(2,1)S(1)}, bf16[192,1024]{1,0:T(8,128)(2,1)S(1)}, u32[]{:S(2)}, u32[]{:S(2)}) collective-permute-start(bf16[192,1024]{1,0:T(8,128)(2,1)S(1)} %get-tuple-element.64.kv_ref), channel_id=1, source_target_pairs={{0,1},{1,0},{2,3},{3,2},{4,5},{5,4},{6,7},{7,6},{8,9},{9,8},{10,11... | collective-permute-start | bytes 1179656 | tf_op jit(solution)/shard_map/ppermute | solution.py:391
  10.8 10.9 %collective-permute-start.2 = (bf16[384,1024]{1,0:T(8,128)(2,1)S(1)}, bf16[384,1024]{1,0:T(8,128)(2,1)S(1)}, u32[]{:S(2)}, u32[]{:S(2)}) collective-permute-start(bf16[384,1024]{1,0:T(8,128)(2,1)S(1)} %get-tuple-element.79.kv_ref), channel_id=1, source_target_pairs={{0,1},{1,0},{2,3},{3,2},{4,5},{5,4},{6,7},{7,6},{8,9},{9,8},{10,11... | collective-permute-start | bytes 2359304 | tf_op jit(solution)/shard_map/ppermute | solution.py:391
  11.3 4.8 %collective-permute-start.1 = (bf16[192,1024]{1,0:T(8,128)(2,1)S(1)}, bf16[192,1024]{1,0:T(8,128)(2,1)S(1)}, u32[]{:S(2)}, u32[]{:S(2)}) collective-permute-start(bf16[192,1024]{1,0:T(8,128)(2,1)S(1)} %get-tuple-element.76.kv_ref), channel_id=1, source_target_pairs={{0,1},{1,0},{2,3},{3,2},{4,5},{5,4},{6,7},{7,6},{8,9},{9,8},{10,11... | collective-permute-start | bytes 1179656 | tf_op jit(solution)/shard_map/ppermute | solution.py:391
  11.4 13.8 %collective-permute-start.6 = (bf16[96,1024]{1,0:T(8,128)(2,1)S(1)}, bf16[96,1024]{1,0:T(8,128)(2,1)S(1)}, u32[]{:S(2)}, u32[]{:S(2)}) collective-permute-start(bf16[96,1024]{1,0:T(8,128)(2,1)S(1)} %get-tuple-element.110.refs_0_), channel_id=1, source_target_pairs={{0,14},{1,12},{2,15},{3,13},{4,10},{5,8},{6,11},{7,9},{8,5},{9,7},... | collective-permute-start | bytes 589832 | tf_op jit(solution)/shard_map/ppermute | solution.py:404
  16.1 17.5 %collective-permute-start.7 = (bf16[96,1024]{1,0:T(8,128)(2,1)S(1)}, bf16[96,1024]{1,0:T(8,128)(2,1)S(1)}, u32[]{:S(2)}, u32[]{:S(2)}) collective-permute-start(bf16[96,1024]{1,0:T(8,128)(2,1)S(1)} %get-tuple-element.111.refs_1_), channel_id=1, source_target_pairs={{0,10},{1,8},{2,11},{3,9},{4,14},{5,12},{6,15},{7,13},{8,1},{9,3},... | collective-permute-start | bytes 589832 | tf_op jit(solution)/shard_map/ppermute | solution.py:404
  16.1 17.5 %slice-start = ((s8[6291456]{0:T(1024)(128)(4,1)}), s8[4194304]{0:T(1024)(128)(4,1)S(1)}, s32[]{:S(2)}) async-start(s8[6291456]{0:T(1024)(128)(4,1)} %bitcast.2), calls=%async_computation | async-start | bytes 8388608
  17.9 15.7 %collective-permute-start.8 = (bf16[96,1024]{1,0:T(8,128)(2,1)S(1)}, bf16[96,1024]{1,0:T(8,128)(2,1)S(1)}, u32[]{:S(2)}, u32[]{:S(2)}) collective-permute-start(bf16[96,1024]{1,0:T(8,128)(2,1)S(1)} %get-tuple-element.112.refs_2_), channel_id=1, source_target_pairs={{0,4},{1,6},{2,5},{3,7},{4,0},{5,2},{6,1},{7,3},{8,15},{9,13},{10,... | collective-permute-start | bytes 589832 | tf_op jit(solution)/shard_map/ppermute | solution.py:404
  19.5 14.1 %collective-permute-start.9 = (bf16[96,1024]{1,0:T(8,128)(2,1)S(1)}, bf16[96,1024]{1,0:T(8,128)(2,1)S(1)}, u32[]{:S(2)}, u32[]{:S(2)}) collective-permute-start(bf16[96,1024]{1,0:T(8,128)(2,1)S(1)} %get-tuple-element.113.refs_3_), channel_id=1, source_target_pairs={{0,0},{1,2},{2,1},{3,3},{4,4},{5,6},{6,5},{7,7},{8,11},{9,9},{10,1... | collective-permute-start | bytes 589832 | tf_op jit(solution)/shard_map/ppermute | solution.py:404
  35.2 6.2 %collective-permute-start.10 = (bf16[384,1024]{1,0:T(8,128)(2,1)S(1)}, bf16[384,1024]{1,0:T(8,128)(2,1)S(1)}, u32[]{:S(2)}, u32[]{:S(2)}) collective-permute-start(bf16[384,1024]{1,0:T(8,128)(2,1)S(1)} %get-tuple-element.92.refs_1_), channel_id=1, source_target_pairs={{0,1},{1,0},{2,3},{3,2},{4,5},{5,4},{6,7},{7,6},{8,9},{9,8},{10,11... | collective-permute-start | bytes 2359304 | tf_op jit(solution)/shard_map/ppermute | solution.py:391
  36.4 7.0 %collective-permute-start.4 = (bf16[96,1024]{1,0:T(8,128)(2,1)S(1)}, bf16[96,1024]{1,0:T(8,128)(2,1)S(1)}, u32[]{:S(2)}, u32[]{:S(2)}) collective-permute-start(bf16[96,1024]{1,0:T(8,128)(2,1)S(1)} %get-tuple-element.105.refs_2_), channel_id=1, source_target_pairs={{0,4},{1,6},{2,5},{3,7},{4,0},{5,2},{6,1},{7,3},{8,15},{9,13},{10,... | collective-permute-start | bytes 589832 | tf_op jit(solution)/shard_map/ppermute | solution.py:404
  36.4 10.2 %collective-permute-start.5 = (bf16[96,1024]{1,0:T(8,128)(2,1)S(1)}, bf16[96,1024]{1,0:T(8,128)(2,1)S(1)}, u32[]{:S(2)}, u32[]{:S(2)}) collective-permute-start(bf16[96,1024]{1,0:T(8,128)(2,1)S(1)} %get-tuple-element.106.refs_3_), channel_id=1, source_target_pairs={{0,0},{1,2},{2,1},{3,3},{4,4},{5,6},{6,5},{7,7},{8,11},{9,9},{10,1... | collective-permute-start | bytes 589832 | tf_op jit(solution)/shard_map/ppermute | solution.py:404
  39.0 8.0 %collective-permute-start.3 = (bf16[96,1024]{1,0:T(8,128)(2,1)S(1)}, bf16[96,1024]{1,0:T(8,128)(2,1)S(1)}, u32[]{:S(2)}, u32[]{:S(2)}) collective-permute-start(bf16[96,1024]{1,0:T(8,128)(2,1)S(1)} %get-tuple-element.103.refs_0_), channel_id=1, source_target_pairs={{0,14},{1,12},{2,15},{3,13},{4,10},{5,8},{6,11},{7,9},{8,5},{9,7},... | collective-permute-start | bytes 589832 | tf_op jit(solution)/shard_map/ppermute | solution.py:404
  48.2 23.4 %collective-permute-start.11 = (bf16[288,1024]{1,0:T(8,128)(2,1)S(1)}, bf16[288,1024]{1,0:T(8,128)(2,1)S(1)}, u32[]{:S(2)}, u32[]{:S(2)}) collective-permute-start(bf16[288,1024]{1,0:T(8,128)(2,1)S(1)} %get-tuple-element.98.refs_1_), channel_id=1, source_target_pairs={{0,1},{1,0},{2,3},{3,2},{4,5},{5,4},{6,7},{7,6},{8,9},{9,8},{10,11... | collective-permute-start | bytes 1769480 | tf_op jit(solution)/shard_map/ppermute | solution.py:391
  49.7 13.4 %collective-permute-start.12 = (bf16[96,1024]{1,0:T(8,128)(2,1)S(1)}, bf16[96,1024]{1,0:T(8,128)(2,1)S(1)}, u32[]{:S(2)}, u32[]{:S(2)}) collective-permute-start(bf16[96,1024]{1,0:T(8,128)(2,1)S(1)} %get-tuple-element.104.refs_1_), channel_id=1, source_target_pairs={{0,10},{1,8},{2,11},{3,9},{4,14},{5,12},{6,15},{7,13},{8,1},{9,3},... | collective-permute-start | bytes 589832 | tf_op jit(solution)/shard_map/ppermute | solution.py:404
  63.9 16.5 %copy-start = (bf16[2,512,1024]{2,1,0:T(8,128)(2,1)S(1)}, bf16[2,512,1024]{2,1,0:T(8,128)(2,1)}, u32[]{:S(2)}) copy-start(bf16[2,512,1024]{2,1,0:T(8,128)(2,1)} %w_ref.15) | copy-start | bytes 6291460
  63.9 4.6 %collective-permute-start.13 = (bf16[96,1024]{1,0:T(8,128)(2,1)S(1)}, bf16[96,1024]{1,0:T(8,128)(2,1)S(1)}, u32[]{:S(2)}, u32[]{:S(2)}) collective-permute-start(bf16[96,1024]{1,0:T(8,128)(2,1)S(1)} %get-tuple-element.101.refs_4_), channel_id=1, source_target_pairs={{0,1},{1,0},{2,3},{3,2},{4,5},{5,4},{6,7},{7,6},{8,9},{9,8},{10,11... | collective-permute-start | bytes 589832 | tf_op jit(solution)/shard_map/ppermute | solution.py:391
  64.4 10.0 %collective-permute-start.18 = (bf16[96,512]{1,0:T(8,128)(2,1)S(1)}, bf16[96,512]{1,0:T(8,128)(2,1)S(1)}, u32[]{:S(2)}, u32[]{:S(2)}) collective-permute-start(bf16[96,512]{1,0:T(8,128)(2,1)S(1)} %get-tuple-element.93.in_ref), channel_id=1, source_target_pairs={{0,14},{1,12},{2,15},{3,13},{4,10},{5,8},{6,11},{7,9},{8,5},{9,7},... | collective-permute-start | bytes 294920 | tf_op jit(solution)/shard_map/ppermute | solution.py:404
  65.7 9.5 %collective-permute-start.19 = (bf16[96,512]{1,0:T(8,128)(2,1)S(1)}, bf16[96,512]{1,0:T(8,128)(2,1)S(1)}, u32[]{:S(2)}, u32[]{:S(2)}) collective-permute-start(bf16[96,512]{1,0:T(8,128)(2,1)S(1)} %get-tuple-element.114), channel_id=1, source_target_pairs={{0,10},{1,8},{2,11},{3,9},{4,14},{5,12},{6,15},{7,13},{8,1},{9,3},... | collective-permute-start | bytes 294920 | tf_op jit(solution)/shard_map/ppermute | solution.py:404
  65.7 11.5 %collective-permute-start.20 = (bf16[96,512]{1,0:T(8,128)(2,1)S(1)}, bf16[96,512]{1,0:T(8,128)(2,1)S(1)}, u32[]{:S(2)}, u32[]{:S(2)}) collective-permute-start(bf16[96,512]{1,0:T(8,128)(2,1)S(1)} %get-tuple-element.115), channel_id=1, source_target_pairs={{0,4},{1,6},{2,5},{3,7},{4,0},{5,2},{6,1},{7,3},{8,15},{9,13},{10,... | collective-permute-start | bytes 294920 | tf_op jit(solution)/shard_map/ppermute | solution.py:404
  68.5 11.8 %collective-permute-start.21 = (bf16[96,512]{1,0:T(8,128)(2,1)S(1)}, bf16[96,512]{1,0:T(8,128)(2,1)S(1)}, u32[]{:S(2)}, u32[]{:S(2)}) collective-permute-start(bf16[96,512]{1,0:T(8,128)(2,1)S(1)} %get-tuple-element.116), channel_id=1, source_target_pairs={{0,0},{1,2},{2,1},{3,3},{4,4},{5,6},{6,5},{7,7},{8,11},{9,9},{10,1... | collective-permute-start | bytes 294920 | tf_op jit(solution)/shard_map/ppermute | solution.py:404
  73.0 9.3 %collective-permute-start.14 = (bf16[96,512]{1,0:T(8,128)(2,1)S(1)}, bf16[96,512]{1,0:T(8,128)(2,1)S(1)}, u32[]{:S(2)}, u32[]{:S(2)}) collective-permute-start(bf16[96,512]{1,0:T(8,128)(2,1)S(1)} %get-tuple-element.102), channel_id=1, source_target_pairs={{0,14},{1,12},{2,15},{3,13},{4,10},{5,8},{6,11},{7,9},{8,5},{9,7},... | collective-permute-start | bytes 294920 | tf_op jit(solution)/shard_map/ppermute | solution.py:404
  74.4 9.2 %collective-permute-start.15 = (bf16[96,512]{1,0:T(8,128)(2,1)S(1)}, bf16[96,512]{1,0:T(8,128)(2,1)S(1)}, u32[]{:S(2)}, u32[]{:S(2)}) collective-permute-start(bf16[96,512]{1,0:T(8,128)(2,1)S(1)} %get-tuple-element.107), channel_id=1, source_target_pairs={{0,10},{1,8},{2,11},{3,9},{4,14},{5,12},{6,15},{7,13},{8,1},{9,3},... | collective-permute-start | bytes 294920 | tf_op jit(solution)/shard_map/ppermute | solution.py:404
  75.2 8.4 %collective-permute-start.16 = (bf16[96,512]{1,0:T(8,128)(2,1)S(1)}, bf16[96,512]{1,0:T(8,128)(2,1)S(1)}, u32[]{:S(2)}, u32[]{:S(2)}) collective-permute-start(bf16[96,512]{1,0:T(8,128)(2,1)S(1)} %get-tuple-element.108), channel_id=1, source_target_pairs={{0,4},{1,6},{2,5},{3,7},{4,0},{5,2},{6,1},{7,3},{8,15},{9,13},{10,... | collective-permute-start | bytes 294920 | tf_op jit(solution)/shard_map/ppermute | solution.py:404
  77.2 6.9 %collective-permute-start.17 = (bf16[96,512]{1,0:T(8,128)(2,1)S(1)}, bf16[96,512]{1,0:T(8,128)(2,1)S(1)}, u32[]{:S(2)}, u32[]{:S(2)}) collective-permute-start(bf16[96,512]{1,0:T(8,128)(2,1)S(1)} %get-tuple-element.109), channel_id=1, source_target_pairs={{0,0},{1,2},{2,1},{3,3},{4,4},{5,6},{6,5},{7,7},{8,11},{9,9},{10,1... | collective-permute-start | bytes 294920 | tf_op jit(solution)/shard_map/ppermute | solution.py:404
  (2 other events, 22.0 us)

commit v7 on v6

--- a/solution.py
+++ b/solution.py
@@ -171,7 +171,7 @@
 
 
 def gate_kernel(in_ref, out_ref):
-    out_ref[0] = 0
+    pass
 
 
 def time_kernel(groups, ks, *refs):
@@ -223,7 +223,6 @@
         copy.wait()
 
 
-SMEM = pl.BlockSpec(memory_space=pltpu.SMEM)
 HBM = pl.BlockSpec(memory_space=pltpu.HBM)
 
 
@@ -336,8 +335,8 @@
         return pl.pallas_call(
             gate_kernel,
             in_specs=[pl.BlockSpec(memory_space=pl.ANY)],
-            out_specs=SMEM,
-            out_shape=jax.ShapeDtypeStruct((1,), jnp.int32),
+            out_specs=pl.BlockSpec(memory_space=pl.ANY),
+            out_shape=jax.ShapeDtypeStruct((8, 128), jnp.float32),
             compiler_params=params(),
             cost_estimate=cost(1, 8),
             name="gate",
@@ -431,14 +430,16 @@
     home, gates = [], []
     for c in range(CHUNKS):
         sources = []
-        for group in groups[c]:
+        for n, group in enumerate(groups[c]):
             got = after([arrived[c][k] for k in group], last)
             q, kv = time_project(got)
             sources += [q, kv, swap(kv)]
             last = q
-        mixes = timed(groups[c], order, *sources)
-        last = mixes[0]
-        home.append(exchange(dict(zip(order, mixes)), order))
+            if c and not n:
+                home[0].update(exchange(after({half: mixes[half]}, q), [half]))
+        outs = timed(groups[c], order, *sources)
+        last, mixes = outs[0], dict(zip(order, outs))
+        home.append(exchange(mixes, [k for k in order if c or k != half]))
         if c + 1 < CHUNKS:
             last = gate(last)
             gates.append(last)

time: 86.5 us -> 86.4 us (level)
  Pallas kernels: 26.1 us -> 25 us
  transfers between devices with their start and end apart: 22 -> 22, of which waited for: 8 -> 7; matrix products, arithmetic and copies ran while one was open for 0% -> 0% of each run, Pallas kernels for 15% -> 14%
where the time goes in v7:
time: 86.4 us; the launch traced here: 85.3 us
  starting transfers between devices  35.2 us (41%)
  Pallas kernels  25 us (29%)
  waiting for transfers between devices  24.6 us (28%)
    ppermute x16, starting transfers between devices, permute(): return lax.ppermute(piece, ('tm', 'space'), route(k))  31.3 us
    ppermute x16, waiting for transfers between devices, permute(): return lax.ppermute(piece, ('tm', 'space'), route(k))  24.6 us
    pallas_call x4, Pallas kernels, height(): call(functools.partial(height_kernel, at, at * each), 2 * n * work, in_sp...  6.88 us
    pallas_call x2, Pallas kernels, project(): call(functools.partial(project_kernel, c, ks, high), 3 * n * work, in_spe...  4.8 us
    ppermute x6, starting transfers between devices, swap(): return lax.ppermute(a, 'space', [(0, 1), (1, 0)])  3.88 us
    pallas_call x3, Pallas kernels, time_project(): call(time_project_kernel, 3 * n * work, in_specs=[full(piece) for piece i...  3.45 us
    pallas_call x2, Pallas kernels, finish(): call(functools.partial(finish_kernel, items, len(mixes), high), work * le...  2.83 us
    pallas_call x2, Pallas kernels, timed(): call(functools.partial(time_kernel, groups, ks), 2 * len(ks) * work, in_s...  2.82 us
  transfers between devices with their start and end apart: 22, of which 7 were waited for; matrix products, arithmetic and copies ran while one was open for 0% of the time, Pallas kernels for 14%

profile of v7, /device:TPU:1, one launch (start us, length us, event | category | flops | bytes accessed | tf_op | source)
XLA Modules:
  0.0 85.3 jit_solution(17252295226509009390)
XLA Ops:
  0.0 2.6 %shard_map.46 = (bf16[192,1024]{1,0:T(8,128)(2,1)S(1)}, bf16[192,1024]{1,0:T(8,128)(2,1)S(1)}, bf16[1024,1024]{1,0:T(8,128)(2,1)S(1)}, f32[2,1024]{1,0:T(2,128)S(1)}, bf16[2,12,8,1024]{3,2,1,0:T(8,128)(2,1)S(1)}) custom-call(bf16[12,64,1024]{2,1,0:T(8,128)(2,1)} %bitcast.4, f32[2,1024]{1,0:T(2,128)} %refs_1_.1, bf16[2,1024,1536]{2,1,0:T(8,128)(2,1)} %refs_2_.1), custom_call_target="tpu_custom_call" | custom-call | flops 402653184 | bytes 1572864 | tf_op jit(solution)/shard_map/pallas_call | solution.py:283
  2.7 1.6 %shard_map.47 = (bf16[192,512]{1,0:T(8,128)(2,1)S(1)}, bf16[1024,512]{1,0:T(8,128)(2,1)S(1)}) custom-call(bf16[192,1024]{1,0:T(8,128)(2,1)S(1)} %get-tuple-element.63.normed_ref, bf16[2,1024,1536]{2,1,0:T(8,128)(2,1)} %refs_2_.1), custom_call_target="tpu_custom_call" | custom-call | flops 201326592 | bytes 1572864 | tf_op jit(solution)/shard_map/pallas_call | solution.py:298
  4.4 1.6 %shard_map.48 = (bf16[96,1024]{1,0:T(8,128)(2,1)S(1)}, bf16[96,1024]{1,0:T(8,128)(2,1)S(1)}) custom-call(bf16[2,12,8,1024]{3,2,1,0:T(8,128)(2,1)S(1)} %get-tuple-element.62.x_ref, bf16[192,512]{1,0:T(8,128)(2,1)S(1)} %get-tuple-element.64.q_ref, bf16[192,1024]{1,0:T(8,128)(2,1)S(1)} %get-tuple-element.65.kv_ref, ...), custom_call_target="tpu_custom_call" | custom-call | flops 402653184 | bytes 1572864 | tf_op jit(solution)/shard_map/pallas_call | solution.py:321
  6.0 1.9 %shard_map.49 = (bf16[192,512]{1,0:T(8,128)(2,1)S(1)}, bf16[192,1024]{1,0:T(8,128)(2,1)S(1)}, bf16[2,12,8,1024]{3,2,1,0:T(8,128)(2,1)S(1)}) custom-call(bf16[12,64,1024]{2,1,0:T(8,128)(2,1)} %bitcast.5, f32[2,1024]{1,0:T(2,128)S(1)} %get-tuple-element.68.gain_ref, bf16[1024,1024]{1,0:T(8,128)(2,1)S(1)} %get-tuple-element.69.keys_ref, ...), custom_call_target="tpu_custom_call" | custom-call | flops 603979776 | bytes 1572864 | tf_op jit(solution)/shard_map/pallas_call | solution.py:310
  8.0 2.9 %shard_map.50 = (bf16[384,512]{1,0:T(8,128)(2,1)S(1)}, bf16[384,1024]{1,0:T(8,128)(2,1)S(1)}, bf16[4,12,8,1024]{3,2,1,0:T(8,128)(2,1)S(1)}) custom-call(bf16[12,64,1024]{2,1,0:T(8,128)(2,1)} %bitcast.6, f32[2,1024]{1,0:T(2,128)S(1)} %get-tuple-element.68.gain_ref, bf16[1024,1024]{1,0:T(8,128)(2,1)S(1)} %get-tuple-element.69.keys_ref, ...), custom_call_target="tpu_custom_call" | custom-call | flops 1207959552 | bytes 1572864 | tf_op jit(solution)/shard_map/pallas_call | solution.py:310
  11.4 4.7 %collective-permute-start.6 = (bf16[96,1024]{1,0:T(8,128)(2,1)S(1)}, bf16[96,1024]{1,0:T(8,128)(2,1)S(1)}, u32[]{:S(2)}, u32[]{:S(2)}) collective-permute-start(bf16[96,1024]{1,0:T(8,128)(2,1)S(1)} %get-tuple-element.111.refs_0_), channel_id=1, source_target_pairs={{0,14},{1,12},{2,15},{3,13},{4,10},{5,8},{6,11},{7,9},{8,5},{9,7},... | collective-permute-start | bytes 589832 | tf_op jit(solution)/shard_map/ppermute | solution.py:403
  16.1 1.8 %shard_map.51 = (bf16[96,1024]{1,0:T(8,128)(2,1)S(1)}, bf16[96,1024]{1,0:T(8,128)(2,1)S(1)}) custom-call(bf16[2,12,8,1024]{3,2,1,0:T(8,128)(2,1)S(1)} %get-tuple-element.75.x_ref, bf16[192,512]{1,0:T(8,128)(2,1)S(1)} %get-tuple-element.76.q_ref, bf16[192,1024]{1,0:T(8,128)(2,1)S(1)} %get-tuple-element.77.kv_ref, ...), custom_call_target="tpu_custom_call" | custom-call | flops 402653184 | bytes 1572864 | tf_op jit(solution)/shard_map/pallas_call | solution.py:321
  17.9 1.6 %collective-permute-start.8 = (bf16[96,1024]{1,0:T(8,128)(2,1)S(1)}, bf16[96,1024]{1,0:T(8,128)(2,1)S(1)}, u32[]{:S(2)}, u32[]{:S(2)}) collective-permute-start(bf16[96,1024]{1,0:T(8,128)(2,1)S(1)} %get-tuple-element.113.refs_2_), channel_id=1, source_target_pairs={{0,4},{1,6},{2,5},{3,7},{4,0},{5,2},{6,1},{7,3},{8,15},{9,13},{10,... | collective-permute-start | bytes 589832 | tf_op jit(solution)/shard_map/ppermute | solution.py:403
  19.5 2.2 %collective-permute-start.9 = (bf16[96,1024]{1,0:T(8,128)(2,1)S(1)}, bf16[96,1024]{1,0:T(8,128)(2,1)S(1)}, u32[]{:S(2)}, u32[]{:S(2)}) collective-permute-start(bf16[96,1024]{1,0:T(8,128)(2,1)S(1)} %get-tuple-element.114.refs_3_), channel_id=1, source_target_pairs={{0,0},{1,2},{2,1},{3,3},{4,4},{5,6},{6,5},{7,7},{8,11},{9,9},{10,1... | collective-permute-start | bytes 589832 | tf_op jit(solution)/shard_map/ppermute | solution.py:403
  21.7 1.8 %shard_map.52 = (bf16[96,1024]{1,0:T(8,128)(2,1)S(1)}, bf16[96,1024]{1,0:T(8,128)(2,1)S(1)}) custom-call(bf16[4,12,8,1024]{3,2,1,0:T(8,128)(2,1)S(1)} %get-tuple-element.73.x_ref, bf16[384,512]{1,0:T(8,128)(2,1)S(1)} %get-tuple-element.83.q_ref, bf16[384,1024]{1,0:T(8,128)(2,1)S(1)} %get-tuple-element.80.kv_ref, ...), custom_call_target="tpu_custom_call" | custom-call | flops 402653184 | bytes 1572864 | tf_op jit(solution)/shard_map/pallas_call | solution.py:321
  23.5 1.6 %shard_map.53 = (bf16[96,1024]{1,0:T(8,128)(2,1)S(1)}, bf16[96,1024]{1,0:T(8,128)(2,1)S(1)}) custom-call(bf16[4,12,8,1024]{3,2,1,0:T(8,128)(2,1)S(1)} %get-tuple-element.73.x_ref, bf16[384,512]{1,0:T(8,128)(2,1)S(1)} %get-tuple-element.83.q_ref, bf16[384,1024]{1,0:T(8,128)(2,1)S(1)} %get-tuple-element.80.kv_ref, ...), custom_call_target="tpu_custom_call" | custom-call | flops 402653184 | bytes 1572864 | tf_op jit(solution)/shard_map/pallas_call | solution.py:321
  25.2 8.4 %collective-permute-done.7.refs_1_ = bf16[96,1024]{1,0:T(8,128)(2,1)S(1)} collective-permute-done((bf16[96,1024]{1,0:T(8,128)(2,1)S(1)}, bf16[96,1024]{1,0:T(8,128)(2,1)S(1)}, u32[]{:S(2)}, u32[]{:S(2)}) %collective-permute-start.7) | collective-permute-done | bytes 196640 | tf_op jit(solution)/shard_map/ppermute | solution.py:403
  33.6 1.5 %shard_map.54 = (bf16[384,512]{1,0:T(8,128)(2,1)S(1)}, bf16[384,1024]{1,0:T(8,128)(2,1)S(1)}) custom-call(bf16[96,1024]{1,0:T(8,128)(2,1)S(1)} %collective-permute-done.6.refs_0_, bf16[96,1024]{1,0:T(8,128)(2,1)S(1)} %collective-permute-done.7.refs_1_, bf16[96,1024]{1,0:T(8,128)(2,1)S(1)} %collective-permute-done.8.refs_2_, ...), custom_call_target="tpu_custom_call" | custom-call | flops 1207959552 | bytes 1572864 | tf_op jit(solution)/shard_map/pallas_call | solution.py:348
  36.4 2.6 %collective-permute-start.5 = (bf16[96,1024]{1,0:T(8,128)(2,1)S(1)}, bf16[96,1024]{1,0:T(8,128)(2,1)S(1)}, u32[]{:S(2)}, u32[]{:S(2)}) collective-permute-start(bf16[96,1024]{1,0:T(8,128)(2,1)S(1)} %get-tuple-element.107.refs_3_), channel_id=1, source_target_pairs={{0,0},{1,2},{2,1},{3,3},{4,4},{5,6},{6,5},{7,7},{8,11},{9,9},{10,1... | collective-permute-start | bytes 589832 | tf_op jit(solution)/shard_map/ppermute | solution.py:403
  39.0 2.4 %collective-permute-start.3 = (bf16[96,1024]{1,0:T(8,128)(2,1)S(1)}, bf16[96,1024]{1,0:T(8,128)(2,1)S(1)}, u32[]{:S(2)}, u32[]{:S(2)}) collective-permute-start(bf16[96,1024]{1,0:T(8,128)(2,1)S(1)} %get-tuple-element.104.refs_0_), channel_id=1, source_target_pairs={{0,14},{1,12},{2,15},{3,13},{4,10},{5,8},{6,11},{7,9},{8,5},{9,7},... | collective-permute-start | bytes 589832 | tf_op jit(solution)/shard_map/ppermute | solution.py:403
  43.0 3.6 %collective-permute-done.5.refs_2_ = bf16[96,1024]{1,0:T(8,128)(2,1)S(1)} collective-permute-done((bf16[96,1024]{1,0:T(8,128)(2,1)S(1)}, bf16[96,1024]{1,0:T(8,128)(2,1)S(1)}, u32[]{:S(2)}, u32[]{:S(2)}) %collective-permute-start.5) | collective-permute-done | bytes 196640 | tf_op jit(solution)/shard_map/ppermute | solution.py:403
  48.2 1.5 %collective-permute-start.11 = (bf16[288,1024]{1,0:T(8,128)(2,1)S(1)}, bf16[288,1024]{1,0:T(8,128)(2,1)S(1)}, u32[]{:S(2)}, u32[]{:S(2)}) collective-permute-start(bf16[288,1024]{1,0:T(8,128)(2,1)S(1)} %get-tuple-element.99.refs_1_), channel_id=1, source_target_pairs={{0,1},{1,0},{2,3},{3,2},{4,5},{5,4},{6,7},{7,6},{8,9},{9,8},{10,11... | collective-permute-start | bytes 1769480 | tf_op jit(solution)/shard_map/ppermute | solution.py:390
  49.7 3.7 %collective-permute-start.12 = (bf16[96,1024]{1,0:T(8,128)(2,1)S(1)}, bf16[96,1024]{1,0:T(8,128)(2,1)S(1)}, u32[]{:S(2)}, u32[]{:S(2)}) collective-permute-start(bf16[96,1024]{1,0:T(8,128)(2,1)S(1)} %get-tuple-element.105.refs_1_), channel_id=1, source_target_pairs={{0,10},{1,8},{2,11},{3,9},{4,14},{5,12},{6,15},{7,13},{8,1},{9,3},... | collective-permute-start | bytes 589832 | tf_op jit(solution)/shard_map/ppermute | solution.py:403
  53.4 9.7 %collective-permute-done.12.refs_0_ = bf16[96,1024]{1,0:T(8,128)(2,1)S(1)} collective-permute-done((bf16[96,1024]{1,0:T(8,128)(2,1)S(1)}, bf16[96,1024]{1,0:T(8,128)(2,1)S(1)}, u32[]{:S(2)}, u32[]{:S(2)}) %collective-permute-start.12) | collective-permute-done | bytes 196640 | tf_op jit(solution)/shard_map/ppermute | solution.py:403
  65.7 1.9 %collective-permute-start.20 = (bf16[96,512]{1,0:T(8,128)(2,1)S(1)}, bf16[96,512]{1,0:T(8,128)(2,1)S(1)}, u32[]{:S(2)}, u32[]{:S(2)}) collective-permute-start(bf16[96,512]{1,0:T(8,128)(2,1)S(1)} %get-tuple-element.117), channel_id=1, source_target_pairs={{0,4},{1,6},{2,5},{3,7},{4,0},{5,2},{6,1},{7,3},{8,15},{9,13},{10,... | collective-permute-start | bytes 294920 | tf_op jit(solution)/shard_map/ppermute | solution.py:403
  67.6 3.1 %collective-permute-start.21 = (bf16[96,512]{1,0:T(8,128)(2,1)S(1)}, bf16[96,512]{1,0:T(8,128)(2,1)S(1)}, u32[]{:S(2)}, u32[]{:S(2)}) collective-permute-start(bf16[96,512]{1,0:T(8,128)(2,1)S(1)} %get-tuple-element.118), channel_id=1, source_target_pairs={{0,0},{1,2},{2,1},{3,3},{4,4},{5,6},{6,5},{7,7},{8,11},{9,9},{10,1... | collective-permute-start | bytes 294920 | tf_op jit(solution)/shard_map/ppermute | solution.py:403
  73.5 2.8 %collective-permute-start.16 = (bf16[96,512]{1,0:T(8,128)(2,1)S(1)}, bf16[96,512]{1,0:T(8,128)(2,1)S(1)}, u32[]{:S(2)}, u32[]{:S(2)}) collective-permute-start(bf16[96,512]{1,0:T(8,128)(2,1)S(1)} %get-tuple-element.109), channel_id=1, source_target_pairs={{0,4},{1,6},{2,5},{3,7},{4,0},{5,2},{6,1},{7,3},{8,15},{9,13},{10,... | collective-permute-start | bytes 294920 | tf_op jit(solution)/shard_map/ppermute | solution.py:403
  76.3 3.7 %collective-permute-start.17 = (bf16[96,512]{1,0:T(8,128)(2,1)S(1)}, bf16[96,512]{1,0:T(8,128)(2,1)S(1)}, u32[]{:S(2)}, u32[]{:S(2)}) collective-permute-start(bf16[96,512]{1,0:T(8,128)(2,1)S(1)} %get-tuple-element.110), channel_id=1, source_target_pairs={{0,0},{1,2},{2,1},{3,3},{4,4},{5,6},{6,5},{7,7},{8,11},{9,9},{10,1... | collective-permute-start | bytes 294920 | tf_op jit(solution)/shard_map/ppermute | solution.py:403
  81.5 2.2 %collective-permute-done.15.refs_5_ = bf16[96,512]{1,0:T(8,128)(2,1)S(1)} collective-permute-done((bf16[96,512]{1,0:T(8,128)(2,1)S(1)}, bf16[96,512]{1,0:T(8,128)(2,1)S(1)}, u32[]{:S(2)}, u32[]{:S(2)}) %collective-permute-start.15) | collective-permute-done | bytes 98336 | tf_op jit(solution)/shard_map/ppermute | solution.py:403
  (45 shorter events, 13.4 us)
Async XLA Ops:
  2.6 1.8 %collective-permute-start = (bf16[192,1024]{1,0:T(8,128)(2,1)S(1)}, bf16[192,1024]{1,0:T(8,128)(2,1)S(1)}, u32[]{:S(2)}, u32[]{:S(2)}) collective-permute-start(bf16[192,1024]{1,0:T(8,128)(2,1)S(1)} %get-tuple-element.65.kv_ref), channel_id=1, source_target_pairs={{0,1},{1,0},{2,3},{3,2},{4,5},{5,4},{6,7},{7,6},{8,9},{9,8},{10,11... | collective-permute-start | bytes 1179656 | tf_op jit(solution)/shard_map/ppermute | solution.py:390
  10.8 10.9 %collective-permute-start.2 = (bf16[384,1024]{1,0:T(8,128)(2,1)S(1)}, bf16[384,1024]{1,0:T(8,128)(2,1)S(1)}, u32[]{:S(2)}, u32[]{:S(2)}) collective-permute-start(bf16[384,1024]{1,0:T(8,128)(2,1)S(1)} %get-tuple-element.80.kv_ref), channel_id=1, source_target_pairs={{0,1},{1,0},{2,3},{3,2},{4,5},{5,4},{6,7},{7,6},{8,9},{9,8},{10,11... | collective-permute-start | bytes 2359304 | tf_op jit(solution)/shard_map/ppermute | solution.py:390
  11.3 4.8 %collective-permute-start.1 = (bf16[192,1024]{1,0:T(8,128)(2,1)S(1)}, bf16[192,1024]{1,0:T(8,128)(2,1)S(1)}, u32[]{:S(2)}, u32[]{:S(2)}) collective-permute-start(bf16[192,1024]{1,0:T(8,128)(2,1)S(1)} %get-tuple-element.77.kv_ref), channel_id=1, source_target_pairs={{0,1},{1,0},{2,3},{3,2},{4,5},{5,4},{6,7},{7,6},{8,9},{9,8},{10,11... | collective-permute-start | bytes 1179656 | tf_op jit(solution)/shard_map/ppermute | solution.py:390
  11.4 13.8 %collective-permute-start.6 = (bf16[96,1024]{1,0:T(8,128)(2,1)S(1)}, bf16[96,1024]{1,0:T(8,128)(2,1)S(1)}, u32[]{:S(2)}, u32[]{:S(2)}) collective-permute-start(bf16[96,1024]{1,0:T(8,128)(2,1)S(1)} %get-tuple-element.111.refs_0_), channel_id=1, source_target_pairs={{0,14},{1,12},{2,15},{3,13},{4,10},{5,8},{6,11},{7,9},{8,5},{9,7},... | collective-permute-start | bytes 589832 | tf_op jit(solution)/shard_map/ppermute | solution.py:403
  16.1 17.5 %collective-permute-start.7 = (bf16[96,1024]{1,0:T(8,128)(2,1)S(1)}, bf16[96,1024]{1,0:T(8,128)(2,1)S(1)}, u32[]{:S(2)}, u32[]{:S(2)}) collective-permute-start(bf16[96,1024]{1,0:T(8,128)(2,1)S(1)} %get-tuple-element.112.refs_1_), channel_id=1, source_target_pairs={{0,10},{1,8},{2,11},{3,9},{4,14},{5,12},{6,15},{7,13},{8,1},{9,3},... | collective-permute-start | bytes 589832 | tf_op jit(solution)/shard_map/ppermute | solution.py:403
  16.1 17.5 %slice-start = ((s8[6291456]{0:T(1024)(128)(4,1)}), s8[4194304]{0:T(1024)(128)(4,1)S(1)}, s32[]{:S(2)}) async-start(s8[6291456]{0:T(1024)(128)(4,1)} %bitcast.2), calls=%async_computation | async-start | bytes 8388608
  17.9 15.7 %collective-permute-start.8 = (bf16[96,1024]{1,0:T(8,128)(2,1)S(1)}, bf16[96,1024]{1,0:T(8,128)(2,1)S(1)}, u32[]{:S(2)}, u32[]{:S(2)}) collective-permute-start(bf16[96,1024]{1,0:T(8,128)(2,1)S(1)} %get-tuple-element.113.refs_2_), channel_id=1, source_target_pairs={{0,4},{1,6},{2,5},{3,7},{4,0},{5,2},{6,1},{7,3},{8,15},{9,13},{10,... | collective-permute-start | bytes 589832 | tf_op jit(solution)/shard_map/ppermute | solution.py:403
  19.5 14.1 %collective-permute-start.9 = (bf16[96,1024]{1,0:T(8,128)(2,1)S(1)}, bf16[96,1024]{1,0:T(8,128)(2,1)S(1)}, u32[]{:S(2)}, u32[]{:S(2)}) collective-permute-start(bf16[96,1024]{1,0:T(8,128)(2,1)S(1)} %get-tuple-element.114.refs_3_), channel_id=1, source_target_pairs={{0,0},{1,2},{2,1},{3,3},{4,4},{5,6},{6,5},{7,7},{8,11},{9,9},{10,1... | collective-permute-start | bytes 589832 | tf_op jit(solution)/shard_map/ppermute | solution.py:403
  35.2 6.2 %collective-permute-start.10 = (bf16[384,1024]{1,0:T(8,128)(2,1)S(1)}, bf16[384,1024]{1,0:T(8,128)(2,1)S(1)}, u32[]{:S(2)}, u32[]{:S(2)}) collective-permute-start(bf16[384,1024]{1,0:T(8,128)(2,1)S(1)} %get-tuple-element.93.refs_1_), channel_id=1, source_target_pairs={{0,1},{1,0},{2,3},{3,2},{4,5},{5,4},{6,7},{7,6},{8,9},{9,8},{10,11... | collective-permute-start | bytes 2359304 | tf_op jit(solution)/shard_map/ppermute | solution.py:390
  36.4 6.7 %collective-permute-start.4 = (bf16[96,1024]{1,0:T(8,128)(2,1)S(1)}, bf16[96,1024]{1,0:T(8,128)(2,1)S(1)}, u32[]{:S(2)}, u32[]{:S(2)}) collective-permute-start(bf16[96,1024]{1,0:T(8,128)(2,1)S(1)} %get-tuple-element.106.refs_2_), channel_id=1, source_target_pairs={{0,4},{1,6},{2,5},{3,7},{4,0},{5,2},{6,1},{7,3},{8,15},{9,13},{10,... | collective-permute-start | bytes 589832 | tf_op jit(solution)/shard_map/ppermute | solution.py:403
  36.4 10.2 %collective-permute-start.5 = (bf16[96,1024]{1,0:T(8,128)(2,1)S(1)}, bf16[96,1024]{1,0:T(8,128)(2,1)S(1)}, u32[]{:S(2)}, u32[]{:S(2)}) collective-permute-start(bf16[96,1024]{1,0:T(8,128)(2,1)S(1)} %get-tuple-element.107.refs_3_), channel_id=1, source_target_pairs={{0,0},{1,2},{2,1},{3,3},{4,4},{5,6},{6,5},{7,7},{8,11},{9,9},{10,1... | collective-permute-start | bytes 589832 | tf_op jit(solution)/shard_map/ppermute | solution.py:403
  39.0 8.0 %collective-permute-start.3 = (bf16[96,1024]{1,0:T(8,128)(2,1)S(1)}, bf16[96,1024]{1,0:T(8,128)(2,1)S(1)}, u32[]{:S(2)}, u32[]{:S(2)}) collective-permute-start(bf16[96,1024]{1,0:T(8,128)(2,1)S(1)} %get-tuple-element.104.refs_0_), channel_id=1, source_target_pairs={{0,14},{1,12},{2,15},{3,13},{4,10},{5,8},{6,11},{7,9},{8,5},{9,7},... | collective-permute-start | bytes 589832 | tf_op jit(solution)/shard_map/ppermute | solution.py:403
  48.2 22.5 %collective-permute-start.11 = (bf16[288,1024]{1,0:T(8,128)(2,1)S(1)}, bf16[288,1024]{1,0:T(8,128)(2,1)S(1)}, u32[]{:S(2)}, u32[]{:S(2)}) collective-permute-start(bf16[288,1024]{1,0:T(8,128)(2,1)S(1)} %get-tuple-element.99.refs_1_), channel_id=1, source_target_pairs={{0,1},{1,0},{2,3},{3,2},{4,5},{5,4},{6,7},{7,6},{8,9},{9,8},{10,11... | collective-permute-start | bytes 1769480 | tf_op jit(solution)/shard_map/ppermute | solution.py:390
  49.7 13.4 %collective-permute-start.12 = (bf16[96,1024]{1,0:T(8,128)(2,1)S(1)}, bf16[96,1024]{1,0:T(8,128)(2,1)S(1)}, u32[]{:S(2)}, u32[]{:S(2)}) collective-permute-start(bf16[96,1024]{1,0:T(8,128)(2,1)S(1)} %get-tuple-element.105.refs_1_), channel_id=1, source_target_pairs={{0,10},{1,8},{2,11},{3,9},{4,14},{5,12},{6,15},{7,13},{8,1},{9,3},... | collective-permute-start | bytes 589832 | tf_op jit(solution)/shard_map/ppermute | solution.py:403
  63.9 16.2 %copy-start = (bf16[2,512,1024]{2,1,0:T(8,128)(2,1)S(1)}, bf16[2,512,1024]{2,1,0:T(8,128)(2,1)}, u32[]{:S(2)}) copy-start(bf16[2,512,1024]{2,1,0:T(8,128)(2,1)} %w_ref.15) | copy-start | bytes 6291460
  63.9 3.7 %collective-permute-start.13 = (bf16[96,1024]{1,0:T(8,128)(2,1)S(1)}, bf16[96,1024]{1,0:T(8,128)(2,1)S(1)}, u32[]{:S(2)}, u32[]{:S(2)}) collective-permute-start(bf16[96,1024]{1,0:T(8,128)(2,1)S(1)} %get-tuple-element.102.refs_4_), channel_id=1, source_target_pairs={{0,1},{1,0},{2,3},{3,2},{4,5},{5,4},{6,7},{7,6},{8,9},{9,8},{10,11... | collective-permute-start | bytes 589832 | tf_op jit(solution)/shard_map/ppermute | solution.py:390
  64.4 9.1 %collective-permute-start.19 = (bf16[96,512]{1,0:T(8,128)(2,1)S(1)}, bf16[96,512]{1,0:T(8,128)(2,1)S(1)}, u32[]{:S(2)}, u32[]{:S(2)}) collective-permute-start(bf16[96,512]{1,0:T(8,128)(2,1)S(1)} %get-tuple-element.116), channel_id=1, source_target_pairs={{0,10},{1,8},{2,11},{3,9},{4,14},{5,12},{6,15},{7,13},{8,1},{9,3},... | collective-permute-start | bytes 294920 | tf_op jit(solution)/shard_map/ppermute | solution.py:403
  64.4 9.1 %collective-permute-start.18 = (bf16[96,512]{1,0:T(8,128)(2,1)S(1)}, bf16[96,512]{1,0:T(8,128)(2,1)S(1)}, u32[]{:S(2)}, u32[]{:S(2)}) collective-permute-start(bf16[96,512]{1,0:T(8,128)(2,1)S(1)} %get-tuple-element.94.in_ref), channel_id=1, source_target_pairs={{0,14},{1,12},{2,15},{3,13},{4,10},{5,8},{6,11},{7,9},{8,5},{9,7},... | collective-permute-start | bytes 294920 | tf_op jit(solution)/shard_map/ppermute | solution.py:403
  65.7 10.6 %collective-permute-start.20 = (bf16[96,512]{1,0:T(8,128)(2,1)S(1)}, bf16[96,512]{1,0:T(8,128)(2,1)S(1)}, u32[]{:S(2)}, u32[]{:S(2)}) collective-permute-start(bf16[96,512]{1,0:T(8,128)(2,1)S(1)} %get-tuple-element.117), channel_id=1, source_target_pairs={{0,4},{1,6},{2,5},{3,7},{4,0},{5,2},{6,1},{7,3},{8,15},{9,13},{10,... | collective-permute-start | bytes 294920 | tf_op jit(solution)/shard_map/ppermute | solution.py:403
  67.6 12.4 %collective-permute-start.21 = (bf16[96,512]{1,0:T(8,128)(2,1)S(1)}, bf16[96,512]{1,0:T(8,128)(2,1)S(1)}, u32[]{:S(2)}, u32[]{:S(2)}) collective-permute-start(bf16[96,512]{1,0:T(8,128)(2,1)S(1)} %get-tuple-element.118), channel_id=1, source_target_pairs={{0,0},{1,2},{2,1},{3,3},{4,4},{5,6},{6,5},{7,7},{8,11},{9,9},{10,1... | collective-permute-start | bytes 294920 | tf_op jit(solution)/shard_map/ppermute | solution.py:403
  72.1 9.3 %collective-permute-start.14 = (bf16[96,512]{1,0:T(8,128)(2,1)S(1)}, bf16[96,512]{1,0:T(8,128)(2,1)S(1)}, u32[]{:S(2)}, u32[]{:S(2)}) collective-permute-start(bf16[96,512]{1,0:T(8,128)(2,1)S(1)} %get-tuple-element.103), channel_id=1, source_target_pairs={{0,14},{1,12},{2,15},{3,13},{4,10},{5,8},{6,11},{7,9},{8,5},{9,7},... | collective-permute-start | bytes 294920 | tf_op jit(solution)/shard_map/ppermute | solution.py:403
  73.5 10.2 %collective-permute-start.15 = (bf16[96,512]{1,0:T(8,128)(2,1)S(1)}, bf16[96,512]{1,0:T(8,128)(2,1)S(1)}, u32[]{:S(2)}, u32[]{:S(2)}) collective-permute-start(bf16[96,512]{1,0:T(8,128)(2,1)S(1)} %get-tuple-element.108), channel_id=1, source_target_pairs={{0,10},{1,8},{2,11},{3,9},{4,14},{5,12},{6,15},{7,13},{8,1},{9,3},... | collective-permute-start | bytes 294920 | tf_op jit(solution)/shard_map/ppermute | solution.py:403
  73.5 10.2 %collective-permute-start.16 = (bf16[96,512]{1,0:T(8,128)(2,1)S(1)}, bf16[96,512]{1,0:T(8,128)(2,1)S(1)}, u32[]{:S(2)}, u32[]{:S(2)}) collective-permute-start(bf16[96,512]{1,0:T(8,128)(2,1)S(1)} %get-tuple-element.109), channel_id=1, source_target_pairs={{0,4},{1,6},{2,5},{3,7},{4,0},{5,2},{6,1},{7,3},{8,15},{9,13},{10,... | collective-permute-start | bytes 294920 | tf_op jit(solution)/shard_map/ppermute | solution.py:403
  76.3 7.4 %collective-permute-start.17 = (bf16[96,512]{1,0:T(8,128)(2,1)S(1)}, bf16[96,512]{1,0:T(8,128)(2,1)S(1)}, u32[]{:S(2)}, u32[]{:S(2)}) collective-permute-start(bf16[96,512]{1,0:T(8,128)(2,1)S(1)} %get-tuple-element.110), channel_id=1, source_target_pairs={{0,0},{1,2},{2,1},{3,3},{4,4},{5,6},{6,5},{7,7},{8,11},{9,9},{10,1... | collective-permute-start | bytes 294920 | tf_op jit(solution)/shard_map/ppermute | solution.py:403
  (2 other events, 22.0 us)

commit v8 on v7

--- a/solution.py
+++ b/solution.py
@@ -13,7 +13,7 @@
 QUAD = 4
 CHUNKS = 2
 COLB = 8
-SPLIT = 2
+SPLIT = 1
 POSB = 16
 NEG = -1e30
 VMEM_BYTES = 16 * 1024 * 1024
@@ -34,7 +34,7 @@
     return jnp.where(left == right, 0.0, NEG)
 
 
-def attend_quad(query, key, value, bias):
+def attend_quad(query, key, value, bias, early):
     rows, width = query.shape
     keys = key.shape[0]
     lanes = lax.broadcasted_iota(jnp.int32, (rows, width), 1) // HEAD
@@ -46,9 +46,13 @@
     )
     scores = scores.reshape(heads * rows // bias.shape[1], bias.shape[1], keys) + bias
     raised = jnp.exp(scores - jnp.max(scores, axis=-1, keepdims=True))
-    total = jnp.sum(raised, axis=-1, keepdims=True).reshape(heads * rows, 1)
+    share = 1.0 / jnp.sum(raised, axis=-1, keepdims=True)
+    if early:
+        raised = raised * share
     raised = raised.reshape(heads * rows, keys).astype(jnp.bfloat16)
-    mixed = jnp.dot(raised, value, preferred_element_type=jnp.float32) * (1.0 / total)
+    mixed = jnp.dot(raised, value, preferred_element_type=jnp.float32)
+    if not early:
+        mixed = mixed * share.reshape(heads * rows, 1)
     out = mixed[:rows]
     for h in range(1, heads):
         out = jnp.where(lanes == h, mixed[h * rows : (h + 1) * rows], out)
@@ -153,7 +157,7 @@
             key = join([kv_ref[span, here], other_ref[span, here]])
             value = join([kv_ref[span, there], other_ref[span, there]])
             mix_ref[i * per : (i + 1) * per, here] = attend_quad(
-                q_ref[span, here], key, value, bias
+                q_ref[span, here], key, value, bias, True
             )
     fetch.wait()
     update = jnp.dot(mix_ref[...], w_buf[...], preferred_element_type=jnp.float32)
@@ -194,7 +198,7 @@
             key = join(rows(1, p, lo) + rows(2, p, lo))
             value = join(rows(1, p, inner + lo) + rows(2, p, inner + lo))
             asking = [entry for k in ks for entry in flat if entry[2] == k]
-            out = attend_quad(join(rows(0, p, lo, asking)), key, value, bias)
+            out = attend_quad(join(rows(0, p, lo, asking)), key, value, bias, False)
             for n, ref in enumerate(mix_refs):
                 ref[p : p + POSB, lo : lo + width] = out[n * POSB : (n + 1) * POSB]
 

time: 86.4 us -> 86.4 us (level)
  no operation moved by 1% of the time
where the time goes in v8:
time: 86.4 us; the launch traced here: 85.3 us
  starting transfers between devices  35.1 us (41%)
  Pallas kernels  25.3 us (29%)
  waiting for transfers between devices  24.5 us (28%)
    ppermute x16, starting transfers between devices, permute(): return lax.ppermute(piece, ('tm', 'space'), route(k))  31.3 us
    ppermute x16, waiting for transfers between devices, permute(): return lax.ppermute(piece, ('tm', 'space'), route(k))  24.4 us
    pallas_call x4, Pallas kernels, height(): call(functools.partial(height_kernel, at, at * each), 2 * n * work, in_sp...  7.31 us
    pallas_call x2, Pallas kernels, project(): call(functools.partial(project_kernel, c, ks, high), 3 * n * work, in_spe...  4.81 us
    ppermute x6, starting transfers between devices, swap(): return lax.ppermute(a, 'space', [(0, 1), (1, 0)])  3.78 us
    pallas_call x3, Pallas kernels, time_project(): call(time_project_kernel, 3 * n * work, in_specs=[full(piece) for piece i...  3.45 us
    pallas_call x2, Pallas kernels, finish(): call(functools.partial(finish_kernel, items, len(mixes), high), work * le...  2.83 us
    pallas_call x2, Pallas kernels, timed(): call(functools.partial(time_kernel, groups, ks), 2 * len(ks) * work, in_s...  2.82 us
  transfers between devices with their start and end apart: 22, of which 7 were waited for; matrix products, arithmetic and copies ran while one was open for 0% of the time, Pallas kernels for 14%

profile of v8, /device:TPU:1, one launch (start us, length us, event | category | flops | bytes accessed | tf_op | source)
XLA Modules:
  0.0 85.3 jit_solution(6076493646872148582)
XLA Ops:
  0.0 2.5 %shard_map.46 = (bf16[192,1024]{1,0:T(8,128)(2,1)S(1)}, bf16[192,1024]{1,0:T(8,128)(2,1)S(1)}, bf16[1024,1024]{1,0:T(8,128)(2,1)S(1)}, f32[2,1024]{1,0:T(2,128)S(1)}, bf16[2,12,8,1024]{3,2,1,0:T(8,128)(2,1)S(1)}) custom-call(bf16[12,64,1024]{2,1,0:T(8,128)(2,1)} %bitcast.4, f32[2,1024]{1,0:T(2,128)} %refs_1_.1, bf16[2,1024,1536]{2,1,0:T(8,128)(2,1)} %refs_2_.1), custom_call_target="tpu_custom_call" | custom-call | flops 402653184 | bytes 1572864 | tf_op jit(solution)/shard_map/pallas_call | solution.py:287
  2.6 1.6 %shard_map.47 = (bf16[192,512]{1,0:T(8,128)(2,1)S(1)}, bf16[1024,512]{1,0:T(8,128)(2,1)S(1)}) custom-call(bf16[192,1024]{1,0:T(8,128)(2,1)S(1)} %get-tuple-element.63.normed_ref, bf16[2,1024,1536]{2,1,0:T(8,128)(2,1)} %refs_2_.1), custom_call_target="tpu_custom_call" | custom-call | flops 201326592 | bytes 1572864 | tf_op jit(solution)/shard_map/pallas_call | solution.py:302
  4.3 1.8 %shard_map.48 = (bf16[96,1024]{1,0:T(8,128)(2,1)S(1)}, bf16[96,1024]{1,0:T(8,128)(2,1)S(1)}) custom-call(bf16[2,12,8,1024]{3,2,1,0:T(8,128)(2,1)S(1)} %get-tuple-element.62.x_ref, bf16[192,512]{1,0:T(8,128)(2,1)S(1)} %get-tuple-element.64.q_ref, bf16[192,1024]{1,0:T(8,128)(2,1)S(1)} %get-tuple-element.65.kv_ref, ...), custom_call_target="tpu_custom_call" | custom-call | flops 402653184 | bytes 1572864 | tf_op jit(solution)/shard_map/pallas_call | solution.py:325
  6.1 1.9 %shard_map.49 = (bf16[192,512]{1,0:T(8,128)(2,1)S(1)}, bf16[192,1024]{1,0:T(8,128)(2,1)S(1)}, bf16[2,12,8,1024]{3,2,1,0:T(8,128)(2,1)S(1)}) custom-call(bf16[12,64,1024]{2,1,0:T(8,128)(2,1)} %bitcast.5, f32[2,1024]{1,0:T(2,128)S(1)} %get-tuple-element.68.gain_ref, bf16[1024,1024]{1,0:T(8,128)(2,1)S(1)} %get-tuple-element.69.keys_ref, ...), custom_call_target="tpu_custom_call" | custom-call | flops 603979776 | bytes 1572864 | tf_op jit(solution)/shard_map/pallas_call | solution.py:314
  8.1 2.9 %shard_map.50 = (bf16[384,512]{1,0:T(8,128)(2,1)S(1)}, bf16[384,1024]{1,0:T(8,128)(2,1)S(1)}, bf16[4,12,8,1024]{3,2,1,0:T(8,128)(2,1)S(1)}) custom-call(bf16[12,64,1024]{2,1,0:T(8,128)(2,1)} %bitcast.6, f32[2,1024]{1,0:T(2,128)S(1)} %get-tuple-element.68.gain_ref, bf16[1024,1024]{1,0:T(8,128)(2,1)S(1)} %get-tuple-element.69.keys_ref, ...), custom_call_target="tpu_custom_call" | custom-call | flops 1207959552 | bytes 1572864 | tf_op jit(solution)/shard_map/pallas_call | solution.py:314
  11.5 4.7 %collective-permute-start.6 = (bf16[96,1024]{1,0:T(8,128)(2,1)S(1)}, bf16[96,1024]{1,0:T(8,128)(2,1)S(1)}, u32[]{:S(2)}, u32[]{:S(2)}) collective-permute-start(bf16[96,1024]{1,0:T(8,128)(2,1)S(1)} %get-tuple-element.111.refs_0_), channel_id=1, source_target_pairs={{0,14},{1,12},{2,15},{3,13},{4,10},{5,8},{6,11},{7,9},{8,5},{9,7},... | collective-permute-start | bytes 589832 | tf_op jit(solution)/shard_map/ppermute | solution.py:407
  16.2 1.8 %shard_map.51 = (bf16[96,1024]{1,0:T(8,128)(2,1)S(1)}, bf16[96,1024]{1,0:T(8,128)(2,1)S(1)}) custom-call(bf16[2,12,8,1024]{3,2,1,0:T(8,128)(2,1)S(1)} %get-tuple-element.75.x_ref, bf16[192,512]{1,0:T(8,128)(2,1)S(1)} %get-tuple-element.76.q_ref, bf16[192,1024]{1,0:T(8,128)(2,1)S(1)} %get-tuple-element.77.kv_ref, ...), custom_call_target="tpu_custom_call" | custom-call | flops 402653184 | bytes 1572864 | tf_op jit(solution)/shard_map/pallas_call | solution.py:325
  18.1 1.6 %collective-permute-start.8 = (bf16[96,1024]{1,0:T(8,128)(2,1)S(1)}, bf16[96,1024]{1,0:T(8,128)(2,1)S(1)}, u32[]{:S(2)}, u32[]{:S(2)}) collective-permute-start(bf16[96,1024]{1,0:T(8,128)(2,1)S(1)} %get-tuple-element.113.refs_2_), channel_id=1, source_target_pairs={{0,4},{1,6},{2,5},{3,7},{4,0},{5,2},{6,1},{7,3},{8,15},{9,13},{10,... | collective-permute-start | bytes 589832 | tf_op jit(solution)/shard_map/ppermute | solution.py:407
  19.6 2.2 %collective-permute-start.9 = (bf16[96,1024]{1,0:T(8,128)(2,1)S(1)}, bf16[96,1024]{1,0:T(8,128)(2,1)S(1)}, u32[]{:S(2)}, u32[]{:S(2)}) collective-permute-start(bf16[96,1024]{1,0:T(8,128)(2,1)S(1)} %get-tuple-element.114.refs_3_), channel_id=1, source_target_pairs={{0,0},{1,2},{2,1},{3,3},{4,4},{5,6},{6,5},{7,7},{8,11},{9,9},{10,1... | collective-permute-start | bytes 589832 | tf_op jit(solution)/shard_map/ppermute | solution.py:407
  21.8 1.8 %shard_map.52 = (bf16[96,1024]{1,0:T(8,128)(2,1)S(1)}, bf16[96,1024]{1,0:T(8,128)(2,1)S(1)}) custom-call(bf16[4,12,8,1024]{3,2,1,0:T(8,128)(2,1)S(1)} %get-tuple-element.73.x_ref, bf16[384,512]{1,0:T(8,128)(2,1)S(1)} %get-tuple-element.83.q_ref, bf16[384,1024]{1,0:T(8,128)(2,1)S(1)} %get-tuple-element.80.kv_ref, ...), custom_call_target="tpu_custom_call" | custom-call | flops 402653184 | bytes 1572864 | tf_op jit(solution)/shard_map/pallas_call | solution.py:325
  23.7 1.8 %shard_map.53 = (bf16[96,1024]{1,0:T(8,128)(2,1)S(1)}, bf16[96,1024]{1,0:T(8,128)(2,1)S(1)}) custom-call(bf16[4,12,8,1024]{3,2,1,0:T(8,128)(2,1)S(1)} %get-tuple-element.73.x_ref, bf16[384,512]{1,0:T(8,128)(2,1)S(1)} %get-tuple-element.83.q_ref, bf16[384,1024]{1,0:T(8,128)(2,1)S(1)} %get-tuple-element.80.kv_ref, ...), custom_call_target="tpu_custom_call" | custom-call | flops 402653184 | bytes 1572864 | tf_op jit(solution)/shard_map/pallas_call | solution.py:325
  25.5 8.2 %collective-permute-done.7.refs_1_ = bf16[96,1024]{1,0:T(8,128)(2,1)S(1)} collective-permute-done((bf16[96,1024]{1,0:T(8,128)(2,1)S(1)}, bf16[96,1024]{1,0:T(8,128)(2,1)S(1)}, u32[]{:S(2)}, u32[]{:S(2)}) %collective-permute-start.7) | collective-permute-done | bytes 196640 | tf_op jit(solution)/shard_map/ppermute | solution.py:407
  33.8 1.5 %shard_map.54 = (bf16[384,512]{1,0:T(8,128)(2,1)S(1)}, bf16[384,1024]{1,0:T(8,128)(2,1)S(1)}) custom-call(bf16[96,1024]{1,0:T(8,128)(2,1)S(1)} %collective-permute-done.6.refs_0_, bf16[96,1024]{1,0:T(8,128)(2,1)S(1)} %collective-permute-done.7.refs_1_, bf16[96,1024]{1,0:T(8,128)(2,1)S(1)} %collective-permute-done.8.refs_2_, ...), custom_call_target="tpu_custom_call" | custom-call | flops 1207959552 | bytes 1572864 | tf_op jit(solution)/shard_map/pallas_call | solution.py:352
  36.4 2.7 %collective-permute-start.5 = (bf16[96,1024]{1,0:T(8,128)(2,1)S(1)}, bf16[96,1024]{1,0:T(8,128)(2,1)S(1)}, u32[]{:S(2)}, u32[]{:S(2)}) collective-permute-start(bf16[96,1024]{1,0:T(8,128)(2,1)S(1)} %get-tuple-element.107.refs_3_), channel_id=1, source_target_pairs={{0,0},{1,2},{2,1},{3,3},{4,4},{5,6},{6,5},{7,7},{8,11},{9,9},{10,1... | collective-permute-start | bytes 589832 | tf_op jit(solution)/shard_map/ppermute | solution.py:407
  39.1 2.4 %collective-permute-start.3 = (bf16[96,1024]{1,0:T(8,128)(2,1)S(1)}, bf16[96,1024]{1,0:T(8,128)(2,1)S(1)}, u32[]{:S(2)}, u32[]{:S(2)}) collective-permute-start(bf16[96,1024]{1,0:T(8,128)(2,1)S(1)} %get-tuple-element.104.refs_0_), channel_id=1, source_target_pairs={{0,14},{1,12},{2,15},{3,13},{4,10},{5,8},{6,11},{7,9},{8,5},{9,7},... | collective-permute-start | bytes 589832 | tf_op jit(solution)/shard_map/ppermute | solution.py:407
  43.1 3.5 %collective-permute-done.5.refs_2_ = bf16[96,1024]{1,0:T(8,128)(2,1)S(1)} collective-permute-done((bf16[96,1024]{1,0:T(8,128)(2,1)S(1)}, bf16[96,1024]{1,0:T(8,128)(2,1)S(1)}, u32[]{:S(2)}, u32[]{:S(2)}) %collective-permute-start.5) | collective-permute-done | bytes 196640 | tf_op jit(solution)/shard_map/ppermute | solution.py:407
  48.4 1.5 %collective-permute-start.11 = (bf16[288,1024]{1,0:T(8,128)(2,1)S(1)}, bf16[288,1024]{1,0:T(8,128)(2,1)S(1)}, u32[]{:S(2)}, u32[]{:S(2)}) collective-permute-start(bf16[288,1024]{1,0:T(8,128)(2,1)S(1)} %get-tuple-element.99.refs_1_), channel_id=1, source_target_pairs={{0,1},{1,0},{2,3},{3,2},{4,5},{5,4},{6,7},{7,6},{8,9},{9,8},{10,11... | collective-permute-start | bytes 1769480 | tf_op jit(solution)/shard_map/ppermute | solution.py:394
  49.9 3.7 %collective-permute-start.12 = (bf16[96,1024]{1,0:T(8,128)(2,1)S(1)}, bf16[96,1024]{1,0:T(8,128)(2,1)S(1)}, u32[]{:S(2)}, u32[]{:S(2)}) collective-permute-start(bf16[96,1024]{1,0:T(8,128)(2,1)S(1)} %get-tuple-element.105.refs_1_), channel_id=1, source_target_pairs={{0,10},{1,8},{2,11},{3,9},{4,14},{5,12},{6,15},{7,13},{8,1},{9,3},... | collective-permute-start | bytes 589832 | tf_op jit(solution)/shard_map/ppermute | solution.py:407
  53.5 9.7 %collective-permute-done.12.refs_0_ = bf16[96,1024]{1,0:T(8,128)(2,1)S(1)} collective-permute-done((bf16[96,1024]{1,0:T(8,128)(2,1)S(1)}, bf16[96,1024]{1,0:T(8,128)(2,1)S(1)}, u32[]{:S(2)}, u32[]{:S(2)}) %collective-permute-start.12) | collective-permute-done | bytes 196640 | tf_op jit(solution)/shard_map/ppermute | solution.py:407
  65.8 1.9 %collective-permute-start.20 = (bf16[96,512]{1,0:T(8,128)(2,1)S(1)}, bf16[96,512]{1,0:T(8,128)(2,1)S(1)}, u32[]{:S(2)}, u32[]{:S(2)}) collective-permute-start(bf16[96,512]{1,0:T(8,128)(2,1)S(1)} %get-tuple-element.117), channel_id=1, source_target_pairs={{0,4},{1,6},{2,5},{3,7},{4,0},{5,2},{6,1},{7,3},{8,15},{9,13},{10,... | collective-permute-start | bytes 294920 | tf_op jit(solution)/shard_map/ppermute | solution.py:407
  67.7 3.1 %collective-permute-start.21 = (bf16[96,512]{1,0:T(8,128)(2,1)S(1)}, bf16[96,512]{1,0:T(8,128)(2,1)S(1)}, u32[]{:S(2)}, u32[]{:S(2)}) collective-permute-start(bf16[96,512]{1,0:T(8,128)(2,1)S(1)} %get-tuple-element.118), channel_id=1, source_target_pairs={{0,0},{1,2},{2,1},{3,3},{4,4},{5,6},{6,5},{7,7},{8,11},{9,9},{10,1... | collective-permute-start | bytes 294920 | tf_op jit(solution)/shard_map/ppermute | solution.py:407
  73.6 2.8 %collective-permute-start.16 = (bf16[96,512]{1,0:T(8,128)(2,1)S(1)}, bf16[96,512]{1,0:T(8,128)(2,1)S(1)}, u32[]{:S(2)}, u32[]{:S(2)}) collective-permute-start(bf16[96,512]{1,0:T(8,128)(2,1)S(1)} %get-tuple-element.109), channel_id=1, source_target_pairs={{0,4},{1,6},{2,5},{3,7},{4,0},{5,2},{6,1},{7,3},{8,15},{9,13},{10,... | collective-permute-start | bytes 294920 | tf_op jit(solution)/shard_map/ppermute | solution.py:407
  76.4 3.7 %collective-permute-start.17 = (bf16[96,512]{1,0:T(8,128)(2,1)S(1)}, bf16[96,512]{1,0:T(8,128)(2,1)S(1)}, u32[]{:S(2)}, u32[]{:S(2)}) collective-permute-start(bf16[96,512]{1,0:T(8,128)(2,1)S(1)} %get-tuple-element.110), channel_id=1, source_target_pairs={{0,0},{1,2},{2,1},{3,3},{4,4},{5,6},{6,5},{7,7},{8,11},{9,9},{10,1... | collective-permute-start | bytes 294920 | tf_op jit(solution)/shard_map/ppermute | solution.py:407
  81.5 2.2 %collective-permute-done.15.refs_5_ = bf16[96,512]{1,0:T(8,128)(2,1)S(1)} collective-permute-done((bf16[96,512]{1,0:T(8,128)(2,1)S(1)}, bf16[96,512]{1,0:T(8,128)(2,1)S(1)}, u32[]{:S(2)}, u32[]{:S(2)}) %collective-permute-start.15) | collective-permute-done | bytes 98336 | tf_op jit(solution)/shard_map/ppermute | solution.py:407
  (45 shorter events, 13.4 us)
Async XLA Ops:
  2.5 1.8 %collective-permute-start = (bf16[192,1024]{1,0:T(8,128)(2,1)S(1)}, bf16[192,1024]{1,0:T(8,128)(2,1)S(1)}, u32[]{:S(2)}, u32[]{:S(2)}) collective-permute-start(bf16[192,1024]{1,0:T(8,128)(2,1)S(1)} %get-tuple-element.65.kv_ref), channel_id=1, source_target_pairs={{0,1},{1,0},{2,3},{3,2},{4,5},{5,4},{6,7},{7,6},{8,9},{9,8},{10,11... | collective-permute-start | bytes 1179656 | tf_op jit(solution)/shard_map/ppermute | solution.py:394
  10.9 10.9 %collective-permute-start.2 = (bf16[384,1024]{1,0:T(8,128)(2,1)S(1)}, bf16[384,1024]{1,0:T(8,128)(2,1)S(1)}, u32[]{:S(2)}, u32[]{:S(2)}) collective-permute-start(bf16[384,1024]{1,0:T(8,128)(2,1)S(1)} %get-tuple-element.80.kv_ref), channel_id=1, source_target_pairs={{0,1},{1,0},{2,3},{3,2},{4,5},{5,4},{6,7},{7,6},{8,9},{9,8},{10,11... | collective-permute-start | bytes 2359304 | tf_op jit(solution)/shard_map/ppermute | solution.py:394
  11.4 4.8 %collective-permute-start.1 = (bf16[192,1024]{1,0:T(8,128)(2,1)S(1)}, bf16[192,1024]{1,0:T(8,128)(2,1)S(1)}, u32[]{:S(2)}, u32[]{:S(2)}) collective-permute-start(bf16[192,1024]{1,0:T(8,128)(2,1)S(1)} %get-tuple-element.77.kv_ref), channel_id=1, source_target_pairs={{0,1},{1,0},{2,3},{3,2},{4,5},{5,4},{6,7},{7,6},{8,9},{9,8},{10,11... | collective-permute-start | bytes 1179656 | tf_op jit(solution)/shard_map/ppermute | solution.py:394
  11.5 14.0 %collective-permute-start.6 = (bf16[96,1024]{1,0:T(8,128)(2,1)S(1)}, bf16[96,1024]{1,0:T(8,128)(2,1)S(1)}, u32[]{:S(2)}, u32[]{:S(2)}) collective-permute-start(bf16[96,1024]{1,0:T(8,128)(2,1)S(1)} %get-tuple-element.111.refs_0_), channel_id=1, source_target_pairs={{0,14},{1,12},{2,15},{3,13},{4,10},{5,8},{6,11},{7,9},{8,5},{9,7},... | collective-permute-start | bytes 589832 | tf_op jit(solution)/shard_map/ppermute | solution.py:407
  16.2 17.5 %collective-permute-start.7 = (bf16[96,1024]{1,0:T(8,128)(2,1)S(1)}, bf16[96,1024]{1,0:T(8,128)(2,1)S(1)}, u32[]{:S(2)}, u32[]{:S(2)}) collective-permute-start(bf16[96,1024]{1,0:T(8,128)(2,1)S(1)} %get-tuple-element.112.refs_1_), channel_id=1, source_target_pairs={{0,10},{1,8},{2,11},{3,9},{4,14},{5,12},{6,15},{7,13},{8,1},{9,3},... | collective-permute-start | bytes 589832 | tf_op jit(solution)/shard_map/ppermute | solution.py:407
  16.2 17.5 %slice-start = ((s8[6291456]{0:T(1024)(128)(4,1)}), s8[4194304]{0:T(1024)(128)(4,1)S(1)}, s32[]{:S(2)}) async-start(s8[6291456]{0:T(1024)(128)(4,1)} %bitcast.2), calls=%async_computation | async-start | bytes 8388608
  18.1 15.7 %collective-permute-start.8 = (bf16[96,1024]{1,0:T(8,128)(2,1)S(1)}, bf16[96,1024]{1,0:T(8,128)(2,1)S(1)}, u32[]{:S(2)}, u32[]{:S(2)}) collective-permute-start(bf16[96,1024]{1,0:T(8,128)(2,1)S(1)} %get-tuple-element.113.refs_2_), channel_id=1, source_target_pairs={{0,4},{1,6},{2,5},{3,7},{4,0},{5,2},{6,1},{7,3},{8,15},{9,13},{10,... | collective-permute-start | bytes 589832 | tf_op jit(solution)/shard_map/ppermute | solution.py:407
  19.6 14.1 %collective-permute-start.9 = (bf16[96,1024]{1,0:T(8,128)(2,1)S(1)}, bf16[96,1024]{1,0:T(8,128)(2,1)S(1)}, u32[]{:S(2)}, u32[]{:S(2)}) collective-permute-start(bf16[96,1024]{1,0:T(8,128)(2,1)S(1)} %get-tuple-element.114.refs_3_), channel_id=1, source_target_pairs={{0,0},{1,2},{2,1},{3,3},{4,4},{5,6},{6,5},{7,7},{8,11},{9,9},{10,1... | collective-permute-start | bytes 589832 | tf_op jit(solution)/shard_map/ppermute | solution.py:407
  35.3 6.2 %collective-permute-start.10 = (bf16[384,1024]{1,0:T(8,128)(2,1)S(1)}, bf16[384,1024]{1,0:T(8,128)(2,1)S(1)}, u32[]{:S(2)}, u32[]{:S(2)}) collective-permute-start(bf16[384,1024]{1,0:T(8,128)(2,1)S(1)} %get-tuple-element.93.refs_1_), channel_id=1, source_target_pairs={{0,1},{1,0},{2,3},{3,2},{4,5},{5,4},{6,7},{7,6},{8,9},{9,8},{10,11... | collective-permute-start | bytes 2359304 | tf_op jit(solution)/shard_map/ppermute | solution.py:394
  36.4 6.7 %collective-permute-start.4 = (bf16[96,1024]{1,0:T(8,128)(2,1)S(1)}, bf16[96,1024]{1,0:T(8,128)(2,1)S(1)}, u32[]{:S(2)}, u32[]{:S(2)}) collective-permute-start(bf16[96,1024]{1,0:T(8,128)(2,1)S(1)} %get-tuple-element.106.refs_2_), channel_id=1, source_target_pairs={{0,4},{1,6},{2,5},{3,7},{4,0},{5,2},{6,1},{7,3},{8,15},{9,13},{10,... | collective-permute-start | bytes 589832 | tf_op jit(solution)/shard_map/ppermute | solution.py:407
  36.4 10.2 %collective-permute-start.5 = (bf16[96,1024]{1,0:T(8,128)(2,1)S(1)}, bf16[96,1024]{1,0:T(8,128)(2,1)S(1)}, u32[]{:S(2)}, u32[]{:S(2)}) collective-permute-start(bf16[96,1024]{1,0:T(8,128)(2,1)S(1)} %get-tuple-element.107.refs_3_), channel_id=1, source_target_pairs={{0,0},{1,2},{2,1},{3,3},{4,4},{5,6},{6,5},{7,7},{8,11},{9,9},{10,1... | collective-permute-start | bytes 589832 | tf_op jit(solution)/shard_map/ppermute | solution.py:407
  39.1 8.1 %collective-permute-start.3 = (bf16[96,1024]{1,0:T(8,128)(2,1)S(1)}, bf16[96,1024]{1,0:T(8,128)(2,1)S(1)}, u32[]{:S(2)}, u32[]{:S(2)}) collective-permute-start(bf16[96,1024]{1,0:T(8,128)(2,1)S(1)} %get-tuple-element.104.refs_0_), channel_id=1, source_target_pairs={{0,14},{1,12},{2,15},{3,13},{4,10},{5,8},{6,11},{7,9},{8,5},{9,7},... | collective-permute-start | bytes 589832 | tf_op jit(solution)/shard_map/ppermute | solution.py:407
  48.4 22.4 %collective-permute-start.11 = (bf16[288,1024]{1,0:T(8,128)(2,1)S(1)}, bf16[288,1024]{1,0:T(8,128)(2,1)S(1)}, u32[]{:S(2)}, u32[]{:S(2)}) collective-permute-start(bf16[288,1024]{1,0:T(8,128)(2,1)S(1)} %get-tuple-element.99.refs_1_), channel_id=1, source_target_pairs={{0,1},{1,0},{2,3},{3,2},{4,5},{5,4},{6,7},{7,6},{8,9},{9,8},{10,11... | collective-permute-start | bytes 1769480 | tf_op jit(solution)/shard_map/ppermute | solution.py:394
  49.9 13.4 %collective-permute-start.12 = (bf16[96,1024]{1,0:T(8,128)(2,1)S(1)}, bf16[96,1024]{1,0:T(8,128)(2,1)S(1)}, u32[]{:S(2)}, u32[]{:S(2)}) collective-permute-start(bf16[96,1024]{1,0:T(8,128)(2,1)S(1)} %get-tuple-element.105.refs_1_), channel_id=1, source_target_pairs={{0,10},{1,8},{2,11},{3,9},{4,14},{5,12},{6,15},{7,13},{8,1},{9,3},... | collective-permute-start | bytes 589832 | tf_op jit(solution)/shard_map/ppermute | solution.py:407
  64.0 16.1 %copy-start = (bf16[2,512,1024]{2,1,0:T(8,128)(2,1)S(1)}, bf16[2,512,1024]{2,1,0:T(8,128)(2,1)}, u32[]{:S(2)}) copy-start(bf16[2,512,1024]{2,1,0:T(8,128)(2,1)} %w_ref.15) | copy-start | bytes 6291460
  64.0 3.7 %collective-permute-start.13 = (bf16[96,1024]{1,0:T(8,128)(2,1)S(1)}, bf16[96,1024]{1,0:T(8,128)(2,1)S(1)}, u32[]{:S(2)}, u32[]{:S(2)}) collective-permute-start(bf16[96,1024]{1,0:T(8,128)(2,1)S(1)} %get-tuple-element.102.refs_4_), channel_id=1, source_target_pairs={{0,1},{1,0},{2,3},{3,2},{4,5},{5,4},{6,7},{7,6},{8,9},{9,8},{10,11... | collective-permute-start | bytes 589832 | tf_op jit(solution)/shard_map/ppermute | solution.py:394
  64.5 9.1 %collective-permute-start.19 = (bf16[96,512]{1,0:T(8,128)(2,1)S(1)}, bf16[96,512]{1,0:T(8,128)(2,1)S(1)}, u32[]{:S(2)}, u32[]{:S(2)}) collective-permute-start(bf16[96,512]{1,0:T(8,128)(2,1)S(1)} %get-tuple-element.116), channel_id=1, source_target_pairs={{0,10},{1,8},{2,11},{3,9},{4,14},{5,12},{6,15},{7,13},{8,1},{9,3},... | collective-permute-start | bytes 294920 | tf_op jit(solution)/shard_map/ppermute | solution.py:407
  64.5 9.1 %collective-permute-start.18 = (bf16[96,512]{1,0:T(8,128)(2,1)S(1)}, bf16[96,512]{1,0:T(8,128)(2,1)S(1)}, u32[]{:S(2)}, u32[]{:S(2)}) collective-permute-start(bf16[96,512]{1,0:T(8,128)(2,1)S(1)} %get-tuple-element.94.in_ref), channel_id=1, source_target_pairs={{0,14},{1,12},{2,15},{3,13},{4,10},{5,8},{6,11},{7,9},{8,5},{9,7},... | collective-permute-start | bytes 294920 | tf_op jit(solution)/shard_map/ppermute | solution.py:407
  65.8 10.6 %collective-permute-start.20 = (bf16[96,512]{1,0:T(8,128)(2,1)S(1)}, bf16[96,512]{1,0:T(8,128)(2,1)S(1)}, u32[]{:S(2)}, u32[]{:S(2)}) collective-permute-start(bf16[96,512]{1,0:T(8,128)(2,1)S(1)} %get-tuple-element.117), channel_id=1, source_target_pairs={{0,4},{1,6},{2,5},{3,7},{4,0},{5,2},{6,1},{7,3},{8,15},{9,13},{10,... | collective-permute-start | bytes 294920 | tf_op jit(solution)/shard_map/ppermute | solution.py:407
  67.7 12.4 %collective-permute-start.21 = (bf16[96,512]{1,0:T(8,128)(2,1)S(1)}, bf16[96,512]{1,0:T(8,128)(2,1)S(1)}, u32[]{:S(2)}, u32[]{:S(2)}) collective-permute-start(bf16[96,512]{1,0:T(8,128)(2,1)S(1)} %get-tuple-element.118), channel_id=1, source_target_pairs={{0,0},{1,2},{2,1},{3,3},{4,4},{5,6},{6,5},{7,7},{8,11},{9,9},{10,1... | collective-permute-start | bytes 294920 | tf_op jit(solution)/shard_map/ppermute | solution.py:407
  72.2 9.3 %collective-permute-start.14 = (bf16[96,512]{1,0:T(8,128)(2,1)S(1)}, bf16[96,512]{1,0:T(8,128)(2,1)S(1)}, u32[]{:S(2)}, u32[]{:S(2)}) collective-permute-start(bf16[96,512]{1,0:T(8,128)(2,1)S(1)} %get-tuple-element.103), channel_id=1, source_target_pairs={{0,14},{1,12},{2,15},{3,13},{4,10},{5,8},{6,11},{7,9},{8,5},{9,7},... | collective-permute-start | bytes 294920 | tf_op jit(solution)/shard_map/ppermute | solution.py:407
  73.6 10.2 %collective-permute-start.15 = (bf16[96,512]{1,0:T(8,128)(2,1)S(1)}, bf16[96,512]{1,0:T(8,128)(2,1)S(1)}, u32[]{:S(2)}, u32[]{:S(2)}) collective-permute-start(bf16[96,512]{1,0:T(8,128)(2,1)S(1)} %get-tuple-element.108), channel_id=1, source_target_pairs={{0,10},{1,8},{2,11},{3,9},{4,14},{5,12},{6,15},{7,13},{8,1},{9,3},... | collective-permute-start | bytes 294920 | tf_op jit(solution)/shard_map/ppermute | solution.py:407
  73.6 10.2 %collective-permute-start.16 = (bf16[96,512]{1,0:T(8,128)(2,1)S(1)}, bf16[96,512]{1,0:T(8,128)(2,1)S(1)}, u32[]{:S(2)}, u32[]{:S(2)}) collective-permute-start(bf16[96,512]{1,0:T(8,128)(2,1)S(1)} %get-tuple-element.109), channel_id=1, source_target_pairs={{0,4},{1,6},{2,5},{3,7},{4,0},{5,2},{6,1},{7,3},{8,15},{9,13},{10,... | collective-permute-start | bytes 294920 | tf_op jit(solution)/shard_map/ppermute | solution.py:407
  76.4 7.3 %collective-permute-start.17 = (bf16[96,512]{1,0:T(8,128)(2,1)S(1)}, bf16[96,512]{1,0:T(8,128)(2,1)S(1)}, u32[]{:S(2)}, u32[]{:S(2)}) collective-permute-start(bf16[96,512]{1,0:T(8,128)(2,1)S(1)} %get-tuple-element.110), channel_id=1, source_target_pairs={{0,0},{1,2},{2,1},{3,3},{4,4},{5,6},{6,5},{7,7},{8,11},{9,9},{10,1... | collective-permute-start | bytes 294920 | tf_op jit(solution)/shard_map/ppermute | solution.py:407
  (2 other events, 22.0 us)
